TPU v7x, 512 devices: a whole 4x4x16 slice. The times are simulated.
512 devices in a mesh: dp: 128 (over z, y, core), shard: 4 (over x).
Axes of the slice: x: 4, y: 4, z: 16, core: 2. Of those that a mesh axis runs over, the one named last changes fastest.
Arguments:
- key_grad: bfloat16 [128, 512, 2560], P('dp', 'shard'), may hold values from -90 to 90
- key_error: float32 [128, 512, 2560], P('dp', 'shard'), may hold values from -4 to 4
- router_grad: bfloat16 [128, 64, 2560], P('dp', 'shard'), may hold values from -90 to 90
- router_error: float32 [128, 64, 2560], P('dp', 'shard'), may hold values from -4 to 4
- norm_grad: bfloat16 [128, 2, 2560], P('dp', None, 'shard'), may hold values from -8 to 8
- key_basis: float32 [32, 2560], replicated, may hold values from -6 to 6
- router_basis: float32 [32, 2560], replicated, may hold values from -6 to 6
- key_momentum: float32 [512, 2560], P('shard', 'dp'), may hold values from -4 to 4
- key_weight: float32 [512, 2560], P('shard', 'dp'), may hold values from -4 to 4
- router_momentum: float32 [64, 2560], P('shard', 'dp'), may hold values from -4 to 4
- router_weight: float32 [64, 2560], P('shard', 'dp'), may hold values from -4 to 4
- norm_momentum: float32 [2, 2560], P(None, 'shard'), may hold values from -4 to 4
- norm_weight: float32 [2, 2560], P(None, 'shard'), may hold values from 0.5 to 1.5
Outputs:
- key_carry: float32 [128, 512, 2560], P('dp', 'shard')
- router_carry: float32 [128, 64, 2560], P('dp', 'shard')
- key_velocity: float32 [512, 2560], P('shard', 'dp')
- key_master: float32 [512, 2560], P('shard', 'dp')
- key_params: bfloat16 [512, 2560], P(None, 'dp')
- router_velocity: float32 [64, 2560], P('shard', 'dp')
- router_master: float32 [64, 2560], P('shard', 'dp')
- router_params: bfloat16 [64, 2560], P(None, 'dp')
- norm_velocity: float32 [2, 2560], P(None, 'shard')
- norm_master: float32 [2, 2560], P(None, 'shard')
- norm_params: bfloat16 [2, 2560], replicated
All inputs are finite; a program needn't handle non-finite values.
Results may differ from a plain program's by a relative error of at most 0.008.
Values may be sent and summed in bfloat16 or wider, within the bound.
No kernel may reach another device: no remote copies, remote signals or barrier semaphores. Data moves between devices by JAX's collectives and lax.ppermute only.
A program may use at most 64 MiB of HBM per device.

v0:
```python
import jax
import jax.numpy as jnp
from jax import lax
from jax.sharding import PartitionSpec as P

ROOT_STEPS = 4


highest = lax.Precision.HIGHEST
momentum_decay = 0.9
learning_rate = 0.1


def inverse_root(gram_matrix):
    scaling = jnp.sqrt(jnp.sum(gram_matrix * gram_matrix)) + 1e-06
    identity = jnp.eye(gram_matrix.shape[0], dtype=jnp.float32)
    square_side = gram_matrix / scaling
    root_side = identity
    for sweep_index in range(ROOT_STEPS):
        middle = 1.5 * identity - 0.5 * jnp.dot(root_side, square_side, precision=highest)
        square_side = jnp.dot(square_side, middle, precision=highest)
        root_side = jnp.dot(middle, root_side, precision=highest)
    return (root_side, scaling)


def project(old_basis, merged):
    return lax.dot_general(old_basis, merged, (((1,), (1,)), ((), ())), precision=highest)


def gram_of(factor_rows):
    return lax.dot_general(factor_rows, factor_rows, (((1,), (1,)), ((), ())), precision=highest)


def normalize(gram_matrix, factor_rows):
    root_side, scaling = inverse_root(gram_matrix)
    return jnp.dot(root_side, factor_rows, precision=highest) / jnp.sqrt(scaling)


def advance(momentum, weight, direction):
    velocity = momentum_decay * momentum + direction
    return (velocity, weight - learning_rate * velocity)


def body(
    key_grad,
    key_error,
    router_grad,
    router_error,
    norm_grad,
    key_basis,
    router_basis,
    key_momentum,
    key_weight,
    router_momentum,
    router_weight,
    norm_momentum,
    norm_weight,
):
    replicas = lax.axis_size("dp")
    rank_size = key_basis.shape[0]
    merged_key = key_grad[0].astype(jnp.float32) + key_error[0]
    merged_router = router_grad[0].astype(jnp.float32) + router_error[0]
    rows_key, rows_router, norm_sum = lax.psum(
        (
            project(key_basis, merged_key),
            project(router_basis, merged_router),
            norm_grad[0].astype(jnp.float32),
        ),
        "dp",
    )
    gram_key, gram_router = lax.psum((gram_of(rows_key), gram_of(rows_router)), "shard")
    ortho_key = normalize(gram_key, rows_key)
    ortho_router = normalize(gram_router, rows_router)
    key_part = lax.dot_general(merged_key, ortho_key, (((0,), (1,)), ((), ())), precision=highest)
    router_part = lax.dot_general(
        merged_router, ortho_router, (((0,), (1,)), ((), ())), precision=highest
    )
    column_sum = lax.psum(jnp.concatenate([key_part, router_part], axis=1), ("dp", "shard"))
    columns = column_sum / replicas
    approx_key = lax.dot_general(
        ortho_key, columns[:, :rank_size], (((0,), (1,)), ((), ())), precision=highest
    )
    approx_router = lax.dot_general(
        ortho_router, columns[:, rank_size:], (((0,), (1,)), ((), ())), precision=highest
    )
    col_width = key_momentum.shape[1]
    offset = lax.axis_index("dp") * col_width
    key_velocity, key_master = advance(
        key_momentum, key_weight, lax.dynamic_slice_in_dim(approx_key, offset, col_width, 1)
    )
    router_velocity, router_master = advance(
        router_momentum,
        router_weight,
        lax.dynamic_slice_in_dim(approx_router, offset, col_width, 1),
    )
    norm_velocity, norm_master = advance(norm_momentum, norm_weight, norm_sum / replicas)
    key_params, router_params, norm_params = (
        lax.all_gather(key_master.astype(jnp.bfloat16), "shard", axis=0, tiled=True),
        lax.all_gather(router_master.astype(jnp.bfloat16), "shard", axis=0, tiled=True),
        lax.all_gather(norm_master.astype(jnp.bfloat16), "shard", axis=1, tiled=True),
    )
    key_carry = (merged_key - approx_key)[None]
    router_carry = (merged_router - approx_router)[None]
    return (
        key_carry,
        router_carry,
        key_velocity,
        key_master,
        key_params,
        router_velocity,
        router_master,
        router_params,
        norm_velocity,
        norm_master,
        norm_params,
    )


def solution(mesh):
    return jax.shard_map(
        body,
        mesh=mesh,
        in_specs=(
            P("dp", "shard", None),
            P("dp", "shard", None),
            P("dp", "shard", None),
            P("dp", "shard", None),
            P("dp", None, "shard"),
            P(),
            P(),
            P("shard", "dp"),
            P("shard", "dp"),
            P("shard", "dp"),
            P("shard", "dp"),
            P(None, "shard"),
            P(None, "shard"),
        ),
        out_specs=(
            P("dp", "shard", None),
            P("dp", "shard", None),
            P("shard", "dp"),
            P("shard", "dp"),
            P(None, "dp"),
            P("shard", "dp"),
            P("shard", "dp"),
            P(None, "dp"),
            P(None, "shard"),
            P(None, "shard"),
            P(),
        ),
        check_vma=False,
    )
```

profile of v0, /device:TPU:1, one launch (start us, length us, event | category | flops | bytes accessed | tf_op | source)
XLA Modules:
  0.0 1032.7 jit_solution(1657459035492836335)
XLA Ops:
  7.2 0.7 bitcast_convert_fusion
  8.0 1.4 convolution_bitcast_fusion
  9.5 2.9 fusion.5
  12.4 498.1 %all-reduce = (f32[32,128]{1,0:T(8,128)S(1)}, f32[32,16]{0,1:T(8,128)S(1)}, f32[2,640]{1,0:T(2,128)S(1)}) all-reduce(f32[32,128]{1,0:T(8,128)S(1)} %fusion.5, f32[32,16]{0,1:T(8,128)S(1)} %convolution_bitcast_fusion, f32[2,640]{1,0:T(2,128)S(1)} %bitcast_convert_fusion), channel_id=1, replica_groups=mesh['dp'=128,'shard'=4] {'dp'}, use_global_device_ids=true, to_apply=%region_0.0 | all-reduce | flops 5888 | bytes 47104 | tf_op jit(solution)/shard_map/psum | solution.py:63
  510.8 13.3 %all-reduce.1 = (f32[32,32]{1,0:T(8,128)S(1)}, f32[32,32]{1,0:T(8,128)S(1)}) all-reduce(f32[32,32]{1,0:T(8,128)S(1)} %fusion.31, f32[32,32]{1,0:T(8,128)S(1)} %fusion.37), channel_id=1, replica_groups=mesh['dp'=128,'shard'=4] {'shard'}, use_global_device_ids=true, to_apply=%region_1.0 | all-reduce | flops 2048 | bytes 16384 | tf_op jit(solution)/shard_map/psum | solution.py:71
  524.2 0.6 multiply_reduce_fusion
  529.7 0.9 fusion
  531.3 0.9 pad_maximum_fusion
  532.3 0.6 fusion.28
  532.9 8.9 all_gather.11
  542.0 453.4 %all-reduce.4.cloned.1.call-done = f32[2560,64]{0,1:T(8,128)} async-done(((f32[2560,64]{0,1:T(8,128)}), f32[2560,64]{0,1:T(8,128)}) %all-reduce.4.cloned.1.call-update) | async-done | bytes 655376 | tf_op jit(solution)/shard_map/psum | solution.py:78
  995.4 1.1 broadcast_multiply_fusion
  996.8 2.3 fusion.18
  999.1 0.7 fusion.23
  999.8 0.7 fusion.29
  1000.5 9.4 all_gather.10
  1009.9 0.7 copy.29
  1010.6 2.6 fusion.4
  1013.1 1.0 fusion.30
  1014.1 0.7 copy.27
  1014.8 0.7 copy.26
  1015.5 9.1 all_gather.9
  1024.6 0.7 copy.28
  1025.3 0.6 copy.32
  (54 shorter events, 5.0 us)
Async XLA Ops:
  7.2 2.3 copy-start
  7.2 988.2 %all-reduce.4.cloned.1.call-start = ((), (), s32[]{:S(2)}) async-start(), calls=%async_computation | async-start | bytes 1310720 | tf_op jit(solution)/shard_map/psum | solution.py:78
  9.4 520.3 %copy-start.1 = (f32[1,128,2560]{2,1,0:T(8,128)S(1)}, f32[1,128,2560]{2,1,0:T(8,128)}, u32[]{:S(2)}) copy-start(f32[1,128,2560]{2,1,0:T(8,128)} %param.14) | copy-start | bytes 3932164
  9.5 520.3 %copy-start.2 = (bf16[1,128,2560]{2,1,0:T(8,128)(2,1)S(1)}, bf16[1,128,2560]{2,1,0:T(8,128)(2,1)}, u32[]{:S(2)}) copy-start(bf16[1,128,2560]{2,1,0:T(8,128)(2,1)} %param.13) | copy-start | bytes 1966084
  528.8 2.0 copy-start.3
  528.8 2.0 copy-start.4
  530.7 1.6 copy-start.9
  530.7 1.6 copy-start.10
  530.8 10.9 %copy-start.5 = (f32[128,20]{0,1:T(8,128)S(1)}, f32[128,20]{0,1:T(8,128)}, u32[]{:S(2)}) copy-start(f32[128,20]{0,1:T(8,128)} %param.20) | copy-start | bytes 30724
  530.9 11.0 %copy-start.6 = (f32[128,20]{0,1:T(8,128)S(1)}, f32[128,20]{0,1:T(8,128)}, u32[]{:S(2)}) copy-start(f32[128,20]{0,1:T(8,128)} %param.21) | copy-start | bytes 30724
  996.5 3.3 copy-start.7
  996.5 3.3 copy-start.8
Sparse Core Ops, SparseCore 0:
  532.4 462.9 all-reduce.3
where the time goes:
time: 1040 us; the launch traced here: 1030 us
  blocking collectives  539 us (52%)
  waiting for transfers between devices  453 us (44%)
  between operations  15.8 us (2%)
  matrix products  12.1 us (1%)
    psum x1, blocking collectives, body(): lax.psum((project(key_basis, merged_key), project(router_basis, merged_ro...  498 us
    psum x1, waiting for transfers between devices, body(): lax.psum(jnp.concatenate([key_part, router_part], axis=1), ('dp', 'shard'))  453 us
  transfers between devices with their start and end apart: 1, of which 1 were waited for; matrix products, arithmetic and copies ran while one was open for 0% of the time, Pallas kernels for 0%

commit v1 on v0

v1 whole, which is shorter than its diff:
```python
import jax
import jax.numpy as jnp
from jax import lax
from jax.sharding import Mesh, PartitionSpec as P

ROOT_STEPS = 4

highest = lax.Precision.HIGHEST
momentum_decay = 0.9
learning_rate = 0.1
f32 = jnp.float32
bf16 = jnp.bfloat16

DP = ("z", "y", "c")
PLANE = ("y", "c", "shard")
LANES = 128
PACK_ROWS = 48


def inverse_root(gram_matrix):
    scaling = jnp.sqrt(jnp.sum(gram_matrix * gram_matrix, axis=(1, 2), keepdims=True)) + 1e-06
    identity = jnp.eye(gram_matrix.shape[1], dtype=f32)[None]
    square_side = gram_matrix / scaling
    root_side = jnp.broadcast_to(identity, gram_matrix.shape)
    for sweep_index in range(ROOT_STEPS):
        middle = 1.5 * identity - 0.5 * batched(root_side, square_side)
        square_side = batched(square_side, middle)
        root_side = batched(middle, root_side)
    return root_side, scaling


def batched(left, right):
    return lax.dot_general(left, right, (((2,), (1,)), ((0,), (0,))), precision=highest)


def dot(left, right, left_dim, right_dim):
    return lax.dot_general(left, right, (((left_dim,), (right_dim,)), ((), ())), precision=highest)


def to_all(block, axes, size):
    spread = jnp.broadcast_to(block[None], (size,) + block.shape)
    return lax.all_to_all(spread, axes, 0, 0, tiled=True)


def body(
    key_grad,
    key_error,
    router_grad,
    router_error,
    norm_grad,
    key_basis,
    router_basis,
    key_momentum,
    key_weight,
    router_momentum,
    router_weight,
    norm_momentum,
    norm_weight,
):
    n_z, n_y, n_c, n_x = (lax.axis_size(name) for name in DP + ("shard",))
    plane = n_y * n_c * n_x
    replicas = n_z * n_y * n_c
    rank_size, width = key_basis.shape
    key_rows, router_rows = key_grad.shape[1], router_grad.shape[1]
    norm_vecs, norm_width = norm_grad.shape[1:]
    col_width = key_momentum.shape[1]
    half = PACK_ROWS // n_c

    decayed_key = key_weight - (learning_rate * momentum_decay) * key_momentum
    decayed_router = router_weight - (learning_rate * momentum_decay) * router_momentum
    decayed_norm = norm_weight - (learning_rate * momentum_decay) * norm_momentum
    norm_lines = norm_vecs * norm_width // LANES
    decayed = jnp.concatenate(
        [
            decayed_key.T,
            jnp.pad(decayed_router.T, ((0, 0), (0, LANES - router_momentum.shape[0]))),
            decayed_norm.reshape(norm_lines, LANES),
        ],
        axis=0,
    )
    decayed = jnp.pad(decayed, ((0, 512 - decayed.shape[0]), (0, 0)))
    decayed, key_error = lax.optimization_barrier((decayed, key_error))
    decayed = lax.all_gather(decayed, "shard", axis=0, tiled=False)

    merged_key = key_grad[0].astype(f32) + key_error[0]
    merged_router = router_grad[0].astype(f32) + router_error[0]
    router_lines = rank_size * router_rows // LANES
    used = rank_size + router_lines + norm_lines
    pack = jnp.concatenate(
        [
            dot(key_basis, merged_key, 1, 1),
            dot(router_basis, merged_router, 1, 1).reshape(router_lines, LANES),
            norm_grad[0].astype(f32).reshape(norm_lines, LANES),
            jnp.zeros((PACK_ROWS - used, LANES), f32),
        ],
        axis=0,
    )
    pair = lax.all_gather(pack, "c", axis=0, tiled=False)
    mine = jnp.sum(lax.dynamic_slice_in_dim(pair, lax.axis_index("c") * half, half, 1), axis=0)
    mine = jnp.sum(to_all(mine, "z", n_z), axis=0)
    spread = to_all(mine, PLANE, plane).reshape(n_y, n_c, n_x, half, LANES)
    full = jnp.sum(spread, axis=0).transpose(1, 0, 2, 3).reshape(n_x, PACK_ROWS, LANES)
    rows_key = full[:, :rank_size].transpose(1, 0, 2).reshape(rank_size, n_x * LANES)
    rows_router = (
        full[:, rank_size : rank_size + router_lines]
        .reshape(n_x, rank_size, router_rows)
        .transpose(1, 0, 2)
        .reshape(rank_size, n_x * router_rows)
    )
    norm_sum = full[:, rank_size + router_lines : used].reshape(n_x, norm_vecs, norm_width)

    grams = jnp.stack([dot(rows_key, rows_key, 1, 1), dot(rows_router, rows_router, 1, 1)])
    roots, scalings = inverse_root(grams)
    ortho_key = dot(roots[0], rows_key, 1, 0) / jnp.sqrt(scalings[0])
    ortho_router = dot(roots[1], rows_router, 1, 0) / jnp.sqrt(scalings[1])
    shard = lax.axis_index("shard")
    own_key = lax.dynamic_slice_in_dim(ortho_key, shard * key_rows, key_rows, 1)
    own_router = lax.dynamic_slice_in_dim(ortho_router, shard * router_rows, router_rows, 1)

    part = jnp.concatenate([dot(own_key, merged_key, 1, 0), dot(own_router, merged_router, 1, 0)])
    groups, lane_groups = 2 * rank_size // 8, plane // (2 * rank_size // 8)
    part = part.astype(bf16).reshape(groups, 8, lane_groups, width // lane_groups)
    part = part.transpose(0, 2, 1, 3).reshape(plane, 8, width // lane_groups)
    part = lax.all_to_all(part, PLANE, 0, 0, tiled=True)
    mine = jnp.sum(part.astype(f32), axis=0).astype(bf16)
    mine = jnp.sum(to_all(mine, "z", n_z).astype(f32), axis=0) / replicas
    columns = to_all(mine.astype(bf16), PLANE, plane)
    columns = columns.reshape(groups, lane_groups, 8, width // lane_groups)
    columns = columns.transpose(0, 2, 1, 3).reshape(2 * rank_size, width).astype(f32)

    key_carry = (merged_key - dot(own_key, columns[:rank_size], 0, 0))[None]
    router_carry = (merged_router - dot(own_router, columns[rank_size:], 0, 0))[None]

    offset = lax.axis_index(DP) * col_width
    few = lax.dynamic_slice_in_dim(columns, offset, col_width, 1)
    approx_key = dot(ortho_key, few[:rank_size], 0, 0)
    approx_router = dot(ortho_router, few[rank_size:], 0, 0)
    norm_mean = norm_sum / replicas

    def advance(momentum, weight, direction):
        velocity = momentum_decay * momentum + direction
        return velocity, weight - learning_rate * velocity

    key_velocity, key_master = advance(
        key_momentum, key_weight, lax.dynamic_slice_in_dim(approx_key, shard * key_rows, key_rows, 0)
    )
    router_velocity, router_master = advance(
        router_momentum,
        router_weight,
        lax.dynamic_slice_in_dim(approx_router, shard * router_rows, router_rows, 0),
    )
    norm_velocity, norm_master = advance(
        norm_momentum, norm_weight, lax.dynamic_index_in_dim(norm_mean, shard, 0, keepdims=False)
    )

    all_key = decayed[:, :col_width].transpose(0, 2, 1).reshape(n_x * key_rows, col_width)
    all_router = decayed[:, col_width : 2 * col_width, :router_rows]
    all_router = all_router.transpose(0, 2, 1).reshape(n_x * router_rows, col_width)
    all_norm = decayed[:, 2 * col_width : 2 * col_width + norm_lines]
    all_norm = all_norm.reshape(n_x, norm_vecs, norm_width)
    key_params = (all_key - learning_rate * approx_key).astype(bf16)
    router_params = (all_router - learning_rate * approx_router).astype(bf16)
    norm_params = (all_norm - learning_rate * norm_mean).astype(bf16)
    norm_params = norm_params.transpose(1, 0, 2).reshape(norm_vecs, n_x * norm_width)
    return (
        key_carry,
        router_carry,
        key_velocity,
        key_master,
        key_params,
        router_velocity,
        router_master,
        router_params,
        norm_velocity,
        norm_master,
        norm_params,
    )


def solution(mesh):
    n_dp, n_x = mesh.devices.shape
    fine = Mesh(mesh.devices.reshape(n_dp // 8, 4, 2, n_x), DP + ("shard",))
    return jax.shard_map(
        body,
        mesh=fine,
        in_specs=(
            P(DP, "shard", None),
            P(DP, "shard", None),
            P(DP, "shard", None),
            P(DP, "shard", None),
            P(DP, None, "shard"),
            P(),
            P(),
            P("shard", DP),
            P("shard", DP),
            P("shard", DP),
            P("shard", DP),
            P(None, "shard"),
            P(None, "shard"),
        ),
        out_specs=(
            P(DP, "shard", None),
            P(DP, "shard", None),
            P("shard", DP),
            P("shard", DP),
            P(None, DP),
            P("shard", DP),
            P("shard", DP),
            P(None, DP),
            P(None, "shard"),
            P(None, "shard"),
            P(),
        ),
        check_vma=False,
    )
```

time: 1040 us -> 142 us (0.14)
  blocking collectives: 539 us -> 46.7 us
  waiting for transfers between devices: 453 us -> 28.9 us
  starting transfers between devices: 0.04 us -> 23.5 us
    psum x2 -> x0, blocking collectives: 511 us -> none  [the longest x1 498 us: body(): lax.psum((project(key_basis, merged_key), project(router_basis, merged_ro...]
    psum x1 -> x0, waiting for transfers between devices: 453 us -> none  [body(): lax.psum(jnp.concatenate([key_part, router_part], axis=1), ('dp', 'shard'))]
    all_to_all x0 -> x2, blocking collectives: none -> 38.3 us  [the longest x1 22.3 us: to_all(): return lax.all_to_all(spread, axes, 0, 0, tiled=True)]
    all_to_all x0 -> x3, waiting for transfers between devices: none -> 28.2 us  [to_all(): return lax.all_to_all(spread, axes, 0, 0, tiled=True)]
    all_to_all x0 -> x3, starting transfers between devices: none -> 23.5 us  [to_all(): return lax.all_to_all(spread, axes, 0, 0, tiled=True)]
    all_gather x3 -> x1, blocking collectives: 27.3 us -> 8.36 us  [body(): pair = lax.all_gather(pack, 'c', axis=0, tiled=False)]
  transfers between devices with their start and end apart: 1 -> 4, of which waited for: 1 -> 3; matrix products, arithmetic and copies ran while one was open for 0% -> 7% of each run, Pallas kernels for 0% -> 0%
where the time goes in v1:
time: 142 us; the launch traced here: 141 us
  blocking collectives  46.7 us (33%)
  waiting for transfers between devices  28.9 us (20%)
  starting transfers between devices  23.5 us (17%)
  between operations  15.9 us (11%)
  matrix products  12.7 us (9%)
  local copies, waits for them, and re-layouts  8.8 us (6%)
  other arithmetic  4.71 us (3%)
    all_to_all x3, waiting for transfers between devices, to_all(): return lax.all_to_all(spread, axes, 0, 0, tiled=True)  28.2 us
    all_to_all x3, starting transfers between devices, to_all(): return lax.all_to_all(spread, axes, 0, 0, tiled=True)  23.5 us
    all_to_all x1, blocking collectives, to_all(): return lax.all_to_all(spread, axes, 0, 0, tiled=True)  22.3 us
    all_to_all x1, blocking collectives, body(): part = lax.all_to_all(part, PLANE, 0, 0, tiled=True)  16 us
    dot_general x12, matrix products, dot(): lax.dot_general(left, right, (((left_dim,), (right_dim,)), ((), ())), pre...  10.8 us
    all_gather x1, blocking collectives, body(): pair = lax.all_gather(pack, 'c', axis=0, tiled=False)  8.36 us
  transfers between devices with their start and end apart: 4, of which 3 were waited for; matrix products, arithmetic and copies ran while one was open for 7% of the time, Pallas kernels for 0%

profile of v1, /device:TPU:1, one launch (start us, length us, event | category | flops | bytes accessed | tf_op | source)
XLA Modules:
  0.0 141.2 jit_solution(18306863851812318569)
XLA Ops:
  7.2 0.8 multiply_subtract_fusion.3
  8.7 1.4 %convolution_bitcast_fusion.2 = f32[32,16]{0,1:T(8,128)S(1)} fusion(f32[32,2560]{1,0:T(8,128)} %param.19, f32[1,16,2560]{2,1,0:T(8,128)} %param.16, bf16[1,16,2560]{2,1,0:T(8,128)(2,1)} %param.15), kind=kOutput, calls=%fused_computation.23 | convolution fusion | flops 15810560 | bytes 575488 | tf_op jit(solution)/shard_map/dot_general | solution.py:37
  10.3 0.7 subtract_bitcast_fusion.1
  11.2 0.7 subtract_bitcast_fusion
  12.7 2.6 %fusion.9 = f32[32,128]{1,0:T(8,128)S(1)} fusion(f32[32,2560]{1,0:T(8,128)S(1)} %copy-done, f32[1,128,2560]{2,1,0:T(8,128)} %param.14, bf16[1,128,2560]{2,1,0:T(8,128)(2,1)S(1)} %copy-done.2), kind=kOutput, calls=%fused_computation.19 | convolution fusion | flops 126484480 | bytes 2310144 | tf_op jit(solution)/shard_map/dot_general | solution.py:37
  15.4 8.4 %all-gather = f32[96,128]{1,0:T(8,128)S(1)} all-gather(f32[48,128]{1,0:T(8,128)S(1)} %maximum_maximum_fusion), channel_id=2, replica_groups=mesh['z'=16,'y'=4,'c'=2,'shard'=4] {'c'}, dimensions={0}, use_global_device_ids=true | all-gather | bytes 73728 | tf_op jit(solution)/shard_map/all_gather | solution.py:98
  23.8 22.3 %all_to_all.25 = f32[16,24,128]{2,1,0:T(8,128)S(1)} all-to-all(f32[16,24,128]{2,1,0:T(8,128)S(1)} %broadcast_in_dim.20), channel_id=1, replica_groups=mesh['z'=16,'y'=4,'c'=2,'shard'=4] {'z'}, dimensions={0} | all-to-all | bytes 393216 | tf_op jit(solution)/shard_map/all_to_all | solution.py:42
  46.1 0.8 broadcast_in_dim.21
  46.9 10.3 %all-to-all-start.1 = ((f32[32,24,128]{2,1,0:T(8,128)}), f32[32,24,128]{2,1,0:T(8,128)S(1)}, u32[]{:S(2)}, u32[]{:S(2)}) async-start(f32[32,24,128]{2,1,0:T(8,128)} %broadcast_in_dim.21), calls=%async_computation.1 | async-start | bytes 786432 | tf_op jit(solution)/shard_map/all_to_all | solution.py:42
  58.0 9.4 %all-to-all-done.1 = f32[32,24,128]{2,1,0:T(8,128)S(1)} async-done(((f32[32,24,128]{2,1,0:T(8,128)}), f32[32,24,128]{2,1,0:T(8,128)S(1)}, u32[]{:S(2)}, u32[]{:S(2)}) %all-to-all-start.1) | async-done | bytes 393248 | tf_op jit(solution)/shard_map/all_to_all | solution.py:42
  73.0 0.9 convolution_convert_fusion.1
  74.0 16.0 %all_to_all.26 = bf16[32,8,640]{2,1,0:T(8,128)(2,1)S(1)} all-to-all(bf16[32,8,640]{2,1,0:T(8,128)(2,1)S(1)} %bitcast.120), channel_id=1, replica_groups=mesh['z'=16,'y'=4,'c'=2,'shard'=4] {'y','c','shard'}, dimensions={0} | all-to-all | bytes 655360 | tf_op jit(solution)/shard_map/all_to_all | solution.py:124
  90.8 6.3 %all-to-all-start.3 = ((bf16[16,8,640]{2,1,0:T(8,128)(2,1)}), bf16[16,8,640]{2,1,0:T(8,128)(2,1)S(1)}, u32[]{:S(2)}, u32[]{:S(2)}) async-start(bf16[16,8,640]{2,1,0:T(8,128)(2,1)} %broadcast_in_dim.22), calls=%async_computation.3 | async-start | bytes 327680 | tf_op jit(solution)/shard_map/all_to_all | solution.py:42
  97.3 0.9 slice_bitcast_fusion.1
  98.1 0.8 fusion.18
  98.9 11.5 %all-to-all-done.3 = bf16[16,8,640]{2,1,0:T(8,128)(2,1)S(1)} async-done(((bf16[16,8,640]{2,1,0:T(8,128)(2,1)}), bf16[16,8,640]{2,1,0:T(8,128)(2,1)S(1)}, u32[]{:S(2)}, u32[]{:S(2)}) %all-to-all-start.3) | async-done | bytes 163872 | tf_op jit(solution)/shard_map/all_to_all | solution.py:42
  110.5 0.8 broadcast_in_dim.23
  111.2 6.8 %all-to-all-start.4 = ((bf16[32,8,640]{2,1,0:T(8,128)(2,1)}), bf16[32,8,640]{2,1,0:T(8,128)(2,1)S(1)}, u32[]{:S(2)}, u32[]{:S(2)}) async-start(bf16[32,8,640]{2,1,0:T(8,128)(2,1)} %broadcast_in_dim.23), calls=%async_computation.4 | async-start | bytes 655360 | tf_op jit(solution)/shard_map/all_to_all | solution.py:42
  118.1 0.8 slice_bitcast_fusion.2
  120.3 7.3 %all-to-all-done.4 = bf16[32,8,640]{2,1,0:T(8,128)(2,1)S(1)} async-done(((bf16[32,8,640]{2,1,0:T(8,128)(2,1)}), bf16[32,8,640]{2,1,0:T(8,128)(2,1)S(1)}, u32[]{:S(2)}, u32[]{:S(2)}) %all-to-all-start.4) | async-done | bytes 327712 | tf_op jit(solution)/shard_map/all_to_all | solution.py:42
  127.6 0.9 subtract_convert_fusion.1
  129.9 0.9 subtract_convert_fusion
  131.5 1.0 fusion.1
  132.5 1.8 %fusion = f32[1,128,2560]{2,1,0:T(8,128)} fusion(bf16[32,2560]{1,0:T(8,128)(2,1)S(1)} %bitcast.121, f32[1,128,2560]{2,1,0:T(8,128)S(1)} %copy-done.1, bf16[1,128,2560]{2,1,0:T(8,128)(2,1)S(1)} %copy-done.2, f32[32,512]{1,0:T(8,128)S(1)} %convolution_divide_fusion, s32[]{:T(128)S(6)} %select_n.19), kind=kOutput, calls=%fused_computation.1 | convolution fusion | flops 126812160 | bytes 3457028 | tf_op jit(solution)/shard_map/dot_general | solution.py:37
  (84 shorter events, 11.2 us)
Async XLA Ops:
  7.2 5.5 %copy-start = (f32[32,2560]{1,0:T(8,128)S(1)}, f32[32,2560]{1,0:T(8,128)}, u32[]{:S(2)}) copy-start(f32[32,2560]{1,0:T(8,128)} %param.18) | copy-start | bytes 983044
  7.2 5.5 %copy-start.2 = (bf16[1,128,2560]{2,1,0:T(8,128)(2,1)S(1)}, bf16[1,128,2560]{2,1,0:T(8,128)(2,1)}, u32[]{:S(2)}) copy-start(bf16[1,128,2560]{2,1,0:T(8,128)(2,1)} %param.13) | copy-start | bytes 1966084
  46.9 20.5 %all-to-all-start.1 = ((f32[32,24,128]{2,1,0:T(8,128)}), f32[32,24,128]{2,1,0:T(8,128)S(1)}, u32[]{:S(2)}, u32[]{:S(2)}) async-start(f32[32,24,128]{2,1,0:T(8,128)} %broadcast_in_dim.21), calls=%async_computation.1 | async-start | bytes 786432 | tf_op jit(solution)/shard_map/all_to_all | solution.py:42
  57.2 40.1 %all-gather.4.cloned.1.call-start = ((), (), s32[]{:S(2)}) async-start(), calls=%async_computation.5 | async-start | bytes 1310720 | tf_op jit(solution)/shard_map/all_gather | solution.py:83
  58.0 14.6 %copy-start.3 = (f32[1,16,2560]{2,1,0:T(8,128)S(1)}, f32[1,16,2560]{2,1,0:T(8,128)}, u32[]{:S(2)}) copy-start(f32[1,16,2560]{2,1,0:T(8,128)} %param.16) | copy-start | bytes 491524
  58.0 14.6 %copy-start.4 = (bf16[1,16,2560]{2,1,0:T(8,128)(2,1)S(1)}, bf16[1,16,2560]{2,1,0:T(8,128)(2,1)}, u32[]{:S(2)}) copy-start(bf16[1,16,2560]{2,1,0:T(8,128)(2,1)} %param.15) | copy-start | bytes 245764
  67.4 5.6 %copy-start.1 = (f32[1,128,2560]{2,1,0:T(8,128)S(1)}, f32[1,128,2560]{2,1,0:T(8,128)}, u32[]{:S(2)}) copy-start(f32[1,128,2560]{2,1,0:T(8,128)} %param.14) | copy-start | bytes 3932164
  73.9 23.2 %copy-start.7 = (f32[16,20]{1,0:T(8,128)S(1)}, f32[16,20]{1,0:T(8,128)}, u32[]{:S(2)}) copy-start(f32[16,20]{1,0:T(8,128)} %param.22) | copy-start | bytes 3844
  74.0 23.2 %copy-start.8 = (f32[16,20]{1,0:T(8,128)S(1)}, f32[16,20]{1,0:T(8,128)}, u32[]{:S(2)}) copy-start(f32[16,20]{1,0:T(8,128)} %param.23) | copy-start | bytes 3844
  90.1 29.6 %copy-start.9 = (f32[2,640]{1,0:T(2,128)S(1)}, f32[2,640]{1,0:T(2,128)}, u32[]{:S(2)}) copy-start(f32[2,640]{1,0:T(2,128)} %param.25) | copy-start | bytes 15364
  90.1 29.6 %copy-start.10 = (f32[2,640]{1,0:T(2,128)S(1)}, f32[2,640]{1,0:T(2,128)}, u32[]{:S(2)}) copy-start(f32[2,640]{1,0:T(2,128)} %param.24) | copy-start | bytes 15364
  90.8 19.7 %all-to-all-start.3 = ((bf16[16,8,640]{2,1,0:T(8,128)(2,1)}), bf16[16,8,640]{2,1,0:T(8,128)(2,1)S(1)}, u32[]{:S(2)}, u32[]{:S(2)}) async-start(bf16[16,8,640]{2,1,0:T(8,128)(2,1)} %broadcast_in_dim.22), calls=%async_computation.3 | async-start | bytes 327680 | tf_op jit(solution)/shard_map/all_to_all | solution.py:42
  97.1 33.7 %copy-start.5 = (f32[128,20]{0,1:T(8,128)S(1)}, f32[128,20]{0,1:T(8,128)}, u32[]{:S(2)}) copy-start(f32[128,20]{0,1:T(8,128)} %param.21) | copy-start | bytes 30724
  97.1 33.7 %copy-start.6 = (f32[128,20]{0,1:T(8,128)S(1)}, f32[128,20]{0,1:T(8,128)}, u32[]{:S(2)}) copy-start(f32[128,20]{0,1:T(8,128)} %param.20) | copy-start | bytes 30724
  111.2 16.4 %all-to-all-start.4 = ((bf16[32,8,640]{2,1,0:T(8,128)(2,1)}), bf16[32,8,640]{2,1,0:T(8,128)(2,1)S(1)}, u32[]{:S(2)}, u32[]{:S(2)}) async-start(bf16[32,8,640]{2,1,0:T(8,128)(2,1)} %broadcast_in_dim.23), calls=%async_computation.4 | async-start | bytes 655360 | tf_op jit(solution)/shard_map/all_to_all | solution.py:42
Sparse Core Ops, SparseCore 0:
  60.2 28.0 all-gather.3

commit v2 on v1

--- a/solution.py
+++ b/solution.py
@@ -12,9 +12,10 @@
 bf16 = jnp.bfloat16
 
 DP = ("z", "y", "c")
+PAIRS = ("y", "c")
 PLANE = ("y", "c", "shard")
 LANES = 128
-PACK_ROWS = 48
+PACK_ROWS = 64
 
 
 def inverse_root(gram_matrix):
@@ -64,7 +65,6 @@
     key_rows, router_rows = key_grad.shape[1], router_grad.shape[1]
     norm_vecs, norm_width = norm_grad.shape[1:]
     col_width = key_momentum.shape[1]
-    half = PACK_ROWS // n_c
 
     decayed_key = key_weight - (learning_rate * momentum_decay) * key_momentum
     decayed_router = router_weight - (learning_rate * momentum_decay) * router_momentum
@@ -78,36 +78,34 @@
         ],
         axis=0,
     )
-    decayed = jnp.pad(decayed, ((0, 512 - decayed.shape[0]), (0, 0)))
-    decayed, key_error = lax.optimization_barrier((decayed, key_error))
-    decayed = lax.all_gather(decayed, "shard", axis=0, tiled=False)
+    near = lax.ppermute(decayed, "shard", [(i, i ^ 1) for i in range(n_x)])
+    far = lax.ppermute(decayed, "shard", [(i, i ^ 2) for i in range(n_x)])
+    last = lax.ppermute(decayed, "shard", [(i, i ^ 3) for i in range(n_x)])
+    by_distance = jnp.stack([decayed, near, far, last])
 
     merged_key = key_grad[0].astype(f32) + key_error[0]
     merged_router = router_grad[0].astype(f32) + router_error[0]
-    router_lines = rank_size * router_rows // LANES
-    used = rank_size + router_lines + norm_lines
+    router_end = rank_size + router_rows
+    used = router_end + norm_lines
     pack = jnp.concatenate(
         [
             dot(key_basis, merged_key, 1, 1),
-            dot(router_basis, merged_router, 1, 1).reshape(router_lines, LANES),
+            jnp.pad(dot(merged_router, router_basis, 1, 1), ((0, 0), (0, LANES - rank_size))),
             norm_grad[0].astype(f32).reshape(norm_lines, LANES),
             jnp.zeros((PACK_ROWS - used, LANES), f32),
         ],
         axis=0,
     )
-    pair = lax.all_gather(pack, "c", axis=0, tiled=False)
-    mine = jnp.sum(lax.dynamic_slice_in_dim(pair, lax.axis_index("c") * half, half, 1), axis=0)
+    pack = pack.reshape(n_y * n_c, PACK_ROWS // (n_y * n_c), LANES)
+    mine = jnp.sum(lax.all_to_all(pack, PAIRS, 0, 0, tiled=True), axis=0)
     mine = jnp.sum(to_all(mine, "z", n_z), axis=0)
-    spread = to_all(mine, PLANE, plane).reshape(n_y, n_c, n_x, half, LANES)
-    full = jnp.sum(spread, axis=0).transpose(1, 0, 2, 3).reshape(n_x, PACK_ROWS, LANES)
+    full = to_all(mine, PLANE, plane).reshape(n_y * n_c, n_x, PACK_ROWS // (n_y * n_c), LANES)
+    full, by_distance = lax.optimization_barrier((full, by_distance))
+    decayed = jnp.stack([lax.dynamic_index_in_dim(by_distance, lax.axis_index("shard") ^ x, 0, keepdims=False) for x in range(n_x)])
+    full = full.transpose(1, 0, 2, 3).reshape(n_x, PACK_ROWS, LANES)
     rows_key = full[:, :rank_size].transpose(1, 0, 2).reshape(rank_size, n_x * LANES)
-    rows_router = (
-        full[:, rank_size : rank_size + router_lines]
-        .reshape(n_x, rank_size, router_rows)
-        .transpose(1, 0, 2)
-        .reshape(rank_size, n_x * router_rows)
-    )
-    norm_sum = full[:, rank_size + router_lines : used].reshape(n_x, norm_vecs, norm_width)
+    rows_router = full[:, rank_size:router_end, :rank_size].reshape(n_x * router_rows, rank_size).T
+    norm_sum = full[:, router_end:used].reshape(n_x, norm_vecs, norm_width)
 
     grams = jnp.stack([dot(rows_key, rows_key, 1, 1), dot(rows_router, rows_router, 1, 1)])
     roots, scalings = inverse_root(grams)

time: 142 us -> 128 us (0.901)
  blocking collectives: 46.7 us -> 0 us
  starting transfers between devices: 23.5 us -> 57.8 us
  waiting for transfers between devices: 28.9 us -> 43.6 us
  between operations: 15.9 us -> 2.62 us
  local copies, waits for them, and re-layouts: 8.8 us -> 6.86 us
  other arithmetic: 4.71 us -> 3.27 us
    all_to_all x2 -> x0, blocking collectives: 38.3 us -> none  [the longest x1 22.3 us: to_all(): return lax.all_to_all(spread, axes, 0, 0, tiled=True)]
    all_to_all x0 -> x2, starting transfers between devices: none -> 14.2 us  [the longest x1 10.1 us: body(): mine = jnp.sum(lax.all_to_all(pack, PAIRS, 0, 0, tiled=True), axis=0)]
    all_to_all x0 -> x2, waiting for transfers between devices: none -> 13.8 us  [the longest x1 9.25 us: body(): part = lax.all_to_all(part, PLANE, 0, 0, tiled=True)]
    all_to_all x3 -> x4, starting transfers between devices: 23.5 us -> 34.3 us  [to_all(): return lax.all_to_all(spread, axes, 0, 0, tiled=True)]
    ppermute x0 -> x3, starting transfers between devices: none -> 9.34 us  [the longest x1 4.65 us: body(): far = lax.ppermute(decayed, 'shard', [(i, i ^ 2) for i in range(n_x)])]
    all_gather x1 -> x0, blocking collectives: 8.36 us -> none  [body(): pair = lax.all_gather(pack, 'c', axis=0, tiled=False)]
    all_to_all x3 -> x4, waiting for transfers between devices: 28.2 us -> 29.8 us  [to_all(): return lax.all_to_all(spread, axes, 0, 0, tiled=True)]
    transpose x2, other arithmetic: 1.46 us -> 0.01 us  [body(): decayed = jnp.concatenate([decayed_key.T, jnp.pad(decayed_router.T, ((0,...]
  transfers between devices with their start and end apart: 4 -> 9, of which waited for: 3 -> 6; matrix products, arithmetic and copies ran while one was open for 7% -> 2% of each run, Pallas kernels for 0% -> 0%
where the time goes in v2:
time: 128 us; the launch traced here: 127 us
  starting transfers between devices  57.8 us (45%)
  waiting for transfers between devices  43.6 us (34%)
  matrix products  12.9 us (10%)
  local copies, waits for them, and re-layouts  6.86 us (5%)
  other arithmetic  3.27 us (3%)
  between operations  2.62 us (2%)
    all_to_all x4, starting transfers between devices, to_all(): return lax.all_to_all(spread, axes, 0, 0, tiled=True)  34.3 us
    all_to_all x4, waiting for transfers between devices, to_all(): return lax.all_to_all(spread, axes, 0, 0, tiled=True)  29.8 us
    dot_general x12, matrix products, dot(): lax.dot_general(left, right, (((left_dim,), (right_dim,)), ((), ())), pre...  11 us
    all_to_all x1, starting transfers between devices, body(): mine = jnp.sum(lax.all_to_all(pack, PAIRS, 0, 0, tiled=True), axis=0)  10.1 us
    all_to_all x1, waiting for transfers between devices, body(): part = lax.all_to_all(part, PLANE, 0, 0, tiled=True)  9.25 us
    ppermute x1, starting transfers between devices, body(): far = lax.ppermute(decayed, 'shard', [(i, i ^ 2) for i in range(n_x)])  4.65 us
    all_to_all x1, waiting for transfers between devices, body(): mine = jnp.sum(lax.all_to_all(pack, PAIRS, 0, 0, tiled=True), axis=0)  4.55 us
    all_to_all x1, starting transfers between devices, body(): part = lax.all_to_all(part, PLANE, 0, 0, tiled=True)  4.04 us
  transfers between devices with their start and end apart: 9, of which 6 were waited for; matrix products, arithmetic and copies ran while one was open for 2% of the time, Pallas kernels for 0%

profile of v2, /device:TPU:1, one launch (start us, length us, event | category | flops | bytes accessed | tf_op | source)
XLA Modules:
  0.0 127.1 jit_solution(4271702533050963573)
XLA Ops:
  1.5 1.4 %fusion.13 = f32[16,32]{1,0:T(8,128)S(1)} fusion(f32[32,2560]{1,0:T(8,128)} %param.19, f32[1,16,2560]{2,1,0:T(8,128)} %param.16, bf16[1,16,2560]{2,1,0:T(8,128)(2,1)} %param.15), kind=kOutput, calls=%fused_computation.26 | convolution fusion | flops 15810560 | bytes 575488 | tf_op jit(solution)/shard_map/dot_general | solution.py:38
  3.0 2.8 %fusion.9 = f32[32,128]{1,0:T(8,128)S(1)} fusion(f32[32,2560]{1,0:T(8,128)S(1)} %copy-done, f32[1,128,2560]{2,1,0:T(8,128)} %param.14, bf16[1,128,2560]{2,1,0:T(8,128)(2,1)} %param.13), kind=kOutput, calls=%fused_computation.19 | convolution fusion | flops 126484480 | bytes 2310144 | tf_op jit(solution)/shard_map/dot_general | solution.py:38
  6.5 10.1 %all-to-all-start = ((f32[8,8,128]{2,1,0:T(8,128)}), f32[8,8,128]{2,1,0:T(8,128)S(1)}, u32[]{:S(2)}, u32[]{:S(2)}) async-start(f32[8,8,128]{2,1,0:T(8,128)} %fusion.21), calls=%async_computation | async-start | bytes 65536 | tf_op jit(solution)/shard_map/all_to_all | solution.py:100
  16.9 4.6 %all-to-all-done = f32[8,8,128]{2,1,0:T(8,128)S(1)} async-done(((f32[8,8,128]{2,1,0:T(8,128)}), f32[8,8,128]{2,1,0:T(8,128)S(1)}, u32[]{:S(2)}, u32[]{:S(2)}) %all-to-all-start) | async-done | bytes 32800 | tf_op jit(solution)/shard_map/all_to_all | solution.py:100
  22.1 10.7 %all-to-all-start.1 = ((f32[16,8,128]{2,1,0:T(8,128)}), f32[16,8,128]{2,1,0:T(8,128)S(1)}, u32[]{:S(2)}, u32[]{:S(2)}) async-start(f32[16,8,128]{2,1,0:T(8,128)} %broadcast_in_dim.20), calls=%async_computation.1 | async-start | bytes 131072 | tf_op jit(solution)/shard_map/all_to_all | solution.py:43
  32.8 4.7 %collective-permute-start.1 = (f32[50,128]{1,0:T(8,128)S(1)}, f32[50,128]{1,0:T(8,128)S(1)}, u32[]{:S(2)}, u32[]{:S(2)}) collective-permute-start(f32[50,128]{1,0:T(8,128)S(1)} %fusion.24), channel_id=1, source_target_pairs={{0,2},{1,3},{2,0},{3,1},{4,6},{5,7},{6,4},{7,5},{8,10},{9,11},{10,... | collective-permute-start | bytes 76808 | tf_op jit(solution)/shard_map/ppermute | solution.py:82
  37.5 2.2 %collective-permute-start = (f32[50,128]{1,0:T(8,128)S(1)}, f32[50,128]{1,0:T(8,128)S(1)}, u32[]{:S(2)}, u32[]{:S(2)}) collective-permute-start(f32[50,128]{1,0:T(8,128)S(1)} %fusion.24), channel_id=1, source_target_pairs={{0,1},{1,0},{2,3},{3,2},{4,5},{5,4},{6,7},{7,6},{8,9},{9,8},{10,11... | collective-permute-start | bytes 76808 | tf_op jit(solution)/shard_map/ppermute | solution.py:81
  39.7 2.5 %collective-permute-start.2 = (f32[50,128]{1,0:T(8,128)S(1)}, f32[50,128]{1,0:T(8,128)S(1)}, u32[]{:S(2)}, u32[]{:S(2)}) collective-permute-start(f32[50,128]{1,0:T(8,128)S(1)} %fusion.24), channel_id=1, source_target_pairs={{0,3},{1,2},{2,1},{3,0},{4,7},{5,6},{6,5},{7,4},{8,11},{9,10},{10,... | collective-permute-start | bytes 76808 | tf_op jit(solution)/shard_map/ppermute | solution.py:83
  42.2 2.2 %all-to-all-done.1 = f32[16,8,128]{2,1,0:T(8,128)S(1)} async-done(((f32[16,8,128]{2,1,0:T(8,128)}), f32[16,8,128]{2,1,0:T(8,128)S(1)}, u32[]{:S(2)}, u32[]{:S(2)}) %all-to-all-start.1) | async-done | bytes 65568 | tf_op jit(solution)/shard_map/all_to_all | solution.py:43
  45.1 7.2 %all-to-all-start.2 = ((f32[32,8,128]{2,1,0:T(8,128)}), f32[32,8,128]{2,1,0:T(8,128)S(1)}, u32[]{:S(2)}, u32[]{:S(2)}) async-start(f32[32,8,128]{2,1,0:T(8,128)} %broadcast_in_dim.21), calls=%async_computation.2 | async-start | bytes 262144 | tf_op jit(solution)/shard_map/all_to_all | solution.py:43
  52.6 7.3 %all-to-all-done.2 = f32[32,8,128]{2,1,0:T(8,128)S(1)} async-done(((f32[32,8,128]{2,1,0:T(8,128)}), f32[32,8,128]{2,1,0:T(8,128)S(1)}, u32[]{:S(2)}, u32[]{:S(2)}) %all-to-all-start.2) | async-done | bytes 131104 | tf_op jit(solution)/shard_map/all_to_all | solution.py:43
  64.9 0.9 convolution_convert_fusion.1
  66.3 0.7 pad_maximum_fusion
  67.0 4.0 %all-to-all-start.3 = ((bf16[32,8,640]{2,1,0:T(8,128)(2,1)}), bf16[32,8,640]{2,1,0:T(8,128)(2,1)S(1)}, u32[]{:S(2)}, u32[]{:S(2)}) async-start(bf16[32,8,640]{2,1,0:T(8,128)(2,1)} %bitcast.25), calls=%async_computation.3 | async-start | bytes 655360 | tf_op jit(solution)/shard_map/all_to_all | solution.py:122
  71.4 9.2 %all-to-all-done.3 = bf16[32,8,640]{2,1,0:T(8,128)(2,1)S(1)} async-done(((bf16[32,8,640]{2,1,0:T(8,128)(2,1)}), bf16[32,8,640]{2,1,0:T(8,128)(2,1)S(1)}, u32[]{:S(2)}, u32[]{:S(2)}) %all-to-all-start.3) | async-done | bytes 327712 | tf_op jit(solution)/shard_map/all_to_all | solution.py:122
  81.4 8.9 %all-to-all-start.4 = ((bf16[16,8,640]{2,1,0:T(8,128)(2,1)}), bf16[16,8,640]{2,1,0:T(8,128)(2,1)S(1)}, u32[]{:S(2)}, u32[]{:S(2)}) async-start(bf16[16,8,640]{2,1,0:T(8,128)(2,1)} %broadcast_in_dim.22), calls=%async_computation.4 | async-start | bytes 327680 | tf_op jit(solution)/shard_map/all_to_all | solution.py:43
  90.4 12.2 %all-to-all-done.4 = bf16[16,8,640]{2,1,0:T(8,128)(2,1)S(1)} async-done(((bf16[16,8,640]{2,1,0:T(8,128)(2,1)}), bf16[16,8,640]{2,1,0:T(8,128)(2,1)S(1)}, u32[]{:S(2)}, u32[]{:S(2)}) %all-to-all-start.4) | async-done | bytes 163872 | tf_op jit(solution)/shard_map/all_to_all | solution.py:43
  102.7 0.8 broadcast_in_dim.23
  103.4 7.4 %all-to-all-start.5 = ((bf16[32,8,640]{2,1,0:T(8,128)(2,1)}), bf16[32,8,640]{2,1,0:T(8,128)(2,1)S(1)}, u32[]{:S(2)}, u32[]{:S(2)}) async-start(bf16[32,8,640]{2,1,0:T(8,128)(2,1)} %broadcast_in_dim.23), calls=%async_computation.5 | async-start | bytes 655360 | tf_op jit(solution)/shard_map/all_to_all | solution.py:43
  112.2 8.2 %all-to-all-done.5 = bf16[32,8,640]{2,1,0:T(8,128)(2,1)S(1)} async-done(((bf16[32,8,640]{2,1,0:T(8,128)(2,1)}), bf16[32,8,640]{2,1,0:T(8,128)(2,1)S(1)}, u32[]{:S(2)}, u32[]{:S(2)}) %all-to-all-start.5) | async-done | bytes 327712 | tf_op jit(solution)/shard_map/all_to_all | solution.py:43
  120.4 0.9 subtract_convert_fusion.1
  122.7 0.9 subtract_convert_fusion
  124.2 1.0 fusion.1
  125.3 1.8 %fusion = f32[1,128,2560]{2,1,0:T(8,128)} fusion(bf16[32,2560]{1,0:T(8,128)(2,1)S(1)} %bitcast.119, f32[1,128,2560]{2,1,0:T(8,128)S(1)} %copy-done.1, bf16[1,128,2560]{2,1,0:T(8,128)(2,1)S(1)} %copy-done.2, f32[32,512]{1,0:T(8,128)S(1)} %convolution_divide_fusion, s32[]{:T(128)S(6)} %select_n.26), kind=kOutput, calls=%fused_computation.1 | convolution fusion | flops 126812160 | bytes 3457028 | tf_op jit(solution)/shard_map/dot_general | solution.py:38
  (91 shorter events, 11.8 us)
Async XLA Ops:
  0.6 2.3 %copy-start = (f32[32,2560]{1,0:T(8,128)S(1)}, f32[32,2560]{1,0:T(8,128)}, u32[]{:S(2)}) copy-start(f32[32,2560]{1,0:T(8,128)} %param.18) | copy-start | bytes 983044
  3.0 13.7 %copy-start.7 = (f32[16,20]{1,0:T(8,128)S(1)}, f32[16,20]{1,0:T(8,128)}, u32[]{:S(2)}) copy-start(f32[16,20]{1,0:T(8,128)} %param.22) | copy-start | bytes 3844
  3.0 13.7 %copy-start.8 = (f32[16,20]{1,0:T(8,128)S(1)}, f32[16,20]{1,0:T(8,128)}, u32[]{:S(2)}) copy-start(f32[16,20]{1,0:T(8,128)} %param.23) | copy-start | bytes 3844
  3.0 13.7 %copy-start.5 = (f32[128,20]{0,1:T(8,128)S(1)}, f32[128,20]{0,1:T(8,128)}, u32[]{:S(2)}) copy-start(f32[128,20]{0,1:T(8,128)} %param.21) | copy-start | bytes 30724
  3.0 13.7 %copy-start.6 = (f32[128,20]{0,1:T(8,128)S(1)}, f32[128,20]{0,1:T(8,128)}, u32[]{:S(2)}) copy-start(f32[128,20]{0,1:T(8,128)} %param.20) | copy-start | bytes 30724
  3.0 13.7 %copy-start.9 = (f32[2,640]{1,0:T(2,128)S(1)}, f32[2,640]{1,0:T(2,128)}, u32[]{:S(2)}) copy-start(f32[2,640]{1,0:T(2,128)} %param.25) | copy-start | bytes 15364
  3.0 13.7 %copy-start.10 = (f32[2,640]{1,0:T(2,128)S(1)}, f32[2,640]{1,0:T(2,128)}, u32[]{:S(2)}) copy-start(f32[2,640]{1,0:T(2,128)} %param.24) | copy-start | bytes 15364
  6.5 14.9 %all-to-all-start = ((f32[8,8,128]{2,1,0:T(8,128)}), f32[8,8,128]{2,1,0:T(8,128)S(1)}, u32[]{:S(2)}, u32[]{:S(2)}) async-start(f32[8,8,128]{2,1,0:T(8,128)} %fusion.21), calls=%async_computation | async-start | bytes 65536 | tf_op jit(solution)/shard_map/all_to_all | solution.py:100
  22.1 22.3 %all-to-all-start.1 = ((f32[16,8,128]{2,1,0:T(8,128)}), f32[16,8,128]{2,1,0:T(8,128)S(1)}, u32[]{:S(2)}, u32[]{:S(2)}) async-start(f32[16,8,128]{2,1,0:T(8,128)} %broadcast_in_dim.20), calls=%async_computation.1 | async-start | bytes 131072 | tf_op jit(solution)/shard_map/all_to_all | solution.py:43
  32.8 19.6 %collective-permute-start.1 = (f32[50,128]{1,0:T(8,128)S(1)}, f32[50,128]{1,0:T(8,128)S(1)}, u32[]{:S(2)}, u32[]{:S(2)}) collective-permute-start(f32[50,128]{1,0:T(8,128)S(1)} %fusion.24), channel_id=1, source_target_pairs={{0,2},{1,3},{2,0},{3,1},{4,6},{5,7},{6,4},{7,5},{8,10},{9,11},{10,... | collective-permute-start | bytes 76808 | tf_op jit(solution)/shard_map/ppermute | solution.py:82
  37.5 15.0 %collective-permute-start = (f32[50,128]{1,0:T(8,128)S(1)}, f32[50,128]{1,0:T(8,128)S(1)}, u32[]{:S(2)}, u32[]{:S(2)}) collective-permute-start(f32[50,128]{1,0:T(8,128)S(1)} %fusion.24), channel_id=1, source_target_pairs={{0,1},{1,0},{2,3},{3,2},{4,5},{5,4},{6,7},{7,6},{8,9},{9,8},{10,11... | collective-permute-start | bytes 76808 | tf_op jit(solution)/shard_map/ppermute | solution.py:81
  39.7 12.8 %collective-permute-start.2 = (f32[50,128]{1,0:T(8,128)S(1)}, f32[50,128]{1,0:T(8,128)S(1)}, u32[]{:S(2)}, u32[]{:S(2)}) collective-permute-start(f32[50,128]{1,0:T(8,128)S(1)} %fusion.24), channel_id=1, source_target_pairs={{0,3},{1,2},{2,1},{3,0},{4,7},{5,6},{6,5},{7,4},{8,11},{9,10},{10,... | collective-permute-start | bytes 76808 | tf_op jit(solution)/shard_map/ppermute | solution.py:83
  45.1 14.9 %all-to-all-start.2 = ((f32[32,8,128]{2,1,0:T(8,128)}), f32[32,8,128]{2,1,0:T(8,128)S(1)}, u32[]{:S(2)}, u32[]{:S(2)}) async-start(f32[32,8,128]{2,1,0:T(8,128)} %broadcast_in_dim.21), calls=%async_computation.2 | async-start | bytes 262144 | tf_op jit(solution)/shard_map/all_to_all | solution.py:43
  52.3 12.6 %copy-start.1 = (f32[1,128,2560]{2,1,0:T(8,128)S(1)}, f32[1,128,2560]{2,1,0:T(8,128)}, u32[]{:S(2)}) copy-start(f32[1,128,2560]{2,1,0:T(8,128)} %param.14) | copy-start | bytes 3932164
  52.3 12.6 %copy-start.2 = (bf16[1,128,2560]{2,1,0:T(8,128)(2,1)S(1)}, bf16[1,128,2560]{2,1,0:T(8,128)(2,1)}, u32[]{:S(2)}) copy-start(bf16[1,128,2560]{2,1,0:T(8,128)(2,1)} %param.13) | copy-start | bytes 1966084
  64.3 1.5 %copy-start.3 = (f32[1,16,2560]{2,1,0:T(8,128)S(1)}, f32[1,16,2560]{2,1,0:T(8,128)}, u32[]{:S(2)}) copy-start(f32[1,16,2560]{2,1,0:T(8,128)} %param.16) | copy-start | bytes 491524
  64.3 1.5 %copy-start.4 = (bf16[1,16,2560]{2,1,0:T(8,128)(2,1)S(1)}, bf16[1,16,2560]{2,1,0:T(8,128)(2,1)}, u32[]{:S(2)}) copy-start(bf16[1,16,2560]{2,1,0:T(8,128)(2,1)} %param.15) | copy-start | bytes 245764
  67.0 13.6 %all-to-all-start.3 = ((bf16[32,8,640]{2,1,0:T(8,128)(2,1)}), bf16[32,8,640]{2,1,0:T(8,128)(2,1)S(1)}, u32[]{:S(2)}, u32[]{:S(2)}) async-start(bf16[32,8,640]{2,1,0:T(8,128)(2,1)} %bitcast.25), calls=%async_computation.3 | async-start | bytes 655360 | tf_op jit(solution)/shard_map/all_to_all | solution.py:122
  81.4 21.3 %all-to-all-start.4 = ((bf16[16,8,640]{2,1,0:T(8,128)(2,1)}), bf16[16,8,640]{2,1,0:T(8,128)(2,1)S(1)}, u32[]{:S(2)}, u32[]{:S(2)}) async-start(bf16[16,8,640]{2,1,0:T(8,128)(2,1)} %broadcast_in_dim.22), calls=%async_computation.4 | async-start | bytes 327680 | tf_op jit(solution)/shard_map/all_to_all | solution.py:43
  103.4 17.0 %all-to-all-start.5 = ((bf16[32,8,640]{2,1,0:T(8,128)(2,1)}), bf16[32,8,640]{2,1,0:T(8,128)(2,1)S(1)}, u32[]{:S(2)}, u32[]{:S(2)}) async-start(bf16[32,8,640]{2,1,0:T(8,128)(2,1)} %broadcast_in_dim.23), calls=%async_computation.5 | async-start | bytes 655360 | tf_op jit(solution)/shard_map/all_to_all | solution.py:43

commit v3 on v2

--- a/solution.py
+++ b/solution.py
@@ -78,11 +78,6 @@
         ],
         axis=0,
     )
-    near = lax.ppermute(decayed, "shard", [(i, i ^ 1) for i in range(n_x)])
-    far = lax.ppermute(decayed, "shard", [(i, i ^ 2) for i in range(n_x)])
-    last = lax.ppermute(decayed, "shard", [(i, i ^ 3) for i in range(n_x)])
-    by_distance = jnp.stack([decayed, near, far, last])
-
     merged_key = key_grad[0].astype(f32) + key_error[0]
     merged_router = router_grad[0].astype(f32) + router_error[0]
     router_end = rank_size + router_rows
@@ -96,43 +91,65 @@
         ],
         axis=0,
     )
-    pack = pack.reshape(n_y * n_c, PACK_ROWS // (n_y * n_c), LANES)
-    mine = jnp.sum(lax.all_to_all(pack, PAIRS, 0, 0, tiled=True), axis=0)
-    mine = jnp.sum(to_all(mine, "z", n_z), axis=0)
-    full = to_all(mine, PLANE, plane).reshape(n_y * n_c, n_x, PACK_ROWS // (n_y * n_c), LANES)
-    full, by_distance = lax.optimization_barrier((full, by_distance))
-    decayed = jnp.stack([lax.dynamic_index_in_dim(by_distance, lax.axis_index("shard") ^ x, 0, keepdims=False) for x in range(n_x)])
-    full = full.transpose(1, 0, 2, 3).reshape(n_x, PACK_ROWS, LANES)
-    rows_key = full[:, :rank_size].transpose(1, 0, 2).reshape(rank_size, n_x * LANES)
-    rows_router = full[:, rank_size:router_end, :rank_size].reshape(n_x * router_rows, rank_size).T
-    norm_sum = full[:, router_end:used].reshape(n_x, norm_vecs, norm_width)
-
-    grams = jnp.stack([dot(rows_key, rows_key, 1, 1), dot(rows_router, rows_router, 1, 1)])
-    roots, scalings = inverse_root(grams)
-    ortho_key = dot(roots[0], rows_key, 1, 0) / jnp.sqrt(scalings[0])
-    ortho_router = dot(roots[1], rows_router, 1, 0) / jnp.sqrt(scalings[1])
-    shard = lax.axis_index("shard")
-    own_key = lax.dynamic_slice_in_dim(ortho_key, shard * key_rows, key_rows, 1)
-    own_router = lax.dynamic_slice_in_dim(ortho_router, shard * router_rows, router_rows, 1)
-
-    part = jnp.concatenate([dot(own_key, merged_key, 1, 0), dot(own_router, merged_router, 1, 0)])
+    pair = lax.all_gather(pack, "c", axis=0, tiled=False)
+    half = PACK_ROWS // n_c
+    mine = jnp.sum(lax.dynamic_slice_in_dim(pair, lax.axis_index("c") * half, half, 1), axis=0)
+    mine = jnp.sum(to_all(mine.astype(bf16), "z", n_z).astype(f32), axis=0)
+    spread = to_all(mine, PAIRS, n_y * n_c).reshape(n_y, n_c, half, LANES)
+    own = jnp.sum(spread, axis=0).reshape(PACK_ROWS, LANES)
+
+    part = jnp.concatenate(
+        [
+            dot(own[:rank_size], merged_key, 1, 0),
+            dot(own[rank_size:router_end, :rank_size], merged_router, 0, 0),
+        ]
+    )
     groups, lane_groups = 2 * rank_size // 8, plane // (2 * rank_size // 8)
     part = part.astype(bf16).reshape(groups, 8, lane_groups, width // lane_groups)
     part = part.transpose(0, 2, 1, 3).reshape(plane, 8, width // lane_groups)
+    sent = jnp.concatenate([own, decayed])
+    near = lax.ppermute(sent, "shard", [(i, i ^ 1) for i in range(n_x)])
+    far = lax.ppermute(sent, "shard", [(i, i ^ 2) for i in range(n_x)])
+    last = lax.ppermute(sent, "shard", [(i, i ^ 3) for i in range(n_x)])
     part = lax.all_to_all(part, PLANE, 0, 0, tiled=True)
     mine = jnp.sum(part.astype(f32), axis=0).astype(bf16)
-    mine = jnp.sum(to_all(mine, "z", n_z).astype(f32), axis=0) / replicas
-    columns = to_all(mine.astype(bf16), PLANE, plane)
-    columns = columns.reshape(groups, lane_groups, 8, width // lane_groups)
-    columns = columns.transpose(0, 2, 1, 3).reshape(2 * rank_size, width).astype(f32)
-
-    key_carry = (merged_key - dot(own_key, columns[:rank_size], 0, 0))[None]
-    router_carry = (merged_router - dot(own_router, columns[rank_size:], 0, 0))[None]
+    mine, near, far, last = lax.optimization_barrier((mine, near, far, last))
+    by_distance = jnp.stack([sent, near, far, last])
+    some_key = by_distance[:, :rank_size]
+    some_router = by_distance[:, rank_size:router_end, :rank_size]
+    grams = jnp.stack(
+        [
+            lax.dot_general(some_key, some_key, (((0, 2), (0, 2)), ((), ())), precision=highest),
+            lax.dot_general(some_router, some_router, (((0, 1), (0, 1)), ((), ())), precision=highest),
+        ]
+    )
+    roots, scalings = inverse_root(grams)
+    squares = lax.dot_general(roots, roots, (((1,), (1,)), ((0,), (0,))), precision=highest)
+    squares = squares / (scalings * replicas)
+    shard = lax.axis_index("shard")
+    by_shard = jnp.stack(
+        [lax.dynamic_index_in_dim(by_distance, shard ^ x, 0, keepdims=False) for x in range(n_x)]
+    )
+    mine = jnp.sum(to_all(mine, "z", n_z).astype(f32), axis=0).astype(bf16)
+    mine, squares, by_shard = lax.optimization_barrier((mine, squares, by_shard))
+    sums = to_all(mine, PLANE, plane)
+    sums = sums.reshape(groups, lane_groups, 8, width // lane_groups)
+    sums = sums.transpose(0, 2, 1, 3).reshape(2 * rank_size, width).astype(f32)
+
+    rows_key = by_shard[:, :rank_size].transpose(1, 0, 2).reshape(rank_size, n_x * LANES)
+    rows_router = by_shard[:, rank_size:router_end, :rank_size].reshape(n_x * router_rows, rank_size)
+    norm_sum = by_shard[:, router_end:used].reshape(n_x, norm_vecs, norm_width)
+    decayed = by_shard[:, PACK_ROWS:]
+
+    left_key = dot(own[:rank_size], squares[0], 0, 0)
+    left_router = dot(own[rank_size:router_end, :rank_size], squares[1], 1, 0)
+    key_carry = (merged_key - dot(left_key, sums[:rank_size], 1, 0))[None]
+    router_carry = (merged_router - dot(left_router, sums[rank_size:], 1, 0))[None]
 
     offset = lax.axis_index(DP) * col_width
-    few = lax.dynamic_slice_in_dim(columns, offset, col_width, 1)
-    approx_key = dot(ortho_key, few[:rank_size], 0, 0)
-    approx_router = dot(ortho_router, few[rank_size:], 0, 0)
+    few = lax.dynamic_slice_in_dim(sums, offset, col_width, 1)
+    approx_key = dot(rows_key, dot(squares[0], few[:rank_size], 1, 0), 0, 0)
+    approx_router = dot(rows_router, dot(squares[1], few[rank_size:], 1, 0), 1, 0)
     norm_mean = norm_sum / replicas
 
     def advance(momentum, weight, direction):

time: 128 us -> 119 us (0.930)
  starting transfers between devices: 57.8 us -> 47.2 us
  blocking collectives: 0 us -> 8.51 us
  waiting for transfers between devices: 43.6 us -> 39.7 us
  between operations: 2.62 us -> 1.15 us
    all_to_all x1 -> x0, starting transfers between devices: 10.1 us -> none  [body(): mine = jnp.sum(lax.all_to_all(pack, PAIRS, 0, 0, tiled=True), axis=0)]
    all_to_all x1, waiting for transfers between devices: 9.25 us -> 0.48 us  [body(): part = lax.all_to_all(part, PLANE, 0, 0, tiled=True)]
    all_gather x0 -> x1, blocking collectives: none -> 8.51 us  [body(): pair = lax.all_gather(pack, 'c', axis=0, tiled=False)]
    all_to_all x4, waiting for transfers between devices: 29.8 us -> 36.5 us  [to_all(): return lax.all_to_all(spread, axes, 0, 0, tiled=True)]
    all_to_all x1 -> x0, waiting for transfers between devices: 4.55 us -> none  [body(): mine = jnp.sum(lax.all_to_all(pack, PAIRS, 0, 0, tiled=True), axis=0)]
    ppermute x3, waiting for transfers between devices: 0.01 us -> 2.69 us  [the longest x1 1.41 us: body(): far = lax.ppermute(sent, 'shard', [(i, i ^ 2) for i in range(n_x)])]
    all_to_all x4, starting transfers between devices: 34.3 us -> 32.3 us  [to_all(): return lax.all_to_all(spread, axes, 0, 0, tiled=True)]
    all_to_all x1, starting transfers between devices: 4.04 us -> 5.92 us  [body(): part = lax.all_to_all(part, PLANE, 0, 0, tiled=True)]
  transfers between devices with their start and end apart: 9 -> 8, of which waited for: 6 -> 7; matrix products, arithmetic and copies ran while one was open for 2% -> 2% of each run, Pallas kernels for 0% -> 0%
where the time goes in v3:
time: 119 us
  starting transfers between devices  47.2 us (40%)
  waiting for transfers between devices  39.7 us (33%)
  matrix products  13.4 us (11%)
  blocking collectives  8.51 us (7%)
  local copies, waits for them, and re-layouts  6.14 us (5%)
  other arithmetic  2.48 us (2%)
    all_to_all x4, waiting for transfers between devices, to_all(): return lax.all_to_all(spread, axes, 0, 0, tiled=True)  36.5 us
    all_to_all x4, starting transfers between devices, to_all(): return lax.all_to_all(spread, axes, 0, 0, tiled=True)  32.3 us
    dot_general x12, matrix products, dot(): lax.dot_general(left, right, (((left_dim,), (right_dim,)), ((), ())), pre...  10.8 us
    all_gather x1, blocking collectives, body(): pair = lax.all_gather(pack, 'c', axis=0, tiled=False)  8.51 us
    all_to_all x1, starting transfers between devices, body(): part = lax.all_to_all(part, PLANE, 0, 0, tiled=True)  5.92 us
    ppermute x1, starting transfers between devices, body(): last = lax.ppermute(sent, 'shard', [(i, i ^ 3) for i in range(n_x)])  4.5 us
    broadcast_in_dim x4, local copies, waits for them, and re-layouts, to_all(): spread = jnp.broadcast_to(block[None], (size,) + block.shape)  2.77 us
    ppermute x1, starting transfers between devices, body(): far = lax.ppermute(sent, 'shard', [(i, i ^ 2) for i in range(n_x)])  2.48 us
  transfers between devices with their start and end apart: 8, of which 7 were waited for; matrix products, arithmetic and copies ran while one was open for 2% of the time, Pallas kernels for 0%

profile of v3, /device:TPU:1, one launch (start us, length us, event | category | flops | bytes accessed | tf_op | source)
XLA Modules:
  0.0 118.5 jit_solution(1593328802219890333)
XLA Ops:
  1.5 1.4 %fusion.13 = f32[16,32]{1,0:T(8,128)S(1)} fusion(f32[32,2560]{1,0:T(8,128)} %param.19, f32[1,16,2560]{2,1,0:T(8,128)} %param.16, bf16[1,16,2560]{2,1,0:T(8,128)(2,1)} %param.15), kind=kOutput, calls=%fused_computation.27 | convolution fusion | flops 15810560 | bytes 575488 | tf_op jit(solution)/shard_map/dot_general | solution.py:38
  3.0 2.9 %fusion.9 = f32[32,128]{1,0:T(8,128)S(1)} fusion(f32[32,2560]{1,0:T(8,128)S(1)} %copy-done, f32[1,128,2560]{2,1,0:T(8,128)} %param.14, bf16[1,128,2560]{2,1,0:T(8,128)(2,1)} %param.13), kind=kOutput, calls=%fused_computation.19 | convolution fusion | flops 126484480 | bytes 2310144 | tf_op jit(solution)/shard_map/dot_general | solution.py:38
  6.0 8.5 %all-gather = f32[128,128]{1,0:T(8,128)S(1)} all-gather(f32[64,128]{1,0:T(8,128)S(1)} %fusion.23), channel_id=2, replica_groups=mesh['z'=16,'y'=4,'c'=2,'shard'=4] {'c'}, dimensions={0}, use_global_device_ids=true | all-gather | bytes 98304 | tf_op jit(solution)/shard_map/all_gather | solution.py:94
  15.2 9.5 %all-to-all-start = ((bf16[16,32,128]{2,1,0:T(8,128)(2,1)}), bf16[16,32,128]{2,1,0:T(8,128)(2,1)S(1)}, u32[]{:S(2)}, u32[]{:S(2)}) async-start(bf16[16,32,128]{2,1,0:T(8,128)(2,1)} %broadcast_in_dim.19), calls=%async_computation | async-start | bytes 262144 | tf_op jit(solution)/shard_map/all_to_all | solution.py:43
  24.8 12.0 %all-to-all-done = bf16[16,32,128]{2,1,0:T(8,128)(2,1)S(1)} async-done(((bf16[16,32,128]{2,1,0:T(8,128)(2,1)}), bf16[16,32,128]{2,1,0:T(8,128)(2,1)S(1)}, u32[]{:S(2)}, u32[]{:S(2)}) %all-to-all-start) | async-done | bytes 131104 | tf_op jit(solution)/shard_map/all_to_all | solution.py:43
  37.6 7.8 %all-to-all-start.1 = ((f32[8,32,128]{2,1,0:T(8,128)}), f32[8,32,128]{2,1,0:T(8,128)S(1)}, u32[]{:S(2)}, u32[]{:S(2)}) async-start(f32[8,32,128]{2,1,0:T(8,128)} %broadcast_in_dim.20), calls=%async_computation.1 | async-start | bytes 262144 | tf_op jit(solution)/shard_map/all_to_all | solution.py:43
  45.7 5.0 %all-to-all-done.1 = f32[8,32,128]{2,1,0:T(8,128)S(1)} async-done(((f32[8,32,128]{2,1,0:T(8,128)}), f32[8,32,128]{2,1,0:T(8,128)S(1)}, u32[]{:S(2)}, u32[]{:S(2)}) %all-to-all-start.1) | async-done | bytes 131104 | tf_op jit(solution)/shard_map/all_to_all | solution.py:43
  50.7 0.9 convolution_convert_fusion.1
  52.1 0.7 pad_maximum_fusion
  52.9 5.9 %all-to-all-start.2 = ((bf16[32,8,640]{2,1,0:T(8,128)(2,1)}), bf16[32,8,640]{2,1,0:T(8,128)(2,1)S(1)}, u32[]{:S(2)}, u32[]{:S(2)}) async-start(bf16[32,8,640]{2,1,0:T(8,128)(2,1)} %bitcast.9), calls=%async_computation.2 | async-start | bytes 655360 | tf_op jit(solution)/shard_map/all_to_all | solution.py:114
  58.8 4.5 %collective-permute-start.2 = (f32[114,128]{1,0:T(8,128)S(1)}, f32[114,128]{1,0:T(8,128)S(1)}, u32[]{:S(2)}, u32[]{:S(2)}) collective-permute-start(f32[114,128]{1,0:T(8,128)S(1)} %fusion.19), channel_id=1, source_target_pairs={{0,3},{1,2},{2,1},{3,0},{4,7},{5,6},{6,5},{7,4},{8,11},{9,10},{10,... | collective-permute-start | bytes 175112 | tf_op jit(solution)/shard_map/ppermute | solution.py:113
  63.3 2.5 %collective-permute-start.1 = (f32[114,128]{1,0:T(8,128)S(1)}, f32[114,128]{1,0:T(8,128)S(1)}, u32[]{:S(2)}, u32[]{:S(2)}) collective-permute-start(f32[114,128]{1,0:T(8,128)S(1)} %fusion.19), channel_id=1, source_target_pairs={{0,2},{1,3},{2,0},{3,1},{4,6},{5,7},{6,4},{7,5},{8,10},{9,11},{10,... | collective-permute-start | bytes 175112 | tf_op jit(solution)/shard_map/ppermute | solution.py:112
  65.8 2.0 %collective-permute-start = (f32[114,128]{1,0:T(8,128)S(1)}, f32[114,128]{1,0:T(8,128)S(1)}, u32[]{:S(2)}, u32[]{:S(2)}) collective-permute-start(f32[114,128]{1,0:T(8,128)S(1)} %fusion.19), channel_id=1, source_target_pairs={{0,1},{1,0},{2,3},{3,2},{4,5},{5,4},{6,7},{7,6},{8,9},{9,8},{10,11... | collective-permute-start | bytes 175112 | tf_op jit(solution)/shard_map/ppermute | solution.py:111
  68.4 1.4 %collective-permute-done.1 = f32[114,128]{1,0:T(8,128)S(1)} collective-permute-done((f32[114,128]{1,0:T(8,128)S(1)}, f32[114,128]{1,0:T(8,128)S(1)}, u32[]{:S(2)}, u32[]{:S(2)}) %collective-permute-start.1) | collective-permute-done | bytes 58400 | tf_op jit(solution)/shard_map/ppermute | solution.py:112
  69.8 1.3 %collective-permute-done = f32[114,128]{1,0:T(8,128)S(1)} collective-permute-done((f32[114,128]{1,0:T(8,128)S(1)}, f32[114,128]{1,0:T(8,128)S(1)}, u32[]{:S(2)}, u32[]{:S(2)}) %collective-permute-start) | collective-permute-done | bytes 58400 | tf_op jit(solution)/shard_map/ppermute | solution.py:111
  74.0 3.8 %all-to-all-start.3 = ((bf16[16,8,640]{2,1,0:T(8,128)(2,1)}), bf16[16,8,640]{2,1,0:T(8,128)(2,1)S(1)}, u32[]{:S(2)}, u32[]{:S(2)}) async-start(bf16[16,8,640]{2,1,0:T(8,128)(2,1)} %broadcast_in_dim.21), calls=%async_computation.3 | async-start | bytes 327680 | tf_op jit(solution)/shard_map/all_to_all | solution.py:43
  78.5 11.5 %all-to-all-done.3 = bf16[16,8,640]{2,1,0:T(8,128)(2,1)S(1)} async-done(((bf16[16,8,640]{2,1,0:T(8,128)(2,1)}), bf16[16,8,640]{2,1,0:T(8,128)(2,1)S(1)}, u32[]{:S(2)}, u32[]{:S(2)}) %all-to-all-start.3) | async-done | bytes 163872 | tf_op jit(solution)/shard_map/all_to_all | solution.py:43
  90.2 0.8 broadcast_in_dim.23
  91.0 11.1 %all-to-all-start.4 = ((bf16[32,8,640]{2,1,0:T(8,128)(2,1)}), bf16[32,8,640]{2,1,0:T(8,128)(2,1)S(1)}, u32[]{:S(2)}, u32[]{:S(2)}) async-start(bf16[32,8,640]{2,1,0:T(8,128)(2,1)} %broadcast_in_dim.23), calls=%async_computation.4 | async-start | bytes 655360 | tf_op jit(solution)/shard_map/all_to_all | solution.py:43
  103.7 7.9 %all-to-all-done.4 = bf16[32,8,640]{2,1,0:T(8,128)(2,1)S(1)} async-done(((bf16[32,8,640]{2,1,0:T(8,128)(2,1)}), bf16[32,8,640]{2,1,0:T(8,128)(2,1)S(1)}, u32[]{:S(2)}, u32[]{:S(2)}) %all-to-all-start.4) | async-done | bytes 327712 | tf_op jit(solution)/shard_map/all_to_all | solution.py:43
  112.2 0.8 subtract_convert_fusion.2
  114.4 0.8 subtract_convert_fusion
  115.8 0.9 fusion.1
  116.7 1.8 %fusion = f32[1,128,2560]{2,1,0:T(8,128)} fusion(f32[128,32]{0,1:T(8,128)S(1)} %fusion.32, bf16[32,2560]{1,0:T(8,128)(2,1)S(1)} %bitcast.127, f32[1,128,2560]{2,1,0:T(8,128)S(1)} %copy-done.1, bf16[1,128,2560]{2,1,0:T(8,128)(2,1)S(1)} %copy-done.2), kind=kOutput, calls=%fused_computation.1 | convolution fusion | flops 126812160 | bytes 3457024 | tf_op jit(solution)/shard_map/dot_general | solution.py:38
  (88 shorter events, 11.5 us)
Async XLA Ops:
  0.6 2.3 %copy-start = (f32[32,2560]{1,0:T(8,128)S(1)}, f32[32,2560]{1,0:T(8,128)}, u32[]{:S(2)}) copy-start(f32[32,2560]{1,0:T(8,128)} %param.18) | copy-start | bytes 983044
  3.0 21.8 %copy-start.9 = (f32[2,640]{1,0:T(2,128)S(1)}, f32[2,640]{1,0:T(2,128)}, u32[]{:S(2)}) copy-start(f32[2,640]{1,0:T(2,128)} %param.25) | copy-start | bytes 15364
  3.0 21.8 %copy-start.10 = (f32[2,640]{1,0:T(2,128)S(1)}, f32[2,640]{1,0:T(2,128)}, u32[]{:S(2)}) copy-start(f32[2,640]{1,0:T(2,128)} %param.24) | copy-start | bytes 15364
  3.0 21.8 %copy-start.7 = (f32[16,20]{1,0:T(8,128)S(1)}, f32[16,20]{1,0:T(8,128)}, u32[]{:S(2)}) copy-start(f32[16,20]{1,0:T(8,128)} %param.22) | copy-start | bytes 3844
  3.0 21.8 %copy-start.8 = (f32[16,20]{1,0:T(8,128)S(1)}, f32[16,20]{1,0:T(8,128)}, u32[]{:S(2)}) copy-start(f32[16,20]{1,0:T(8,128)} %param.23) | copy-start | bytes 3844
  3.0 21.8 %copy-start.5 = (f32[128,20]{0,1:T(8,128)S(1)}, f32[128,20]{0,1:T(8,128)}, u32[]{:S(2)}) copy-start(f32[128,20]{0,1:T(8,128)} %param.21) | copy-start | bytes 30724
  3.0 21.8 %copy-start.6 = (f32[128,20]{0,1:T(8,128)S(1)}, f32[128,20]{0,1:T(8,128)}, u32[]{:S(2)}) copy-start(f32[128,20]{0,1:T(8,128)} %param.20) | copy-start | bytes 30724
  3.0 47.7 %copy-start.2 = (bf16[1,128,2560]{2,1,0:T(8,128)(2,1)S(1)}, bf16[1,128,2560]{2,1,0:T(8,128)(2,1)}, u32[]{:S(2)}) copy-start(bf16[1,128,2560]{2,1,0:T(8,128)(2,1)} %param.13) | copy-start | bytes 1966084
  5.9 44.8 %copy-start.1 = (f32[1,128,2560]{2,1,0:T(8,128)S(1)}, f32[1,128,2560]{2,1,0:T(8,128)}, u32[]{:S(2)}) copy-start(f32[1,128,2560]{2,1,0:T(8,128)} %param.14) | copy-start | bytes 3932164
  15.2 21.7 %all-to-all-start = ((bf16[16,32,128]{2,1,0:T(8,128)(2,1)}), bf16[16,32,128]{2,1,0:T(8,128)(2,1)S(1)}, u32[]{:S(2)}, u32[]{:S(2)}) async-start(bf16[16,32,128]{2,1,0:T(8,128)(2,1)} %broadcast_in_dim.19), calls=%async_computation | async-start | bytes 262144 | tf_op jit(solution)/shard_map/all_to_all | solution.py:43
  37.6 14.0 %copy-start.3 = (f32[1,16,2560]{2,1,0:T(8,128)S(1)}, f32[1,16,2560]{2,1,0:T(8,128)}, u32[]{:S(2)}) copy-start(f32[1,16,2560]{2,1,0:T(8,128)} %param.16) | copy-start | bytes 491524
  37.6 14.0 %copy-start.4 = (bf16[1,16,2560]{2,1,0:T(8,128)(2,1)S(1)}, bf16[1,16,2560]{2,1,0:T(8,128)(2,1)}, u32[]{:S(2)}) copy-start(bf16[1,16,2560]{2,1,0:T(8,128)(2,1)} %param.15) | copy-start | bytes 245764
  37.6 13.1 %all-to-all-start.1 = ((f32[8,32,128]{2,1,0:T(8,128)}), f32[8,32,128]{2,1,0:T(8,128)S(1)}, u32[]{:S(2)}, u32[]{:S(2)}) async-start(f32[8,32,128]{2,1,0:T(8,128)} %broadcast_in_dim.20), calls=%async_computation.1 | async-start | bytes 262144 | tf_op jit(solution)/shard_map/all_to_all | solution.py:43
  52.9 15.5 %all-to-all-start.2 = ((bf16[32,8,640]{2,1,0:T(8,128)(2,1)}), bf16[32,8,640]{2,1,0:T(8,128)(2,1)S(1)}, u32[]{:S(2)}, u32[]{:S(2)}) async-start(bf16[32,8,640]{2,1,0:T(8,128)(2,1)} %bitcast.9), calls=%async_computation.2 | async-start | bytes 655360 | tf_op jit(solution)/shard_map/all_to_all | solution.py:114
  58.8 9.6 %collective-permute-start.2 = (f32[114,128]{1,0:T(8,128)S(1)}, f32[114,128]{1,0:T(8,128)S(1)}, u32[]{:S(2)}, u32[]{:S(2)}) collective-permute-start(f32[114,128]{1,0:T(8,128)S(1)} %fusion.19), channel_id=1, source_target_pairs={{0,3},{1,2},{2,1},{3,0},{4,7},{5,6},{6,5},{7,4},{8,11},{9,10},{10,... | collective-permute-start | bytes 175112 | tf_op jit(solution)/shard_map/ppermute | solution.py:113
  63.3 6.5 %collective-permute-start.1 = (f32[114,128]{1,0:T(8,128)S(1)}, f32[114,128]{1,0:T(8,128)S(1)}, u32[]{:S(2)}, u32[]{:S(2)}) collective-permute-start(f32[114,128]{1,0:T(8,128)S(1)} %fusion.19), channel_id=1, source_target_pairs={{0,2},{1,3},{2,0},{3,1},{4,6},{5,7},{6,4},{7,5},{8,10},{9,11},{10,... | collective-permute-start | bytes 175112 | tf_op jit(solution)/shard_map/ppermute | solution.py:112
  65.8 5.3 %collective-permute-start = (f32[114,128]{1,0:T(8,128)S(1)}, f32[114,128]{1,0:T(8,128)S(1)}, u32[]{:S(2)}, u32[]{:S(2)}) collective-permute-start(f32[114,128]{1,0:T(8,128)S(1)} %fusion.19), channel_id=1, source_target_pairs={{0,1},{1,0},{2,3},{3,2},{4,5},{5,4},{6,7},{7,6},{8,9},{9,8},{10,11... | collective-permute-start | bytes 175112 | tf_op jit(solution)/shard_map/ppermute | solution.py:111
  74.0 16.0 %all-to-all-start.3 = ((bf16[16,8,640]{2,1,0:T(8,128)(2,1)}), bf16[16,8,640]{2,1,0:T(8,128)(2,1)S(1)}, u32[]{:S(2)}, u32[]{:S(2)}) async-start(bf16[16,8,640]{2,1,0:T(8,128)(2,1)} %broadcast_in_dim.21), calls=%async_computation.3 | async-start | bytes 327680 | tf_op jit(solution)/shard_map/all_to_all | solution.py:43
  91.0 20.6 %all-to-all-start.4 = ((bf16[32,8,640]{2,1,0:T(8,128)(2,1)}), bf16[32,8,640]{2,1,0:T(8,128)(2,1)S(1)}, u32[]{:S(2)}, u32[]{:S(2)}) async-start(bf16[32,8,640]{2,1,0:T(8,128)(2,1)} %broadcast_in_dim.23), calls=%async_computation.4 | async-start | bytes 655360 | tf_op jit(solution)/shard_map/all_to_all | solution.py:43

commit v4 on v3

v4 whole, which is shorter than its diff:
```python
import jax
import jax.numpy as jnp
from jax import lax
from jax.experimental import pallas as pl
from jax.experimental.pallas import tpu as pltpu
from jax.sharding import Mesh, PartitionSpec as P

ROOT_STEPS = 4

highest = lax.Precision.HIGHEST
momentum_decay = 0.9
learning_rate = 0.1
f32 = jnp.float32
bf16 = jnp.bfloat16

DP = ("z", "y", "c")
PAIRS = ("y", "c")
PLANE = ("y", "c", "shard")
LANES = 128
PACK_ROWS = 64
KEY_AT, ROUTER_AT, NORM_AT = 64, 88, 104


def dot(left, right, left_dim, right_dim):
    return lax.dot_general(left, right, (((left_dim,), (right_dim,)), ((), ())), precision=highest)


def in_vmem(array):
    return pltpu.with_memory_space_constraint(array, pltpu.VMEM)


def head_kernel(kb_ref, rb_ref, kg_ref, ke_ref, rg_ref, re_ref, ng_ref, out_ref):
    rank_size, router_rows = kb_ref.shape[0], rg_ref.shape[1]
    norm_vecs, norm_width = ng_ref.shape[1:]
    router_end = rank_size + router_rows

    @pl.when(pl.program_id(0) == 0)
    def _():
        out_ref[...] = jnp.zeros_like(out_ref)
        norm = ng_ref[0].astype(f32)
        lines = norm_width // LANES
        for vec in range(norm_vecs):
            for line in range(lines):
                row = router_end + vec * lines + line
                out_ref[row : row + 1, :] = norm[vec : vec + 1, line * LANES : (line + 1) * LANES]

    merged_key = kg_ref[0].astype(f32) + ke_ref[0]
    merged_router = rg_ref[0].astype(f32) + re_ref[0]
    out_ref[:rank_size, :] += dot(kb_ref[...], merged_key, 1, 1)
    out_ref[rank_size:router_end, :rank_size] += dot(merged_router, rb_ref[...], 1, 1)


def head(key_basis, router_basis, key_grad, key_error, router_grad, router_error, norm_grad):
    rank_size, width = key_basis.shape
    key_rows, router_rows = key_grad.shape[1], router_grad.shape[1]
    steps = 5
    block = width // steps
    return pl.pallas_call(
        head_kernel,
        grid=(steps,),
        in_specs=[
            pl.BlockSpec((rank_size, block), lambda i: (0, i)),
            pl.BlockSpec((rank_size, block), lambda i: (0, i)),
            pl.BlockSpec((1, key_rows, block), lambda i: (0, 0, i)),
            pl.BlockSpec((1, key_rows, block), lambda i: (0, 0, i)),
            pl.BlockSpec((1, router_rows, block), lambda i: (0, 0, i)),
            pl.BlockSpec((1, router_rows, block), lambda i: (0, 0, i)),
            pl.BlockSpec(norm_grad.shape, lambda i: (0, 0, 0)),
        ],
        out_specs=pl.BlockSpec((PACK_ROWS, LANES), lambda i: (0, 0)),
        out_shape=jax.ShapeDtypeStruct((PACK_ROWS, LANES), f32),
        name="head",
    )(key_basis, router_basis, key_grad, key_error, router_grad, router_error, norm_grad)


def square_of_root(gram, replicas):
    scaling = jnp.sqrt(jnp.sum(gram * gram, axis=(0, 1), keepdims=True)) + 1e-06
    rows = lax.broadcasted_iota(jnp.int32, gram.shape, 0)
    identity = (rows == lax.broadcasted_iota(jnp.int32, gram.shape, 1)).astype(f32)
    square_side, root_side = gram / scaling, identity
    for sweep_index in range(ROOT_STEPS):
        middle = 1.5 * identity - 0.5 * dot(root_side, square_side, 1, 0)
        square_side = dot(square_side, middle, 1, 0)
        root_side = dot(middle, root_side, 1, 0)
    return dot(root_side, root_side, 0, 0) / (scaling * replicas)


def side_kernel(replicas, rank_size, router_rows, col_width, *refs):
    packs = [ref.at[i] for ref in refs[:2] for i in range(2)]
    outs = refs[2:]
    lk_ref, lt_ref, lr_ref, dk_ref, dr_ref, ns_ref, dn_ref = outs
    router_end = rank_size + router_rows
    shard = lax.axis_index("shard")
    key_rows = [pack[:rank_size, :] for pack in packs]
    rout_rows = [pack[rank_size:router_end, :rank_size] for pack in packs]
    square_key = square_of_root(sum(dot(rows, rows, 1, 1) for rows in key_rows), replicas)
    square_router = square_of_root(sum(dot(rows, rows, 0, 0) for rows in rout_rows), replicas)
    lk_ref[...] = dot(key_rows[0], square_key, 0, 0)
    for distance, pack in enumerate(packs):
        place = lax.bitwise_xor(shard, distance)
        lanes = pl.ds(pl.multiple_of(place * LANES, LANES), LANES)
        lines = pl.ds(pl.multiple_of(place * router_rows, router_rows), router_rows)
        lt_ref[:, lanes] = dot(square_key, key_rows[distance], 0, 0)
        lr_ref[lines, :] = dot(rout_rows[distance], square_router, 1, 0)
        dk_ref[:, lanes] = pack[KEY_AT : KEY_AT + col_width, :]
        dr_ref[lines, :] = pack[ROUTER_AT : ROUTER_AT + router_rows, :]
        ns_ref[place] = pack[router_end : router_end + 16, :]
        dn_ref[place] = pack[NORM_AT : NORM_AT + 16, :]


def side(packs, replicas, rank_size, router_rows, col_width):
    n_x = 2 * len(packs)
    shapes = [
        (LANES, rank_size),
        (rank_size, n_x * LANES),
        (n_x * router_rows, rank_size),
        (col_width, n_x * LANES),
        (n_x * router_rows, LANES),
        (n_x, 16, LANES),
        (n_x, 16, LANES),
    ]
    return pl.pallas_call(
        lambda *refs: side_kernel(replicas, rank_size, router_rows, col_width, *refs),
        out_shape=[jax.ShapeDtypeStruct(shape, f32) for shape in shapes],
        in_specs=[pl.BlockSpec(memory_space=pltpu.VMEM)] * len(packs),
        out_specs=[pl.BlockSpec(memory_space=pltpu.VMEM)] * len(shapes),
        cost_estimate=pl.CostEstimate(flops=200000000, bytes_accessed=8000000, transcendentals=0),
        name="side",
    )(*[in_vmem(x) for x in packs])


def tail_kernel(
    t_ref, kg_ref, ke_ref, rg_ref, re_ref, lk_ref, lt_ref, lr_ref, dk_ref, dr_ref, km_ref, kw_ref, rm_ref, rw_ref,
    kc_ref, rc_ref, kv_ref, kn_ref, kp_ref, rv_ref, rn_ref, rp_ref,
):
    groups, lane_groups, _, block = t_ref.shape
    rank_size = groups * 4
    half = groups // 2
    router_rows, col_width = rm_ref.shape
    shard = lax.axis_index("shard")
    step = pl.program_id(0)
    own_lines = pl.ds(pl.multiple_of(shard * router_rows, router_rows), router_rows)

    def sums(first, lane_group):
        return jnp.concatenate([t_ref[first + i, lane_group].astype(f32) for i in range(half)], axis=0)

    def apply(left, right):
        high = left.astype(bf16)
        low = (left - high.astype(f32)).astype(bf16)
        terms = [
            lax.dot_general(term, right, (((1,), (0,)), ((), ())), preferred_element_type=f32)
            for term in (high, low)
        ]
        return terms[0] + terms[1]

    key_sums = sums(0, step).astype(bf16)
    router_sums = sums(half, step).astype(bf16)
    cols = pl.ds(pl.multiple_of(step * block, LANES), block)
    kc_ref[0] = kg_ref[0, :, cols].astype(f32) + ke_ref[0, :, cols] - apply(lk_ref[...], key_sums)
    rc_ref[0] = rg_ref[0, :, cols].astype(f32) + re_ref[0, :, cols] - apply(lr_ref[own_lines, :], router_sums)

    @pl.when(step == 0)
    def _():
        place = (lax.axis_index("z") * lax.axis_size("y") + lax.axis_index("y")) * lax.axis_size("c")
        column = (place + lax.axis_index("c")) * col_width
        lane_group = column // block
        offset = column - lane_group * block
        lines = lax.broadcasted_iota(jnp.int32, (block, LANES), 0)
        picks = lines == lax.broadcasted_iota(jnp.int32, (block, LANES), 1) + offset
        picks = picks.astype(f32).astype(bf16)

        def few(first):
            return lax.dot_general(
                sums(first, lane_group).astype(bf16), picks, (((1,), (0,)), ((), ())), preferred_element_type=f32
            )

        few_key, few_router = few(0), few(half)
        approx = dot(few_key, lt_ref[...], 0, 0)[:col_width]
        kp_ref[...] = (dk_ref[...] - learning_rate * approx).astype(bf16)
        own_lanes = pl.ds(pl.multiple_of(shard * LANES, LANES), LANES)
        own = dot(few_key, lt_ref[:, own_lanes], 0, 0)[:col_width]
        velocity = momentum_decay * km_ref[...] + own
        kv_ref[...] = velocity
        kn_ref[...] = kw_ref[...] - learning_rate * velocity
        approx = dr_ref[...] - learning_rate * dot(lr_ref[...], few_router, 1, 0)
        rp_ref[...] = approx.T[:col_width].astype(bf16)
        own = dot(lr_ref[own_lines, :], few_router, 1, 0)[:, :col_width]
        velocity = momentum_decay * rm_ref[...] + own
        rv_ref[...] = velocity
        rn_ref[...] = rw_ref[...] - learning_rate * velocity


def tail(sums, key_grad, key_error, router_grad, router_error, *small):
    lane_groups, block = sums.shape[1], sums.shape[3]
    key_rows, router_rows = key_grad.shape[1], router_grad.shape[1]
    dk, dr, km, rm = small[3], small[4], small[5], small[7]
    wide = [
        pl.BlockSpec((1, key_rows, block), lambda i: (0, 0, i)),
        pl.BlockSpec((1, router_rows, block), lambda i: (0, 0, i)),
    ]

    def whole(shape):
        return pl.BlockSpec(shape, lambda i: (0,) * len(shape))

    outs = [
        (key_grad.shape, f32),
        (router_grad.shape, f32),
        (km.shape, f32),
        (km.shape, f32),
        (dk.shape, bf16),
        (rm.shape, f32),
        (rm.shape, f32),
        ((dk.shape[0], dr.shape[0]), bf16),
    ]
    return pl.pallas_call(
        tail_kernel,
        grid=(lane_groups,),
        in_specs=[pl.BlockSpec(memory_space=pltpu.VMEM)] * (5 + len(small)),
        out_specs=wide + [whole(shape) for shape, _ in outs[2:]],
        out_shape=[jax.ShapeDtypeStruct(shape, dtype) for shape, dtype in outs],
        name="tail",
    )(*[in_vmem(x) for x in (sums, key_grad, key_error, router_grad, router_error) + small])


def to_all(block, axes, size):
    spread = jnp.broadcast_to(block[None], (size,) + block.shape)
    return lax.all_to_all(spread, axes, 0, 0, tiled=True)


def body(
    key_grad,
    key_error,
    router_grad,
    router_error,
    norm_grad,
    key_basis,
    router_basis,
    key_momentum,
    key_weight,
    router_momentum,
    router_weight,
    norm_momentum,
    norm_weight,
):
    n_z, n_y, n_c, n_x = (lax.axis_size(name) for name in DP + ("shard",))
    plane = n_y * n_c * n_x
    replicas = n_z * n_y * n_c
    rank_size, width = key_basis.shape
    key_rows, router_rows = key_grad.shape[1], router_grad.shape[1]
    norm_vecs, norm_width = norm_grad.shape[1:]
    col_width = key_momentum.shape[1]

    decayed_key = key_weight - (learning_rate * momentum_decay) * key_momentum
    decayed_router = router_weight - (learning_rate * momentum_decay) * router_momentum
    decayed_norm = norm_weight - (learning_rate * momentum_decay) * norm_momentum
    norm_lines = norm_vecs * norm_width // LANES
    decayed = jnp.concatenate(
        [
            jnp.pad(decayed_key.T, ((0, ROUTER_AT - KEY_AT - col_width), (0, 0))),
            jnp.pad(decayed_router, ((0, 0), (0, LANES - col_width))),
            jnp.pad(decayed_norm.reshape(norm_lines, LANES), ((0, 16 - norm_lines), (0, 0))),
        ],
        axis=0,
    )

    merged = jnp.concatenate(
        [key_grad[0].astype(f32) + key_error[0], router_grad[0].astype(f32) + router_error[0]]
    )
    router_end = rank_size + router_rows
    used = router_end + norm_lines
    pack = head(key_basis, router_basis, key_grad, key_error, router_grad, router_error, norm_grad)
    pair = lax.all_gather(pack, "c", axis=0, tiled=False)
    half = PACK_ROWS // n_c
    mine = jnp.sum(lax.dynamic_slice_in_dim(pair, lax.axis_index("c") * half, half, 1), axis=0)
    mine = jnp.sum(to_all(mine.astype(bf16), "z", n_z).astype(f32), axis=0)
    spread = to_all(mine, PAIRS, n_y * n_c).reshape(n_y, n_c, half, LANES)
    own = jnp.sum(spread, axis=0).reshape(PACK_ROWS, LANES)

    left = jnp.concatenate(
        [
            jnp.pad(own[:rank_size], ((0, 0), (0, router_rows))),
            jnp.pad(own[rank_size:router_end, :rank_size].T, ((0, 0), (key_rows, 0))),
        ]
    )
    part = lax.dot_general(left, merged, (((1,), (0,)), ((), ())), precision=lax.Precision.HIGH)
    groups, lane_groups = 2 * rank_size // 8, plane // (2 * rank_size // 8)
    part = part.astype(bf16).reshape(groups, 8, lane_groups, width // lane_groups)
    part = part.transpose(0, 2, 1, 3).reshape(plane, 8, width // lane_groups)
    sent = jnp.concatenate([own, decayed])
    near = lax.ppermute(sent, "shard", [(i, i ^ 1) for i in range(n_x)])
    part = lax.all_to_all(part, PLANE, 0, 0, tiled=True)
    mine = jnp.sum(part.astype(f32), axis=0).astype(bf16)
    mine, near = lax.optimization_barrier((mine, near))
    packs = jnp.stack([sent, near])
    far = lax.ppermute(packs, "shard", [(i, i ^ 2) for i in range(n_x)])
    *lefts, norm_sum, decayed_norm = side([packs, far], replicas, rank_size, router_rows, col_width)
    mine = jnp.sum(to_all(mine, "z", n_z).astype(f32), axis=0).astype(bf16)
    mine, lefts, norm_sum, decayed_norm = lax.optimization_barrier((mine, lefts, norm_sum, decayed_norm))
    sums = to_all(mine, PLANE, plane).reshape(groups, lane_groups, 8, width // lane_groups)
    (key_carry, router_carry, key_velocity, key_master, key_params, router_velocity, router_master, router_params) = (
        tail(
            sums,
            key_grad,
            key_error,
            router_grad,
            router_error,
            *lefts,
            key_momentum.T,
            key_weight.T,
            router_momentum,
            router_weight,
        )
    )

    norm_mean = norm_sum[:, :norm_lines].reshape(n_x, norm_vecs, norm_width) / replicas
    shard = lax.axis_index("shard")
    def advance(momentum, weight, direction):
        velocity = momentum_decay * momentum + direction
        return velocity, weight - learning_rate * velocity

    norm_velocity, norm_master = advance(
        norm_momentum, norm_weight, lax.dynamic_index_in_dim(norm_mean, shard, 0, keepdims=False)
    )

    all_norm = decayed_norm[:, :norm_lines].reshape(n_x, norm_vecs, norm_width)
    norm_params = (all_norm - learning_rate * norm_mean).astype(bf16)
    norm_params = norm_params.transpose(1, 0, 2).reshape(norm_vecs, n_x * norm_width)
    return (
        key_carry,
        router_carry,
        key_velocity.T,
        key_master.T,
        key_params.T,
        router_velocity,
        router_master,
        router_params.T,
        norm_velocity,
        norm_master,
        norm_params,
    )


def solution(mesh):
    n_dp, n_x = mesh.devices.shape
    fine = Mesh(mesh.devices.reshape(n_dp // 8, 4, 2, n_x), DP + ("shard",))
    return jax.shard_map(
        body,
        mesh=fine,
        in_specs=(
            P(DP, "shard", None),
            P(DP, "shard", None),
            P(DP, "shard", None),
            P(DP, "shard", None),
            P(DP, None, "shard"),
            P(),
            P(),
            P("shard", DP),
            P("shard", DP),
            P("shard", DP),
            P("shard", DP),
            P(None, "shard"),
            P(None, "shard"),
        ),
        out_specs=(
            P(DP, "shard", None),
            P(DP, "shard", None),
            P("shard", DP),
            P("shard", DP),
            P(None, DP),
            P("shard", DP),
            P("shard", DP),
            P(None, DP),
            P(None, "shard"),
            P(None, "shard"),
            P(),
        ),
        check_vma=False,
    )
```

time: 119 us -> 107 us (0.90)
  Pallas kernels: 0 us -> 12.9 us
  matrix products: 13.4 us -> 1.42 us
  starting transfers between devices: 47.2 us -> 40.7 us
  waiting for transfers between devices: 39.7 us -> 35.1 us
  local copies, waits for them, and re-layouts: 6.14 us -> 3.61 us
    all_to_all x4, waiting for transfers between devices: 36.5 us -> 23.5 us  [to_all(): return lax.all_to_all(spread, axes, 0, 0, tiled=True)]
    pallas_call x0 -> x3, Pallas kernels: none -> 12.9 us  [the longest x1 5.21 us: head(): pl.pallas_call(head_kernel, grid=(steps,), in_specs=[pl.BlockSpec((rank_s...]
    dot_general x26 -> x1, matrix products: 13.4 us -> 1.42 us  [body(): lax.dot_general(left, merged, (((1,), (0,)), ((), ())), precision=lax.Pre...]
    all_to_all x1, waiting for transfers between devices: 0.48 us -> 6.32 us  [body(): part = lax.all_to_all(part, PLANE, 0, 0, tiled=True)]
    ppermute x2 -> x1, starting transfers between devices: 6.99 us -> 2.61 us  [body(): far = lax.ppermute(packs, 'shard', [(i, i ^ 2) for i in range(n_x)])]
    ppermute x2 -> x1, waiting for transfers between devices: 1.41 us -> 5.25 us  [body(): far = lax.ppermute(packs, 'shard', [(i, i ^ 2) for i in range(n_x)])]
    all_to_all x4, starting transfers between devices: 32.3 us -> 28.9 us  [to_all(): return lax.all_to_all(spread, axes, 0, 0, tiled=True)]
    unnamed x29 -> x37, local copies, waits for them, and re-layouts: 1.72 us -> 0.19 us
  transfers between devices with their start and end apart: 8 -> 7, of which waited for: 7 -> 5; matrix products, arithmetic and copies ran while one was open for 2% -> 3% of each run, Pallas kernels for 0% -> 4%
where the time goes in v4:
time: 107 us; the launch traced here: 106 us
  starting transfers between devices  40.7 us (38%)
  waiting for transfers between devices  35.1 us (33%)
  Pallas kernels  12.9 us (12%)
  blocking collectives  8.58 us (8%)
  local copies, waits for them, and re-layouts  3.61 us (3%)
  other arithmetic  2.8 us (3%)
  matrix products  1.42 us (1%)
    all_to_all x4, starting transfers between devices, to_all(): return lax.all_to_all(spread, axes, 0, 0, tiled=True)  28.9 us
    all_to_all x4, waiting for transfers between devices, to_all(): return lax.all_to_all(spread, axes, 0, 0, tiled=True)  23.5 us
    all_gather x1, blocking collectives, body(): pair = lax.all_gather(pack, 'c', axis=0, tiled=False)  8.58 us
    all_to_all x1, waiting for transfers between devices, body(): part = lax.all_to_all(part, PLANE, 0, 0, tiled=True)  6.32 us
    all_to_all x1, starting transfers between devices, body(): part = lax.all_to_all(part, PLANE, 0, 0, tiled=True)  5.92 us
    ppermute x1, waiting for transfers between devices, body(): far = lax.ppermute(packs, 'shard', [(i, i ^ 2) for i in range(n_x)])  5.25 us
    pallas_call x1, Pallas kernels, head(): pl.pallas_call(head_kernel, grid=(steps,), in_specs=[pl.BlockSpec((rank_s...  5.21 us
    pallas_call x1, Pallas kernels, side(): pl.pallas_call(lambda *refs: side_kernel(replicas, rank_size, router_rows...  4.64 us
  transfers between devices with their start and end apart: 7, of which 5 were waited for; matrix products, arithmetic and copies ran while one was open for 3% of the time, Pallas kernels for 4%

profile of v4, /device:TPU:1, one launch (start us, length us, event | category | flops | bytes accessed | tf_op | source)
XLA Modules:
  0.0 106.1 jit_solution(17826653246846151581)
XLA Ops:
  0.7 5.2 %head.1 = f32[64,128]{1,0:T(8,128)} custom-call(f32[32,2560]{1,0:T(8,128)} %kb_ref.1, f32[32,2560]{1,0:T(8,128)} %rb_ref.1, bf16[1,128,2560]{2,1,0:T(8,128)(2,1)} %kg_ref.3, f32[1,128,2560]{2,1,0:T(8,128)} %ke_ref.3, bf16[1,16,2560]{2,1,0:T(8,128)(2,1)} %rg_ref.3, f32[1,16,2560]{2,1,0:T(8,128)} %re_ref.3, bf16[1,2,640]{2,1,0:T(2,128)(2,1)} %ng_ref.1), custom_call_target="tpu_custom_call" | custom-call | tf_op jit(solution)/shard_map/head/pallas_call | solution.py:58
  5.9 8.6 %all-gather = f32[128,128]{1,0:T(8,128)S(1)} all-gather(f32[64,128]{1,0:T(8,128)} %head.1), channel_id=2, replica_groups=mesh['z'=16,'y'=4,'c'=2,'shard'=4] {'c'}, dimensions={0}, use_global_device_ids=true | all-gather | bytes 98304 | tf_op jit(solution)/shard_map/all_gather | solution.py:272
  14.5 0.7 broadcast_in_dim.8
  15.1 9.5 %all-to-all-start = ((bf16[16,32,128]{2,1,0:T(8,128)(2,1)}), bf16[16,32,128]{2,1,0:T(8,128)(2,1)S(1)}, u32[]{:S(2)}, u32[]{:S(2)}) async-start(bf16[16,32,128]{2,1,0:T(8,128)(2,1)} %broadcast_in_dim.8), calls=%async_computation | async-start | bytes 262144 | tf_op jit(solution)/shard_map/all_to_all | solution.py:227
  24.8 1.2 %add_bitcast_fusion = f32[128,2560]{1,0:T(8,128)} fusion(f32[1,128,2560]{2,1,0:T(8,128)S(1)} %copy-done, bf16[1,128,2560]{2,1,0:T(8,128)(2,1)S(1)} %copy-done.2), kind=kLoop, calls=%fused_computation.4 | loop fusion | flops 655360 | bytes 3276800 | tf_op jit(solution)/shard_map/add | solution.py:267
  26.1 10.8 %all-to-all-done = bf16[16,32,128]{2,1,0:T(8,128)(2,1)S(1)} async-done(((bf16[16,32,128]{2,1,0:T(8,128)(2,1)}), bf16[16,32,128]{2,1,0:T(8,128)(2,1)S(1)}, u32[]{:S(2)}, u32[]{:S(2)}) %all-to-all-start) | async-done | bytes 131104 | tf_op jit(solution)/shard_map/all_to_all | solution.py:227
  36.9 0.7 broadcast_in_dim.9
  37.5 7.7 %all-to-all-start.1 = ((f32[8,32,128]{2,1,0:T(8,128)}), f32[8,32,128]{2,1,0:T(8,128)S(1)}, u32[]{:S(2)}, u32[]{:S(2)}) async-start(f32[8,32,128]{2,1,0:T(8,128)} %broadcast_in_dim.9), calls=%async_computation.1 | async-start | bytes 262144 | tf_op jit(solution)/shard_map/all_to_all | solution.py:227
  45.3 5.3 %all-to-all-done.1 = f32[8,32,128]{2,1,0:T(8,128)S(1)} async-done(((f32[8,32,128]{2,1,0:T(8,128)}), f32[8,32,128]{2,1,0:T(8,128)S(1)}, u32[]{:S(2)}, u32[]{:S(2)}) %all-to-all-start.1) | async-done | bytes 131104 | tf_op jit(solution)/shard_map/all_to_all | solution.py:227
  50.7 1.4 %convolution_convert_fusion = bf16[64,2560]{1,0:T(8,128)(2,1)} fusion(f32[16,2560]{1,0:T(8,128)S(1)} %add_bitcast_fusion.1, f32[128,2560]{1,0:T(8,128)S(1)} %copy-done.15, f32[32,16]{0,1:T(8,128)S(1)} %slice_bitcast_fusion, f32[32,128]{0,1:T(8,128)S(1)} %bitcast.40), kind=kOutput, calls=%fused_computation | convolution fusion | flops 142136320 | bytes 1820672 | tf_op jit(solution)/shard_map/dot_general | solution.py:285
  52.1 5.9 %all-to-all-start.2 = ((bf16[32,8,640]{2,1,0:T(8,128)(2,1)}), bf16[32,8,640]{2,1,0:T(8,128)(2,1)S(1)}, u32[]{:S(2)}, u32[]{:S(2)}) async-start(bf16[32,8,640]{2,1,0:T(8,128)(2,1)} %bitcast.9), calls=%async_computation.2 | async-start | bytes 655360 | tf_op jit(solution)/shard_map/all_to_all | solution.py:291
  58.1 3.3 %collective-permute-start = (f32[120,128]{1,0:T(8,128)S(1)}, f32[120,128]{1,0:T(8,128)S(1)}, u32[]{:S(2)}, u32[]{:S(2)}) collective-permute-start(f32[120,128]{1,0:T(8,128)S(1)} %select_maximum_fusion.2), channel_id=1, source_target_pairs={{0,1},{1,0},{2,3},{3,2},{4,5},{5,4},{6,7},{7,6},{8,9},{9,8},{10,11... | collective-permute-start | bytes 184328 | tf_op jit(solution)/shard_map/ppermute | solution.py:290
  61.4 6.3 %all-to-all-done.2 = bf16[32,8,640]{2,1,0:T(8,128)(2,1)S(1)} async-done(((bf16[32,8,640]{2,1,0:T(8,128)(2,1)}), bf16[32,8,640]{2,1,0:T(8,128)(2,1)S(1)}, u32[]{:S(2)}, u32[]{:S(2)}) %all-to-all-start.2) | async-done | bytes 327712 | tf_op jit(solution)/shard_map/all_to_all | solution.py:291
  67.8 0.7 broadcast_in_dim.10
  68.4 3.8 %all-to-all-start.3 = ((bf16[16,8,640]{2,1,0:T(8,128)(2,1)}), bf16[16,8,640]{2,1,0:T(8,128)(2,1)S(1)}, u32[]{:S(2)}, u32[]{:S(2)}) async-start(bf16[16,8,640]{2,1,0:T(8,128)(2,1)} %broadcast_in_dim.10), calls=%async_computation.3 | async-start | bytes 327680 | tf_op jit(solution)/shard_map/all_to_all | solution.py:227
  72.3 2.6 %collective-permute-start.1 = (f32[2,120,128]{2,1,0:T(8,128)S(1)}, f32[2,120,128]{2,1,0:T(8,128)S(1)}, u32[]{:S(2)}, u32[]{:S(2)}) collective-permute-start(f32[2,120,128]{2,1,0:T(8,128)S(1)} %pad_maximum_fusion.refs_0_), channel_id=1, source_target_pairs={{0,2},{1,3},{2,0},{3,1},{4,6},{5,7},{6,4},{7,5},{8,10},{9,11},{10,... | collective-permute-start | bytes 368648 | tf_op jit(solution)/shard_map/ppermute | solution.py:295
  75.0 5.2 %collective-permute-done.1.refs_1_ = f32[2,120,128]{2,1,0:T(8,128)S(1)} collective-permute-done((f32[2,120,128]{2,1,0:T(8,128)S(1)}, f32[2,120,128]{2,1,0:T(8,128)S(1)}, u32[]{:S(2)}, u32[]{:S(2)}) %collective-permute-start.1) | collective-permute-done | bytes 122912 | tf_op jit(solution)/shard_map/ppermute | solution.py:295
  80.2 4.6 %side.1 = (f32[128,32]{1,0:T(8,128)}, f32[32,512]{1,0:T(8,128)}, f32[64,32]{1,0:T(8,128)}, f32[20,512]{1,0:T(8,128)}, f32[64,128]{1,0:T(8,128)}, /*index=5*/f32[4,16,128]{2,1,0:T(8,128)}, f32[4,16,128]{2,1,0:T(8,128)}) custom-call(f32[2,120,128]{2,1,0:T(8,128)S(1)} %pad_maximum_fusion.refs_0_, f32[2,120,128]{2,1,0:T(8,128)S(1)} %collective-permute-done.1.refs_1_), custom_call_target="tpu_custom_call" | custom-call | flops 200000000 | bytes 8000000 | tf_op jit(solution)/shard_map/side/pallas_call | solution.py:122
  84.9 0.8 broadcast_in_dim.11
  85.7 7.8 %all-to-all-start.4 = ((bf16[32,8,640]{2,1,0:T(8,128)(2,1)}), bf16[32,8,640]{2,1,0:T(8,128)(2,1)S(1)}, u32[]{:S(2)}, u32[]{:S(2)}) async-start(bf16[32,8,640]{2,1,0:T(8,128)(2,1)} %broadcast_in_dim.11), calls=%async_computation.4 | async-start | bytes 655360 | tf_op jit(solution)/shard_map/all_to_all | solution.py:227
  93.5 0.8 subtract_convert_fusion
  94.3 0.6 convert_element_type.47
  95.6 7.5 %all-to-all-done.4 = bf16[32,8,640]{2,1,0:T(8,128)(2,1)S(1)} async-done(((bf16[32,8,640]{2,1,0:T(8,128)(2,1)}), bf16[32,8,640]{2,1,0:T(8,128)(2,1)S(1)}, u32[]{:S(2)}, u32[]{:S(2)}) %all-to-all-start.4) | async-done | bytes 327712 | tf_op jit(solution)/shard_map/all_to_all | solution.py:227
  103.1 3.0 %tail.1 = (f32[1,128,2560]{2,1,0:T(8,128)}, f32[1,16,2560]{2,1,0:T(8,128)}, f32[20,128]{1,0:T(8,128)}, f32[20,128]{1,0:T(8,128)}, bf16[20,512]{1,0:T(8,128)(2,1)...) custom-call(bf16[8,4,8,640]{3,2,1,0:T(8,128)(2,1)S(1)} %bitcast.33, ...), custom_call_target="tpu_custom_call" | custom-call | tf_op jit(solution)/shard_map/tail/pallas_call | solution.py:215
  (56 shorter events, 1.0 us)
Async XLA Ops:
  0.6 24.0 %copy-start = (f32[1,128,2560]{2,1,0:T(8,128)S(1)}, f32[1,128,2560]{2,1,0:T(8,128)}, u32[]{:S(2)}) copy-start(f32[1,128,2560]{2,1,0:T(8,128)} %ke_ref.3) | copy-start | bytes 3932164
  0.7 24.0 %copy-start.2 = (bf16[1,128,2560]{2,1,0:T(8,128)(2,1)S(1)}, bf16[1,128,2560]{2,1,0:T(8,128)(2,1)}, u32[]{:S(2)}) copy-start(bf16[1,128,2560]{2,1,0:T(8,128)(2,1)} %kg_ref.3) | copy-start | bytes 1966084
  15.1 21.7 %all-to-all-start = ((bf16[16,32,128]{2,1,0:T(8,128)(2,1)}), bf16[16,32,128]{2,1,0:T(8,128)(2,1)S(1)}, u32[]{:S(2)}, u32[]{:S(2)}) async-start(bf16[16,32,128]{2,1,0:T(8,128)(2,1)} %broadcast_in_dim.8), calls=%async_computation | async-start | bytes 262144 | tf_op jit(solution)/shard_map/all_to_all | solution.py:227
  24.7 1.3 %copy-start.16 = (f32[2,640]{1,0:T(2,128)S(1)}, f32[2,640]{1,0:T(2,128)}, u32[]{:S(2)}) copy-start(f32[2,640]{1,0:T(2,128)} %param.25) | copy-start | bytes 15364
  24.7 1.3 %copy-start.3 = (f32[1,16,2560]{2,1,0:T(8,128)S(1)}, f32[1,16,2560]{2,1,0:T(8,128)}, u32[]{:S(2)}) copy-start(f32[1,16,2560]{2,1,0:T(8,128)} %re_ref.3) | copy-start | bytes 491524
  24.8 1.3 %copy-start.5 = (bf16[1,16,2560]{2,1,0:T(8,128)(2,1)S(1)}, bf16[1,16,2560]{2,1,0:T(8,128)(2,1)}, u32[]{:S(2)}) copy-start(bf16[1,16,2560]{2,1,0:T(8,128)(2,1)} %rg_ref.3) | copy-start | bytes 245764
  24.8 20.5 %copy-start.8 = (f32[128,20]{0,1:T(8,128)S(1)}, f32[128,20]{0,1:T(8,128)}, u32[]{:S(2)}) copy-start(f32[128,20]{0,1:T(8,128)} %param.21) | copy-start | bytes 30724
  24.8 20.5 %copy-start.9 = (f32[128,20]{0,1:T(8,128)S(1)}, f32[128,20]{0,1:T(8,128)}, u32[]{:S(2)}) copy-start(f32[128,20]{0,1:T(8,128)} %param.20) | copy-start | bytes 30724
  26.0 24.7 %copy-start.15 = (f32[128,2560]{1,0:T(8,128)S(1)}, f32[128,2560]{1,0:T(8,128)}, u32[]{:S(2)}) copy-start(f32[128,2560]{1,0:T(8,128)} %add_bitcast_fusion) | copy-start | bytes 3932164
  37.5 13.0 %all-to-all-start.1 = ((f32[8,32,128]{2,1,0:T(8,128)}), f32[8,32,128]{2,1,0:T(8,128)S(1)}, u32[]{:S(2)}, u32[]{:S(2)}) async-start(f32[8,32,128]{2,1,0:T(8,128)} %broadcast_in_dim.9), calls=%async_computation.1 | async-start | bytes 262144 | tf_op jit(solution)/shard_map/all_to_all | solution.py:227
  50.5 7.5 %copy-start.13 = (f32[16,20]{1,0:T(8,128)S(1)}, f32[16,20]{1,0:T(8,128)}, u32[]{:S(2)}) copy-start(f32[16,20]{1,0:T(8,128)} %rw_ref.1) | copy-start | bytes 3844
  50.6 7.5 %copy-start.14 = (f32[16,20]{1,0:T(8,128)S(1)}, f32[16,20]{1,0:T(8,128)}, u32[]{:S(2)}) copy-start(f32[16,20]{1,0:T(8,128)} %rm_ref.1) | copy-start | bytes 3844
  52.1 15.6 %all-to-all-start.2 = ((bf16[32,8,640]{2,1,0:T(8,128)(2,1)}), bf16[32,8,640]{2,1,0:T(8,128)(2,1)S(1)}, u32[]{:S(2)}, u32[]{:S(2)}) async-start(bf16[32,8,640]{2,1,0:T(8,128)(2,1)} %bitcast.9), calls=%async_computation.2 | async-start | bytes 655360 | tf_op jit(solution)/shard_map/all_to_all | solution.py:291
  58.1 9.7 %collective-permute-start = (f32[120,128]{1,0:T(8,128)S(1)}, f32[120,128]{1,0:T(8,128)S(1)}, u32[]{:S(2)}, u32[]{:S(2)}) collective-permute-start(f32[120,128]{1,0:T(8,128)S(1)} %select_maximum_fusion.2), channel_id=1, source_target_pairs={{0,1},{1,0},{2,3},{3,2},{4,5},{5,4},{6,7},{7,6},{8,9},{9,8},{10,11... | collective-permute-start | bytes 184328 | tf_op jit(solution)/shard_map/ppermute | solution.py:290
  68.4 16.4 %all-to-all-start.3 = ((bf16[16,8,640]{2,1,0:T(8,128)(2,1)}), bf16[16,8,640]{2,1,0:T(8,128)(2,1)S(1)}, u32[]{:S(2)}, u32[]{:S(2)}) async-start(bf16[16,8,640]{2,1,0:T(8,128)(2,1)} %broadcast_in_dim.10), calls=%async_computation.3 | async-start | bytes 327680 | tf_op jit(solution)/shard_map/all_to_all | solution.py:227
  72.3 30.8 %copy-start.1 = (f32[1,128,2560]{2,1,0:T(8,128)S(1)}, f32[1,128,2560]{2,1,0:T(8,128)}, u32[]{:S(2)}) copy-start(f32[1,128,2560]{2,1,0:T(8,128)} %ke_ref.3) | copy-start | bytes 3932164
  72.3 30.8 %copy-start.4 = (f32[1,16,2560]{2,1,0:T(8,128)S(1)}, f32[1,16,2560]{2,1,0:T(8,128)}, u32[]{:S(2)}) copy-start(f32[1,16,2560]{2,1,0:T(8,128)} %re_ref.3) | copy-start | bytes 491524
  72.3 7.9 %collective-permute-start.1 = (f32[2,120,128]{2,1,0:T(8,128)S(1)}, f32[2,120,128]{2,1,0:T(8,128)S(1)}, u32[]{:S(2)}, u32[]{:S(2)}) collective-permute-start(f32[2,120,128]{2,1,0:T(8,128)S(1)} %pad_maximum_fusion.refs_0_), channel_id=1, source_target_pairs={{0,2},{1,3},{2,0},{3,1},{4,6},{5,7},{6,4},{7,5},{8,10},{9,11},{10,... | collective-permute-start | bytes 368648 | tf_op jit(solution)/shard_map/ppermute | solution.py:295
  84.9 18.2 %copy-start.6 = (f32[128,32]{1,0:T(8,128)S(1)}, f32[128,32]{1,0:T(8,128)}, u32[]{:S(2)}) copy-start(f32[128,32]{1,0:T(8,128)} %get-tuple-element.46.lk_ref) | copy-start | bytes 49156
  84.9 18.2 %copy-start.7 = (f32[32,512]{1,0:T(8,128)S(1)}, f32[32,512]{1,0:T(8,128)}, u32[]{:S(2)}) copy-start(f32[32,512]{1,0:T(8,128)} %get-tuple-element.47.lt_ref) | copy-start | bytes 196612
  84.9 18.2 %copy-start.10 = (f32[20,512]{1,0:T(8,128)S(1)}, f32[20,512]{1,0:T(8,128)}, u32[]{:S(2)}) copy-start(f32[20,512]{1,0:T(8,128)} %get-tuple-element.49.dk_ref) | copy-start | bytes 122884
  84.9 18.2 %copy-start.11 = (f32[64,32]{1,0:T(8,128)S(1)}, f32[64,32]{1,0:T(8,128)}, u32[]{:S(2)}) copy-start(f32[64,32]{1,0:T(8,128)} %get-tuple-element.48.lr_ref) | copy-start | bytes 24580
  84.9 18.2 %copy-start.12 = (f32[64,128]{1,0:T(8,128)S(1)}, f32[64,128]{1,0:T(8,128)}, u32[]{:S(2)}) copy-start(f32[64,128]{1,0:T(8,128)} %get-tuple-element.50.dr_ref) | copy-start | bytes 98308
  85.7 17.4 %all-to-all-start.4 = ((bf16[32,8,640]{2,1,0:T(8,128)(2,1)}), bf16[32,8,640]{2,1,0:T(8,128)(2,1)S(1)}, u32[]{:S(2)}, u32[]{:S(2)}) async-start(bf16[32,8,640]{2,1,0:T(8,128)(2,1)} %broadcast_in_dim.11), calls=%async_computation.4 | async-start | bytes 655360 | tf_op jit(solution)/shard_map/all_to_all | solution.py:227
  (1 other events, 1.3 us)

commit v5 on v4

--- a/solution.py
+++ b/solution.py
@@ -17,12 +17,25 @@
 PAIRS = ("y", "c")
 PLANE = ("y", "c", "shard")
 LANES = 128
+TAIL_PARTS = 2
 PACK_ROWS = 64
 KEY_AT, ROUTER_AT, NORM_AT = 64, 88, 104
 
 
 def dot(left, right, left_dim, right_dim):
     return lax.dot_general(left, right, (((left_dim,), (right_dim,)), ((), ())), precision=highest)
+
+
+def in_halves(left, right, left_dim, right_dim):
+    left_high, right_high = left.astype(bf16), right.astype(bf16)
+    left_low = (left - left_high.astype(f32)).astype(bf16)
+    right_low = (right - right_high.astype(f32)).astype(bf16)
+    total = 0.0
+    for one, other in ((left_low, right_high), (left_high, right_low), (left_high, right_high)):
+        total = total + lax.dot_general(
+            one, other, (((left_dim,), (right_dim,)), ((), ())), preferred_element_type=f32
+        )
+    return total
 
 
 def in_vmem(array):
@@ -46,14 +59,14 @@
 
     merged_key = kg_ref[0].astype(f32) + ke_ref[0]
     merged_router = rg_ref[0].astype(f32) + re_ref[0]
-    out_ref[:rank_size, :] += dot(kb_ref[...], merged_key, 1, 1)
-    out_ref[rank_size:router_end, :rank_size] += dot(merged_router, rb_ref[...], 1, 1)
+    out_ref[:rank_size, :] += in_halves(kb_ref[...], merged_key, 1, 1)
+    out_ref[rank_size:router_end, :rank_size] += in_halves(merged_router, rb_ref[...], 1, 1)
 
 
 def head(key_basis, router_basis, key_grad, key_error, router_grad, router_error, norm_grad):
     rank_size, width = key_basis.shape
     key_rows, router_rows = key_grad.shape[1], router_grad.shape[1]
-    steps = 5
+    steps = 2
     block = width // steps
     return pl.pallas_call(
         head_kernel,
@@ -73,6 +86,44 @@
     )(key_basis, router_basis, key_grad, key_error, router_grad, router_error, norm_grad)
 
 
+def mid_kernel(
+    own_ref, kg_ref, ke_ref, rg_ref, re_ref, km_ref, kw_ref, rm_ref, rw_ref, nm_ref, nw_ref, part_ref, sent_ref
+):
+    groups, lane_groups, lines, block = part_ref.shape
+    half, (router_rows, col_width) = groups // 2, rm_ref.shape
+    rank_size = half * lines
+    key_rows = own_ref[:rank_size, :]
+    rout_rows = own_ref[rank_size : rank_size + router_rows, :rank_size]
+    for group in range(lane_groups):
+        cols = slice(group * block, (group + 1) * block)
+        key_part = in_halves(key_rows, kg_ref[0, :, cols].astype(f32) + ke_ref[0, :, cols], 1, 0)
+        rout_part = in_halves(rout_rows, rg_ref[0, :, cols].astype(f32) + re_ref[0, :, cols], 0, 0)
+        for i in range(half):
+            part_ref[i, group] = key_part[i * lines : (i + 1) * lines].astype(bf16)
+            part_ref[half + i, group] = rout_part[i * lines : (i + 1) * lines].astype(bf16)
+    decay = learning_rate * momentum_decay
+    sent_ref[:KEY_AT, :] = own_ref[...]
+    sent_ref[KEY_AT:, :] = jnp.zeros((sent_ref.shape[0] - KEY_AT, LANES), f32)
+    sent_ref[KEY_AT : KEY_AT + col_width, :] = kw_ref[...] - decay * km_ref[...]
+    sent_ref[ROUTER_AT : ROUTER_AT + router_rows, :col_width] = rw_ref[...] - decay * rm_ref[...]
+    norm = nw_ref[...] - decay * nm_ref[...]
+    norm_vecs, norm_width = norm.shape
+    for vec in range(norm_vecs):
+        for first in range(0, norm_width, LANES):
+            row = NORM_AT + (vec * norm_width + first) // LANES
+            sent_ref[row : row + 1, :] = norm[vec : vec + 1, first : first + LANES]
+
+
+def mid(chunks, *operands):
+    return pl.pallas_call(
+        mid_kernel,
+        in_specs=[pl.BlockSpec(memory_space=pltpu.VMEM)] * len(operands),
+        out_specs=[pl.BlockSpec(chunks, lambda: (0,) * len(chunks)), pl.BlockSpec(memory_space=pltpu.VMEM)],
+        out_shape=[jax.ShapeDtypeStruct(chunks, bf16), pltpu.VMEM((NORM_AT + 16, LANES), f32)],
+        name="mid",
+    )(*[in_vmem(x) for x in operands])
+
+
 def square_of_root(gram, replicas):
     scaling = jnp.sqrt(jnp.sum(gram * gram, axis=(0, 1), keepdims=True)) + 1e-06
     rows = lax.broadcasted_iota(jnp.int32, gram.shape, 0)
@@ -87,8 +138,8 @@
 
 def side_kernel(replicas, rank_size, router_rows, col_width, *refs):
     packs = [ref.at[i] for ref in refs[:2] for i in range(2)]
-    outs = refs[2:]
-    lk_ref, lt_ref, lr_ref, dk_ref, dr_ref, ns_ref, dn_ref = outs
+    nm_ref, nw_ref, lk_ref, lt_ref, lr_ref, dk_ref, dr_ref, nv_ref, nn_ref, np_ref, wide_ref = refs[2:]
+    norm_vecs, norm_width = nm_ref.shape
     router_end = rank_size + router_rows
     shard = lax.axis_index("shard")
     key_rows = [pack[:rank_size, :] for pack in packs]
@@ -104,11 +155,22 @@
         lr_ref[lines, :] = dot(rout_rows[distance], square_router, 1, 0)
         dk_ref[:, lanes] = pack[KEY_AT : KEY_AT + col_width, :]
         dr_ref[lines, :] = pack[ROUTER_AT : ROUTER_AT + router_rows, :]
-        ns_ref[place] = pack[router_end : router_end + 16, :]
-        dn_ref[place] = pack[NORM_AT : NORM_AT + 16, :]
-
-
-def side(packs, replicas, rank_size, router_rows, col_width):
+        for vec in range(norm_vecs):
+            for first in range(0, norm_width, LANES):
+                line = (vec * norm_width + first) // LANES
+                mean = pack[router_end + line : router_end + line + 1, :] / replicas
+                master = pack[NORM_AT + line : NORM_AT + line + 1, :] - learning_rate * mean
+                lanes = pl.ds(pl.multiple_of(place * norm_width + first, LANES), LANES)
+                wide_ref[vec : vec + 1, lanes] = master
+                if distance == 0:
+                    here = slice(first, first + LANES)
+                    velocity = momentum_decay * nm_ref[vec : vec + 1, here] + mean
+                    nv_ref[vec : vec + 1, here] = velocity
+                    nn_ref[vec : vec + 1, here] = nw_ref[vec : vec + 1, here] - learning_rate * velocity
+    np_ref[...] = wide_ref[...].astype(bf16)
+
+
+def side(packs, norm_state, replicas, rank_size, router_rows, col_width):
     n_x = 2 * len(packs)
     shapes = [
         (LANES, rank_size),
@@ -116,17 +178,20 @@
         (n_x * router_rows, rank_size),
         (col_width, n_x * LANES),
         (n_x * router_rows, LANES),
-        (n_x, 16, LANES),
-        (n_x, 16, LANES),
     ]
+    norm_vecs, norm_width = norm_state[0].shape
+    norms = [((norm_vecs, norm_width), f32)] * 2 + [((norm_vecs, n_x * norm_width), bf16)]
     return pl.pallas_call(
         lambda *refs: side_kernel(replicas, rank_size, router_rows, col_width, *refs),
-        out_shape=[jax.ShapeDtypeStruct(shape, f32) for shape in shapes],
-        in_specs=[pl.BlockSpec(memory_space=pltpu.VMEM)] * len(packs),
-        out_specs=[pl.BlockSpec(memory_space=pltpu.VMEM)] * len(shapes),
+        out_shape=[pltpu.VMEM(shape, f32) for shape in shapes]
+        + [jax.ShapeDtypeStruct(shape, dtype) for shape, dtype in norms],
+        in_specs=[pl.BlockSpec(memory_space=pltpu.VMEM)] * (len(packs) + 2),
+        out_specs=[pl.BlockSpec(memory_space=pltpu.VMEM)] * len(shapes)
+        + [pl.BlockSpec(shape, lambda: (0, 0)) for shape, _ in norms],
+        scratch_shapes=[pltpu.VMEM(norms[2][0], f32)],
         cost_estimate=pl.CostEstimate(flops=200000000, bytes_accessed=8000000, transcendentals=0),
         name="side",
-    )(*[in_vmem(x) for x in packs])
+    )(*[in_vmem(x) for x in packs + norm_state])
 
 
 def tail_kernel(
@@ -153,11 +218,14 @@
         ]
         return terms[0] + terms[1]
 
-    key_sums = sums(0, step).astype(bf16)
-    router_sums = sums(half, step).astype(bf16)
-    cols = pl.ds(pl.multiple_of(step * block, LANES), block)
-    kc_ref[0] = kg_ref[0, :, cols].astype(f32) + ke_ref[0, :, cols] - apply(lk_ref[...], key_sums)
-    rc_ref[0] = rg_ref[0, :, cols].astype(f32) + re_ref[0, :, cols] - apply(lr_ref[own_lines, :], router_sums)
+    for part in range(TAIL_PARTS):
+        group = step * TAIL_PARTS + part
+        cols = pl.ds(pl.multiple_of(group * block, LANES), block)
+        here = slice(part * block, (part + 1) * block)
+        left = apply(lk_ref[...], sums(0, group).astype(bf16))
+        kc_ref[0, :, here] = kg_ref[0, :, cols].astype(f32) + ke_ref[0, :, cols] - left
+        left = apply(lr_ref[own_lines, :], sums(half, group).astype(bf16))
+        rc_ref[0, :, here] = rg_ref[0, :, cols].astype(f32) + re_ref[0, :, cols] - left
 
     @pl.when(step == 0)
     def _():
@@ -195,8 +263,8 @@
     key_rows, router_rows = key_grad.shape[1], router_grad.shape[1]
     dk, dr, km, rm = small[3], small[4], small[5], small[7]
     wide = [
-        pl.BlockSpec((1, key_rows, block), lambda i: (0, 0, i)),
-        pl.BlockSpec((1, router_rows, block), lambda i: (0, 0, i)),
+        pl.BlockSpec((1, key_rows, TAIL_PARTS * block), lambda i: (0, 0, i)),
+        pl.BlockSpec((1, router_rows, TAIL_PARTS * block), lambda i: (0, 0, i)),
     ]
 
     def whole(shape):
@@ -214,7 +282,7 @@
     ]
     return pl.pallas_call(
         tail_kernel,
-        grid=(lane_groups,),
+        grid=(lane_groups // TAIL_PARTS,),
         in_specs=[pl.BlockSpec(memory_space=pltpu.VMEM)] * (5 + len(small)),
         out_specs=wide + [whole(shape) for shape, _ in outs[2:]],
         out_shape=[jax.ShapeDtypeStruct(shape, dtype) for shape, dtype in outs],
@@ -250,22 +318,7 @@
     norm_vecs, norm_width = norm_grad.shape[1:]
     col_width = key_momentum.shape[1]
 
-    decayed_key = key_weight - (learning_rate * momentum_decay) * key_momentum
-    decayed_router = router_weight - (learning_rate * momentum_decay) * router_momentum
-    decayed_norm = norm_weight - (learning_rate * momentum_decay) * norm_momentum
     norm_lines = norm_vecs * norm_width // LANES
-    decayed = jnp.concatenate(
-        [
-            jnp.pad(decayed_key.T, ((0, ROUTER_AT - KEY_AT - col_width), (0, 0))),
-            jnp.pad(decayed_router, ((0, 0), (0, LANES - col_width))),
-            jnp.pad(decayed_norm.reshape(norm_lines, LANES), ((0, 16 - norm_lines), (0, 0))),
-        ],
-        axis=0,
-    )
-
-    merged = jnp.concatenate(
-        [key_grad[0].astype(f32) + key_error[0], router_grad[0].astype(f32) + router_error[0]]
-    )
     router_end = rank_size + router_rows
     used = router_end + norm_lines
     pack = head(key_basis, router_basis, key_grad, key_error, router_grad, router_error, norm_grad)
@@ -276,26 +329,35 @@
     spread = to_all(mine, PAIRS, n_y * n_c).reshape(n_y, n_c, half, LANES)
     own = jnp.sum(spread, axis=0).reshape(PACK_ROWS, LANES)
 
-    left = jnp.concatenate(
-        [
-            jnp.pad(own[:rank_size], ((0, 0), (0, router_rows))),
-            jnp.pad(own[rank_size:router_end, :rank_size].T, ((0, 0), (key_rows, 0))),
-        ]
-    )
-    part = lax.dot_general(left, merged, (((1,), (0,)), ((), ())), precision=lax.Precision.HIGH)
     groups, lane_groups = 2 * rank_size // 8, plane // (2 * rank_size // 8)
-    part = part.astype(bf16).reshape(groups, 8, lane_groups, width // lane_groups)
-    part = part.transpose(0, 2, 1, 3).reshape(plane, 8, width // lane_groups)
-    sent = jnp.concatenate([own, decayed])
+    part, sent = mid(
+        (groups, lane_groups, 8, width // lane_groups),
+        own,
+        key_grad,
+        key_error,
+        router_grad,
+        router_error,
+        key_momentum.T,
+        key_weight.T,
+        router_momentum,
+        router_weight,
+        norm_momentum,
+        norm_weight,
+    )
+    part = part.reshape(plane, 8, width // lane_groups)
     near = lax.ppermute(sent, "shard", [(i, i ^ 1) for i in range(n_x)])
     part = lax.all_to_all(part, PLANE, 0, 0, tiled=True)
     mine = jnp.sum(part.astype(f32), axis=0).astype(bf16)
     mine, near = lax.optimization_barrier((mine, near))
     packs = jnp.stack([sent, near])
     far = lax.ppermute(packs, "shard", [(i, i ^ 2) for i in range(n_x)])
-    *lefts, norm_sum, decayed_norm = side([packs, far], replicas, rank_size, router_rows, col_width)
+    *lefts, norm_velocity, norm_master, norm_params = side(
+        [packs, far], [norm_momentum, norm_weight], replicas, rank_size, router_rows, col_width
+    )
     mine = jnp.sum(to_all(mine, "z", n_z).astype(f32), axis=0).astype(bf16)
-    mine, lefts, norm_sum, decayed_norm = lax.optimization_barrier((mine, lefts, norm_sum, decayed_norm))
+    mine, lefts, norm_velocity, norm_master, norm_params = lax.optimization_barrier(
+        (mine, lefts, norm_velocity, norm_master, norm_params)
+    )
     sums = to_all(mine, PLANE, plane).reshape(groups, lane_groups, 8, width // lane_groups)
     (key_carry, router_carry, key_velocity, key_master, key_params, router_velocity, router_master, router_params) = (
         tail(
@@ -312,19 +374,6 @@
         )
     )
 
-    norm_mean = norm_sum[:, :norm_lines].reshape(n_x, norm_vecs, norm_width) / replicas
-    shard = lax.axis_index("shard")
-    def advance(momentum, weight, direction):
-        velocity = momentum_decay * momentum + direction
-        return velocity, weight - learning_rate * velocity
-
-    norm_velocity, norm_master = advance(
-        norm_momentum, norm_weight, lax.dynamic_index_in_dim(norm_mean, shard, 0, keepdims=False)
-    )
-
-    all_norm = decayed_norm[:, :norm_lines].reshape(n_x, norm_vecs, norm_width)
-    norm_params = (all_norm - learning_rate * norm_mean).astype(bf16)
-    norm_params = norm_params.transpose(1, 0, 2).reshape(norm_vecs, n_x * norm_width)
     return (
         key_carry,
         router_carry,

time: 107 us -> 101 us (0.944)
  blocking collectives: 8.58 us -> 60.3 us
  starting transfers between devices: 40.7 us -> 15.5 us
  waiting for transfers between devices: 35.1 us -> 11.8 us
  local copies, waits for them, and re-layouts: 3.61 us -> 0.78 us
  other arithmetic: 2.8 us -> 0.14 us
  Pallas kernels: 12.9 us -> 11.4 us
  matrix products: 1.42 us -> 0 us
    all_to_all x0 -> x3, blocking collectives: none -> 51.6 us  [to_all(): return lax.all_to_all(spread, axes, 0, 0, tiled=True)]
    all_to_all x4 -> x1, starting transfers between devices: 28.9 us -> 3.83 us  [to_all(): return lax.all_to_all(spread, axes, 0, 0, tiled=True)]
    all_to_all x4 -> x1, waiting for transfers between devices: 23.5 us -> 0.14 us  [to_all(): return lax.all_to_all(spread, axes, 0, 0, tiled=True)]
    broadcast_in_dim x4, local copies, waits for them, and re-layouts: 2.77 us -> 0.74 us  [to_all(): spread = jnp.broadcast_to(block[None], (size,) + block.shape)]
    pallas_call x1, Pallas kernels: 5.21 us -> 3.23 us  [head(): pl.pallas_call(head_kernel, grid=(steps,), in_specs=[pl.BlockSpec((rank_s...]
    dot_general x1 -> x0, matrix products: 1.42 us -> none  [body(): lax.dot_general(left, merged, (((1,), (0,)), ((), ())), precision=lax.Pre...]
    add x2 -> x0, other arithmetic: 1.23 us -> none  [the longest x1 1.21 us: body(): key_grad[0].astype(f32) + key_error[0]]
    pallas_call x1 -> x2, Pallas kernels: 3 us -> 3.64 us  [the longest x1 2.3 us: tail(): pl.pallas_call(tail_kernel, grid=(lane_groups // TAIL_PARTS,), in_specs=[...]
  transfers between devices with their start and end apart: 7 -> 4, of which waited for: 5 -> 3; matrix products, arithmetic and copies ran while one was open for 3% -> 0% of each run, Pallas kernels for 4% -> 5%
where the time goes in v5:
time: 101 us
  blocking collectives  60.3 us (60%)
  starting transfers between devices  15.5 us (15%)
  waiting for transfers between devices  11.8 us (12%)
  Pallas kernels  11.4 us (11%)
    all_to_all x3, blocking collectives, to_all(): return lax.all_to_all(spread, axes, 0, 0, tiled=True)  51.6 us
    all_gather x1, blocking collectives, body(): pair = lax.all_gather(pack, 'c', axis=0, tiled=False)  8.73 us
    all_to_all x1, waiting for transfers between devices, body(): part = lax.all_to_all(part, PLANE, 0, 0, tiled=True)  6.37 us
    all_to_all x1, starting transfers between devices, body(): part = lax.all_to_all(part, PLANE, 0, 0, tiled=True)  5.93 us
    ppermute x1, waiting for transfers between devices, body(): far = lax.ppermute(packs, 'shard', [(i, i ^ 2) for i in range(n_x)])  5.25 us
    pallas_call x1, Pallas kernels, side(): pl.pallas_call(lambda *refs: side_kernel(replicas, rank_size, router_rows...  4.56 us
    all_to_all x1, starting transfers between devices, to_all(): return lax.all_to_all(spread, axes, 0, 0, tiled=True)  3.83 us
    ppermute x1, starting transfers between devices, body(): near = lax.ppermute(sent, 'shard', [(i, i ^ 1) for i in range(n_x)])  3.29 us
  transfers between devices with their start and end apart: 4, of which 3 were waited for; matrix products, arithmetic and copies ran while one was open for 0% of the time, Pallas kernels for 5%

profile of v5, /device:TPU:1, one launch (start us, length us, event | category | flops | bytes accessed | tf_op | source)
XLA Modules:
  0.0 100.8 jit_solution(12317371234625538024)
XLA Ops:
  0.7 0.0 copy-start
  0.7 0.0 copy-start.4
  0.7 0.0 copy-start.5
  0.7 0.0 copy-start.6
  0.7 0.0 copy-start.7
  0.7 3.2 %head.1 = f32[64,128]{1,0:T(8,128)} custom-call(f32[32,2560]{1,0:T(8,128)} %kb_ref.1, f32[32,2560]{1,0:T(8,128)} %rb_ref.1, bf16[1,128,2560]{2,1,0:T(8,128)(2,1)} %kg_ref.5, f32[1,128,2560]{2,1,0:T(8,128)} %ke_ref.5, bf16[1,16,2560]{2,1,0:T(8,128)(2,1)} %rg_ref.5, f32[1,16,2560]{2,1,0:T(8,128)} %re_ref.5, bf16[1,2,640]{2,1,0:T(2,128)(2,1)} %ng_ref.1), custom_call_target="tpu_custom_call" | custom-call | tf_op jit(solution)/shard_map/head/pallas_call | solution.py:71
  4.0 0.0 copy-start.3
  4.0 8.7 %all-gather = f32[128,128]{1,0:T(8,128)S(1)} all-gather(f32[64,128]{1,0:T(8,128)} %head.1), channel_id=2, replica_groups=mesh['z'=16,'y'=4,'c'=2,'shard'=4] {'c'}, dimensions={0}, use_global_device_ids=true | all-gather | bytes 98304 | tf_op jit(solution)/shard_map/all_gather | solution.py:325
  12.7 21.5 %all_to_all.25 = bf16[16,32,128]{2,1,0:T(8,128)(2,1)S(1)} all-to-all(bf16[16,32,128]{2,1,0:T(8,128)(2,1)S(1)} %broadcast_in_dim.8), channel_id=1, replica_groups=mesh['z'=16,'y'=4,'c'=2,'shard'=4] {'z'}, dimensions={0} | all-to-all | bytes 262144 | tf_op jit(solution)/shard_map/all_to_all | solution.py:295
  34.3 12.8 %all_to_all.26 = f32[8,32,128]{2,1,0:T(8,128)S(1)} all-to-all(f32[8,32,128]{2,1,0:T(8,128)S(1)} %broadcast_in_dim.9), channel_id=1, replica_groups=mesh['z'=16,'y'=4,'c'=2,'shard'=4] {'y','c'}, dimensions={0} | all-to-all | bytes 262144 | tf_op jit(solution)/shard_map/all_to_all | solution.py:295
  47.2 1.3 %mid.1 = (bf16[8,4,8,640]{3,2,1,0:T(8,128)(2,1)}, f32[120,128]{1,0:T(8,128)S(1)}) custom-call(f32[64,128]{1,0:T(8,128)S(1)} %bitcast.14, bf16[1,128,2560]{2,1,0:T(8,128)(2,1)S(1)} %copy-done.1, f32[1,128,2560]{2,1,0:T(8,128)S(1)} %copy-done, bf16[1,16,2560]{2,1,0:T(8,128)(2,1)S(1)} %copy-done.3, f32[1,16,2560]{2,1,0:T(8,128)S(1)} %copy-done.2, ...), custom_call_target="tpu_custom_call" | custom-call | tf_op jit(solution)/shard_map/mid/pallas_call | solution.py:118
  48.5 5.9 %all-to-all-start.2 = ((bf16[32,8,640]{2,1,0:T(8,128)(2,1)}), bf16[32,8,640]{2,1,0:T(8,128)(2,1)S(1)}, u32[]{:S(2)}, u32[]{:S(2)}) async-start(bf16[32,8,640]{2,1,0:T(8,128)(2,1)} %bitcast.21), calls=%async_computation.2 | async-start | bytes 655360 | tf_op jit(solution)/shard_map/all_to_all | solution.py:349
  54.4 3.3 %collective-permute-start = (f32[120,128]{1,0:T(8,128)S(1)}, f32[120,128]{1,0:T(8,128)S(1)}, u32[]{:S(2)}, u32[]{:S(2)}) collective-permute-start(f32[120,128]{1,0:T(8,128)S(1)} %get-tuple-element.41), channel_id=1, source_target_pairs={{0,1},{1,0},{2,3},{3,2},{4,5},{5,4},{6,7},{7,6},{8,9},{9,8},{10,11... | collective-permute-start | bytes 184328 | tf_op jit(solution)/shard_map/ppermute | solution.py:348
  57.7 6.4 %all-to-all-done.2 = bf16[32,8,640]{2,1,0:T(8,128)(2,1)S(1)} async-done(((bf16[32,8,640]{2,1,0:T(8,128)(2,1)}), bf16[32,8,640]{2,1,0:T(8,128)(2,1)S(1)}, u32[]{:S(2)}, u32[]{:S(2)}) %all-to-all-start.2) | async-done | bytes 327712 | tf_op jit(solution)/shard_map/all_to_all | solution.py:349
  64.1 0.1 reduce_sum.54
  64.2 0.0 collective-permute-done
  64.2 0.7 broadcast_in_dim.10
  64.9 3.8 %all-to-all-start.3 = ((bf16[16,8,640]{2,1,0:T(8,128)(2,1)}), bf16[16,8,640]{2,1,0:T(8,128)(2,1)S(1)}, u32[]{:S(2)}, u32[]{:S(2)}) async-start(bf16[16,8,640]{2,1,0:T(8,128)(2,1)} %broadcast_in_dim.10), calls=%async_computation.3 | async-start | bytes 327680 | tf_op jit(solution)/shard_map/all_to_all | solution.py:295
  68.7 2.5 %collective-permute-start.1 = (f32[2,120,128]{2,1,0:T(8,128)S(1)}, f32[2,120,128]{2,1,0:T(8,128)S(1)}, u32[]{:S(2)}, u32[]{:S(2)}) collective-permute-start(f32[2,120,128]{2,1,0:T(8,128)S(1)} %pad_maximum_fusion.refs_0_), channel_id=1, source_target_pairs={{0,2},{1,3},{2,0},{3,1},{4,6},{5,7},{6,4},{7,5},{8,10},{9,11},{10,... | collective-permute-start | bytes 368648 | tf_op jit(solution)/shard_map/ppermute | solution.py:353
  71.2 5.2 %collective-permute-done.1.refs_1_ = f32[2,120,128]{2,1,0:T(8,128)S(1)} collective-permute-done((f32[2,120,128]{2,1,0:T(8,128)S(1)}, f32[2,120,128]{2,1,0:T(8,128)S(1)}, u32[]{:S(2)}, u32[]{:S(2)}) %collective-permute-start.1) | collective-permute-done | bytes 122912 | tf_op jit(solution)/shard_map/ppermute | solution.py:353
  76.4 4.6 %side.1 = (f32[128,32]{1,0:T(8,128)S(1)}, f32[32,512]{1,0:T(8,128)S(1)}, f32[64,32]{1,0:T(8,128)S(1)}, f32[20,512]{1,0:T(8,128)S(1)}, f32[64,128]{1,0:T(8,128)S(...) custom-call(f32[2,120,128]{2,1,0:T(8,128)S(1)} %pad_maximum_fusion.refs_0_, ...), custom_call_target="tpu_custom_call" | custom-call | flops 200000000 | bytes 8000000 | tf_op jit(solution)/shard_map/side/pallas_call | solution.py:184
  81.0 0.1 all-to-all-done.3
  81.2 17.3 %all_to_all.27 = bf16[32,8,640]{2,1,0:T(8,128)(2,1)S(1)} all-to-all(bf16[32,8,640]{2,1,0:T(8,128)(2,1)S(1)} %broadcast_in_dim.11), channel_id=1, replica_groups=mesh['z'=16,'y'=4,'c'=2,'shard'=4] {'y','c','shard'}, dimensions={0} | all-to-all | bytes 655360 | tf_op jit(solution)/shard_map/all_to_all | solution.py:295
  98.5 2.3 %tail.1 = (f32[1,128,2560]{2,1,0:T(8,128)}, f32[1,16,2560]{2,1,0:T(8,128)}, f32[20,128]{1,0:T(8,128)}, f32[20,128]{1,0:T(8,128)}, bf16[20,512]{1,0:T(8,128)(2,1)...) custom-call(bf16[8,4,8,640]{3,2,1,0:T(8,128)(2,1)S(1)} %bitcast.13, ...), custom_call_target="tpu_custom_call" | custom-call | tf_op jit(solution)/shard_map/tail/pallas_call | solution.py:283
  (22 shorter events, 0.2 us)
Async XLA Ops:
  0.7 46.4 %copy-start = (f32[1,128,2560]{2,1,0:T(8,128)S(1)}, f32[1,128,2560]{2,1,0:T(8,128)}, u32[]{:S(2)}) copy-start(f32[1,128,2560]{2,1,0:T(8,128)} %ke_ref.5) | copy-start | bytes 3932164
  0.7 46.4 %copy-start.4 = (f32[128,20]{0,1:T(8,128)S(1)}, f32[128,20]{0,1:T(8,128)}, u32[]{:S(2)}) copy-start(f32[128,20]{0,1:T(8,128)} %param.20) | copy-start | bytes 30724
  0.7 46.4 %copy-start.5 = (f32[128,20]{0,1:T(8,128)S(1)}, f32[128,20]{0,1:T(8,128)}, u32[]{:S(2)}) copy-start(f32[128,20]{0,1:T(8,128)} %param.21) | copy-start | bytes 30724
  0.7 46.4 %copy-start.6 = (f32[16,20]{1,0:T(8,128)S(1)}, f32[16,20]{1,0:T(8,128)}, u32[]{:S(2)}) copy-start(f32[16,20]{1,0:T(8,128)} %rm_ref.3) | copy-start | bytes 3844
  0.7 46.4 %copy-start.7 = (f32[16,20]{1,0:T(8,128)S(1)}, f32[16,20]{1,0:T(8,128)}, u32[]{:S(2)}) copy-start(f32[16,20]{1,0:T(8,128)} %rw_ref.3) | copy-start | bytes 3844
  0.7 46.4 %copy-start.8 = (f32[2,640]{1,0:T(2,128)S(1)}, f32[2,640]{1,0:T(2,128)}, u32[]{:S(2)}) copy-start(f32[2,640]{1,0:T(2,128)} %refs_2_.1) | copy-start | bytes 15364
  0.7 46.4 %copy-start.9 = (f32[2,640]{1,0:T(2,128)S(1)}, f32[2,640]{1,0:T(2,128)}, u32[]{:S(2)}) copy-start(f32[2,640]{1,0:T(2,128)} %refs_3_.1) | copy-start | bytes 15364
  4.0 43.2 %copy-start.1 = (bf16[1,128,2560]{2,1,0:T(8,128)(2,1)S(1)}, bf16[1,128,2560]{2,1,0:T(8,128)(2,1)}, u32[]{:S(2)}) copy-start(bf16[1,128,2560]{2,1,0:T(8,128)(2,1)} %kg_ref.5) | copy-start | bytes 1966084
  4.0 43.2 %copy-start.2 = (f32[1,16,2560]{2,1,0:T(8,128)S(1)}, f32[1,16,2560]{2,1,0:T(8,128)}, u32[]{:S(2)}) copy-start(f32[1,16,2560]{2,1,0:T(8,128)} %re_ref.5) | copy-start | bytes 491524
  4.0 43.2 %copy-start.3 = (bf16[1,16,2560]{2,1,0:T(8,128)(2,1)S(1)}, bf16[1,16,2560]{2,1,0:T(8,128)(2,1)}, u32[]{:S(2)}) copy-start(bf16[1,16,2560]{2,1,0:T(8,128)(2,1)} %rg_ref.5) | copy-start | bytes 245764
  48.5 15.6 %all-to-all-start.2 = ((bf16[32,8,640]{2,1,0:T(8,128)(2,1)}), bf16[32,8,640]{2,1,0:T(8,128)(2,1)S(1)}, u32[]{:S(2)}, u32[]{:S(2)}) async-start(bf16[32,8,640]{2,1,0:T(8,128)(2,1)} %bitcast.21), calls=%async_computation.2 | async-start | bytes 655360 | tf_op jit(solution)/shard_map/all_to_all | solution.py:349
  54.4 9.7 %collective-permute-start = (f32[120,128]{1,0:T(8,128)S(1)}, f32[120,128]{1,0:T(8,128)S(1)}, u32[]{:S(2)}, u32[]{:S(2)}) collective-permute-start(f32[120,128]{1,0:T(8,128)S(1)} %get-tuple-element.41), channel_id=1, source_target_pairs={{0,1},{1,0},{2,3},{3,2},{4,5},{5,4},{6,7},{7,6},{8,9},{9,8},{10,11... | collective-permute-start | bytes 184328 | tf_op jit(solution)/shard_map/ppermute | solution.py:348
  64.9 16.3 %all-to-all-start.3 = ((bf16[16,8,640]{2,1,0:T(8,128)(2,1)}), bf16[16,8,640]{2,1,0:T(8,128)(2,1)S(1)}, u32[]{:S(2)}, u32[]{:S(2)}) async-start(bf16[16,8,640]{2,1,0:T(8,128)(2,1)} %broadcast_in_dim.10), calls=%async_computation.3 | async-start | bytes 327680 | tf_op jit(solution)/shard_map/all_to_all | solution.py:295
  68.7 7.7 %collective-permute-start.1 = (f32[2,120,128]{2,1,0:T(8,128)S(1)}, f32[2,120,128]{2,1,0:T(8,128)S(1)}, u32[]{:S(2)}, u32[]{:S(2)}) collective-permute-start(f32[2,120,128]{2,1,0:T(8,128)S(1)} %pad_maximum_fusion.refs_0_), channel_id=1, source_target_pairs={{0,2},{1,3},{2,0},{3,1},{4,6},{5,7},{6,4},{7,5},{8,10},{9,11},{10,... | collective-permute-start | bytes 368648 | tf_op jit(solution)/shard_map/ppermute | solution.py:353

commit v6 on v5

--- a/solution.py
+++ b/solution.py
@@ -15,11 +15,12 @@
 
 DP = ("z", "y", "c")
 PAIRS = ("y", "c")
-PLANE = ("y", "c", "shard")
+CHIPS = ("y", "shard")
+PLANE = ("c",) + CHIPS
 LANES = 128
 TAIL_PARTS = 2
-PACK_ROWS = 64
-KEY_AT, ROUTER_AT, NORM_AT = 64, 88, 104
+PACK_ROWS = 48
+KEY_AT, ROUTER_AT, NORM_AT = 48, 72, 88
 
 
 def dot(left, right, left_dim, right_dim):
@@ -50,12 +51,16 @@
     @pl.when(pl.program_id(0) == 0)
     def _():
         out_ref[...] = jnp.zeros_like(out_ref)
-        norm = ng_ref[0].astype(f32)
-        lines = norm_width // LANES
-        for vec in range(norm_vecs):
-            for line in range(lines):
-                row = router_end + vec * lines + line
-                out_ref[row : row + 1, :] = norm[vec : vec + 1, line * LANES : (line + 1) * LANES]
+        norm = jnp.concatenate([ng_ref[0].astype(f32), jnp.zeros((8 - norm_vecs, norm_width), f32)], axis=0)
+        pieces = router_rows // norm_vecs
+        piece = norm_width // pieces
+        lane = lax.broadcasted_iota(jnp.int32, (8, LANES), 1)
+        for index in range(pieces):
+            line = pltpu.roll(norm, (rank_size - index * piece) % norm_width, 1)[:, :LANES]
+            line = jnp.where((lane >= rank_size) & (lane < rank_size + piece), line, 0.0)
+            for vec in range(norm_vecs):
+                row = rank_size + vec * pieces + index
+                out_ref[row : row + 1, :] = line[vec : vec + 1]
 
     merged_key = kg_ref[0].astype(f32) + ke_ref[0]
     merged_router = rg_ref[0].astype(f32) + re_ref[0]
@@ -80,8 +85,8 @@
             pl.BlockSpec((1, router_rows, block), lambda i: (0, 0, i)),
             pl.BlockSpec(norm_grad.shape, lambda i: (0, 0, 0)),
         ],
-        out_specs=pl.BlockSpec((PACK_ROWS, LANES), lambda i: (0, 0)),
-        out_shape=jax.ShapeDtypeStruct((PACK_ROWS, LANES), f32),
+        out_specs=pl.BlockSpec(memory_space=pltpu.VMEM),
+        out_shape=pltpu.VMEM((PACK_ROWS, LANES), f32),
         name="head",
     )(key_basis, router_basis, key_grad, key_error, router_grad, router_error, norm_grad)
 
@@ -136,6 +141,21 @@
     return dot(root_side, root_side, 0, 0) / (scaling * replicas)
 
 
+def norm_rows(lines, start, norm_vecs, norm_width):
+    pieces = lines.shape[0] // norm_vecs
+    piece = norm_width // pieces
+    lane = lax.broadcasted_iota(jnp.int32, lines.shape, 1)
+    lines = jnp.where((lane >= start) & (lane < start + piece), lines, 0.0)
+    lines = jnp.concatenate([lines, jnp.zeros((lines.shape[0], norm_width - LANES), f32)], axis=1)
+    totals = [0.0] * norm_vecs
+    for index in range(pieces):
+        moved = pltpu.roll(lines, (index * piece - start) % norm_width, 1)
+        for vec in range(norm_vecs):
+            row = vec * pieces + index
+            totals[vec] = totals[vec] + moved[row : row + 1]
+    return totals
+
+
 def side_kernel(replicas, rank_size, router_rows, col_width, *refs):
     packs = [ref.at[i] for ref in refs[:2] for i in range(2)]
     nm_ref, nw_ref, lk_ref, lt_ref, lr_ref, dk_ref, dr_ref, nv_ref, nn_ref, np_ref, wide_ref = refs[2:]
@@ -155,18 +175,18 @@
         lr_ref[lines, :] = dot(rout_rows[distance], square_router, 1, 0)
         dk_ref[:, lanes] = pack[KEY_AT : KEY_AT + col_width, :]
         dr_ref[lines, :] = pack[ROUTER_AT : ROUTER_AT + router_rows, :]
-        for vec in range(norm_vecs):
+        means = norm_rows(pack[rank_size:router_end, :], rank_size, norm_vecs, norm_width)
+        for vec, mean in enumerate(means):
+            mean = mean / replicas
             for first in range(0, norm_width, LANES):
-                line = (vec * norm_width + first) // LANES
-                mean = pack[router_end + line : router_end + line + 1, :] / replicas
-                master = pack[NORM_AT + line : NORM_AT + line + 1, :] - learning_rate * mean
+                here = slice(first, first + LANES)
+                row = NORM_AT + (vec * norm_width + first) // LANES
                 lanes = pl.ds(pl.multiple_of(place * norm_width + first, LANES), LANES)
-                wide_ref[vec : vec + 1, lanes] = master
-                if distance == 0:
-                    here = slice(first, first + LANES)
-                    velocity = momentum_decay * nm_ref[vec : vec + 1, here] + mean
-                    nv_ref[vec : vec + 1, here] = velocity
-                    nn_ref[vec : vec + 1, here] = nw_ref[vec : vec + 1, here] - learning_rate * velocity
+                wide_ref[vec : vec + 1, lanes] = pack[row : row + 1, :] - learning_rate * mean[:, here]
+            if distance == 0:
+                velocity = momentum_decay * nm_ref[vec : vec + 1, :] + mean
+                nv_ref[vec : vec + 1, :] = velocity
+                nn_ref[vec : vec + 1, :] = nw_ref[vec : vec + 1, :] - learning_rate * velocity
     np_ref[...] = wide_ref[...].astype(bf16)
 
 
@@ -318,9 +338,7 @@
     norm_vecs, norm_width = norm_grad.shape[1:]
     col_width = key_momentum.shape[1]
 
-    norm_lines = norm_vecs * norm_width // LANES
     router_end = rank_size + router_rows
-    used = router_end + norm_lines
     pack = head(key_basis, router_basis, key_grad, key_error, router_grad, router_error, norm_grad)
     pair = lax.all_gather(pack, "c", axis=0, tiled=False)
     half = PACK_ROWS // n_c
@@ -358,7 +376,8 @@
     mine, lefts, norm_velocity, norm_master, norm_params = lax.optimization_barrier(
         (mine, lefts, norm_velocity, norm_master, norm_params)
     )
-    sums = to_all(mine, PLANE, plane).reshape(groups, lane_groups, 8, width // lane_groups)
+    sums = lax.all_gather(to_all(mine, CHIPS, n_y * n_x), "c", axis=0, tiled=False)
+    sums = sums.reshape(groups, lane_groups, 8, width // lane_groups)
     (key_carry, router_carry, key_velocity, key_master, key_params, router_velocity, router_master, router_params) = (
         tail(
             sums,

time: 101 us -> 98.9 us (0.979)
  waiting for transfers between devices: 11.8 us -> 9.27 us
  starting transfers between devices: 15.5 us -> 16.6 us
    all_to_all x3, blocking collectives: 51.6 us -> 44.6 us  [to_all(): return lax.all_to_all(spread, axes, 0, 0, tiled=True)]
    all_gather x0 -> x1, blocking collectives: none -> 6.87 us  [body(): lax.all_gather(to_all(mine, CHIPS, n_y * n_x), 'c', axis=0, tiled=False)]
    ppermute x1, waiting for transfers between devices: 5.25 us -> 3.06 us  [body(): far = lax.ppermute(packs, 'shard', [(i, i ^ 2) for i in range(n_x)])]
    ppermute x1, starting transfers between devices: 2.48 us -> 3.89 us  [body(): far = lax.ppermute(packs, 'shard', [(i, i ^ 2) for i in range(n_x)])]
where the time goes in v6:
time: 98.9 us; the launch traced here: 98.4 us
  blocking collectives  59.9 us (61%)
  starting transfers between devices  16.6 us (17%)
  Pallas kernels  10.9 us (11%)
  waiting for transfers between devices  9.27 us (9%)
    all_to_all x3, blocking collectives, to_all(): return lax.all_to_all(spread, axes, 0, 0, tiled=True)  44.6 us
    all_gather x1, blocking collectives, body(): pair = lax.all_gather(pack, 'c', axis=0, tiled=False)  8.37 us
    all_gather x1, blocking collectives, body(): lax.all_gather(to_all(mine, CHIPS, n_y * n_x), 'c', axis=0, tiled=False)  6.87 us
    all_to_all x1, starting transfers between devices, body(): part = lax.all_to_all(part, PLANE, 0, 0, tiled=True)  5.88 us
    all_to_all x1, waiting for transfers between devices, body(): part = lax.all_to_all(part, PLANE, 0, 0, tiled=True)  5.64 us
    pallas_call x1, Pallas kernels, side(): pl.pallas_call(lambda *refs: side_kernel(replicas, rank_size, router_rows...  4.54 us
    ppermute x1, starting transfers between devices, body(): far = lax.ppermute(packs, 'shard', [(i, i ^ 2) for i in range(n_x)])  3.89 us
    all_to_all x1, starting transfers between devices, to_all(): return lax.all_to_all(spread, axes, 0, 0, tiled=True)  3.52 us
  transfers between devices with their start and end apart: 4, of which 3 were waited for; matrix products, arithmetic and copies ran while one was open for 0% of the time, Pallas kernels for 5%

profile of v6, /device:TPU:1, one launch (start us, length us, event | category | flops | bytes accessed | tf_op | source)
XLA Modules:
  0.0 98.4 jit_solution(1584532622356171968)
XLA Ops:
  0.7 0.0 copy-start
  0.7 0.0 copy-start.1
  0.7 0.0 copy-start.2
  0.7 0.0 copy-start.3
  0.7 0.0 copy-start.4
  0.8 2.8 %head.1 = f32[48,128]{1,0:T(8,128)S(1)} custom-call(f32[32,2560]{1,0:T(8,128)} %kb_ref.1, f32[32,2560]{1,0:T(8,128)} %rb_ref.1, bf16[1,128,2560]{2,1,0:T(8,128)(2,1)} %kg_ref.5, f32[1,128,2560]{2,1,0:T(8,128)} %ke_ref.5, bf16[1,16,2560]{2,1,0:T(8,128)(2,1)} %rg_ref.5, f32[1,16,2560]{2,1,0:T(8,128)} %re_ref.5, bf16[1,2,640]{2,1,0:T(2,128)(2,1)} %ng_ref.1), custom_call_target="tpu_custom_call" | custom-call | tf_op jit(solution)/shard_map/head/pallas_call | solution.py:76
  3.5 8.4 %all-gather = f32[96,128]{1,0:T(8,128)S(1)} all-gather(f32[48,128]{1,0:T(8,128)S(1)} %head.1), channel_id=2, replica_groups=mesh['z'=16,'y'=4,'c'=2,'shard'=4] {'c'}, dimensions={0}, use_global_device_ids=true | all-gather | bytes 73728 | tf_op jit(solution)/shard_map/all_gather | solution.py:343
  11.9 21.2 %all_to_all.25 = bf16[16,24,128]{2,1,0:T(8,128)(2,1)S(1)} all-to-all(bf16[16,24,128]{2,1,0:T(8,128)(2,1)S(1)} %broadcast_in_dim.8), channel_id=1, replica_groups=mesh['z'=16,'y'=4,'c'=2,'shard'=4] {'z'}, dimensions={0} | all-to-all | bytes 196608 | tf_op jit(solution)/shard_map/all_to_all | solution.py:315
  33.2 11.9 %all_to_all.26 = f32[8,24,128]{2,1,0:T(8,128)S(1)} all-to-all(f32[8,24,128]{2,1,0:T(8,128)S(1)} %broadcast_in_dim.9), channel_id=1, replica_groups=mesh['z'=16,'y'=4,'c'=2,'shard'=4] {'y','c'}, dimensions={0} | all-to-all | bytes 196608 | tf_op jit(solution)/shard_map/all_to_all | solution.py:315
  45.2 1.3 %mid.1 = (bf16[8,4,8,640]{3,2,1,0:T(8,128)(2,1)}, f32[104,128]{1,0:T(8,128)S(1)}) custom-call(f32[48,128]{1,0:T(8,128)S(1)} %bitcast.14, bf16[1,128,2560]{2,1,0:T(8,128)(2,1)S(1)} %copy-done.1, f32[1,128,2560]{2,1,0:T(8,128)S(1)} %copy-done, bf16[1,16,2560]{2,1,0:T(8,128)(2,1)S(1)} %copy-done.3, f32[1,16,2560]{2,1,0:T(8,128)S(1)} %copy-done.2, ...), custom_call_target="tpu_custom_call" | custom-call | tf_op jit(solution)/shard_map/mid/pallas_call | solution.py:123
  46.5 5.9 %all-to-all-start.2 = ((bf16[32,8,640]{2,1,0:T(8,128)(2,1)}), bf16[32,8,640]{2,1,0:T(8,128)(2,1)S(1)}, u32[]{:S(2)}, u32[]{:S(2)}) async-start(bf16[32,8,640]{2,1,0:T(8,128)(2,1)} %bitcast.21), calls=%async_computation.2 | async-start | bytes 655360 | tf_op jit(solution)/shard_map/all_to_all | solution.py:367
  52.4 3.3 %collective-permute-start = (f32[104,128]{1,0:T(8,128)S(1)}, f32[104,128]{1,0:T(8,128)S(1)}, u32[]{:S(2)}, u32[]{:S(2)}) collective-permute-start(f32[104,128]{1,0:T(8,128)S(1)} %get-tuple-element.41), channel_id=1, source_target_pairs={{0,1},{1,0},{2,3},{3,2},{4,5},{5,4},{6,7},{7,6},{8,9},{9,8},{10,11... | collective-permute-start | bytes 159752 | tf_op jit(solution)/shard_map/ppermute | solution.py:366
  55.7 5.6 %all-to-all-done.2 = bf16[32,8,640]{2,1,0:T(8,128)(2,1)S(1)} async-done(((bf16[32,8,640]{2,1,0:T(8,128)(2,1)}), bf16[32,8,640]{2,1,0:T(8,128)(2,1)S(1)}, u32[]{:S(2)}, u32[]{:S(2)}) %all-to-all-start.2) | async-done | bytes 327712 | tf_op jit(solution)/shard_map/all_to_all | solution.py:367
  61.4 0.1 reduce_sum.54
  61.4 0.0 collective-permute-done
  61.4 0.7 broadcast_in_dim.10
  62.1 3.5 %all-to-all-start.3 = ((bf16[16,8,640]{2,1,0:T(8,128)(2,1)}), bf16[16,8,640]{2,1,0:T(8,128)(2,1)S(1)}, u32[]{:S(2)}, u32[]{:S(2)}) async-start(bf16[16,8,640]{2,1,0:T(8,128)(2,1)} %broadcast_in_dim.10), calls=%async_computation.3 | async-start | bytes 327680 | tf_op jit(solution)/shard_map/all_to_all | solution.py:315
  65.7 3.9 %collective-permute-start.1 = (f32[2,104,128]{2,1,0:T(8,128)S(1)}, f32[2,104,128]{2,1,0:T(8,128)S(1)}, u32[]{:S(2)}, u32[]{:S(2)}) collective-permute-start(f32[2,104,128]{2,1,0:T(8,128)S(1)} %pad_maximum_fusion.refs_0_), channel_id=1, source_target_pairs={{0,2},{1,3},{2,0},{3,1},{4,6},{5,7},{6,4},{7,5},{8,10},{9,11},{10,... | collective-permute-start | bytes 319496 | tf_op jit(solution)/shard_map/ppermute | solution.py:371
  69.6 3.1 %collective-permute-done.1.refs_1_ = f32[2,104,128]{2,1,0:T(8,128)S(1)} collective-permute-done((f32[2,104,128]{2,1,0:T(8,128)S(1)}, f32[2,104,128]{2,1,0:T(8,128)S(1)}, u32[]{:S(2)}, u32[]{:S(2)}) %collective-permute-start.1) | collective-permute-done | bytes 106528 | tf_op jit(solution)/shard_map/ppermute | solution.py:371
  72.6 4.5 %side.1 = (f32[128,32]{1,0:T(8,128)S(1)}, f32[32,512]{1,0:T(8,128)S(1)}, f32[64,32]{1,0:T(8,128)S(1)}, f32[20,512]{1,0:T(8,128)S(1)}, f32[64,128]{1,0:T(8,128)S(...) custom-call(f32[2,104,128]{2,1,0:T(8,128)S(1)} %pad_maximum_fusion.refs_0_, ...), custom_call_target="tpu_custom_call" | custom-call | flops 200000000 | bytes 8000000 | tf_op jit(solution)/shard_map/side/pallas_call | solution.py:204
  77.2 0.6 all-to-all-done.3
  77.8 11.5 %all_to_all.27 = bf16[16,8,640]{2,1,0:T(8,128)(2,1)S(1)} all-to-all(bf16[16,8,640]{2,1,0:T(8,128)(2,1)S(1)} %broadcast_in_dim.11), channel_id=1, replica_groups=mesh['z'=16,'y'=4,'c'=2,'shard'=4] {'y','shard'}, dimensions={0} | all-to-all | bytes 327680 | tf_op jit(solution)/shard_map/all_to_all | solution.py:315
  89.3 6.9 %all-gather.1 = bf16[32,8,640]{2,1,0:T(8,128)(2,1)S(1)} all-gather(bf16[16,8,640]{2,1,0:T(8,128)(2,1)S(1)} %all_to_all.27), channel_id=3, replica_groups=mesh['z'=16,'y'=4,'c'=2,'shard'=4] {'c'}, dimensions={0}, use_global_device_ids=true | all-gather | bytes 491520 | tf_op jit(solution)/shard_map/all_gather | solution.py:379
  96.1 2.3 %tail.1 = (f32[1,128,2560]{2,1,0:T(8,128)}, f32[1,16,2560]{2,1,0:T(8,128)}, f32[20,128]{1,0:T(8,128)}, f32[20,128]{1,0:T(8,128)}, bf16[20,512]{1,0:T(8,128)(2,1)...) custom-call(bf16[8,4,8,640]{3,2,1,0:T(8,128)(2,1)S(1)} %bitcast.13, ...), custom_call_target="tpu_custom_call" | custom-call | tf_op jit(solution)/shard_map/tail/pallas_call | solution.py:303
  (23 shorter events, 0.1 us)
Async XLA Ops:
  0.7 44.5 %copy-start = (f32[1,128,2560]{2,1,0:T(8,128)S(1)}, f32[1,128,2560]{2,1,0:T(8,128)}, u32[]{:S(2)}) copy-start(f32[1,128,2560]{2,1,0:T(8,128)} %ke_ref.5) | copy-start | bytes 3932164
  0.7 44.5 %copy-start.1 = (bf16[1,128,2560]{2,1,0:T(8,128)(2,1)S(1)}, bf16[1,128,2560]{2,1,0:T(8,128)(2,1)}, u32[]{:S(2)}) copy-start(bf16[1,128,2560]{2,1,0:T(8,128)(2,1)} %kg_ref.5) | copy-start | bytes 1966084
  0.7 44.5 %copy-start.2 = (f32[1,16,2560]{2,1,0:T(8,128)S(1)}, f32[1,16,2560]{2,1,0:T(8,128)}, u32[]{:S(2)}) copy-start(f32[1,16,2560]{2,1,0:T(8,128)} %re_ref.5) | copy-start | bytes 491524
  0.7 44.5 %copy-start.3 = (bf16[1,16,2560]{2,1,0:T(8,128)(2,1)S(1)}, bf16[1,16,2560]{2,1,0:T(8,128)(2,1)}, u32[]{:S(2)}) copy-start(bf16[1,16,2560]{2,1,0:T(8,128)(2,1)} %rg_ref.5) | copy-start | bytes 245764
  0.7 44.5 %copy-start.4 = (f32[128,20]{0,1:T(8,128)S(1)}, f32[128,20]{0,1:T(8,128)}, u32[]{:S(2)}) copy-start(f32[128,20]{0,1:T(8,128)} %param.20) | copy-start | bytes 30724
  0.7 44.5 %copy-start.5 = (f32[128,20]{0,1:T(8,128)S(1)}, f32[128,20]{0,1:T(8,128)}, u32[]{:S(2)}) copy-start(f32[128,20]{0,1:T(8,128)} %param.21) | copy-start | bytes 30724
  0.7 44.5 %copy-start.6 = (f32[16,20]{1,0:T(8,128)S(1)}, f32[16,20]{1,0:T(8,128)}, u32[]{:S(2)}) copy-start(f32[16,20]{1,0:T(8,128)} %rm_ref.3) | copy-start | bytes 3844
  0.7 44.5 %copy-start.7 = (f32[16,20]{1,0:T(8,128)S(1)}, f32[16,20]{1,0:T(8,128)}, u32[]{:S(2)}) copy-start(f32[16,20]{1,0:T(8,128)} %rw_ref.3) | copy-start | bytes 3844
  0.7 44.5 %copy-start.8 = (f32[2,640]{1,0:T(2,128)S(1)}, f32[2,640]{1,0:T(2,128)}, u32[]{:S(2)}) copy-start(f32[2,640]{1,0:T(2,128)} %refs_2_.1) | copy-start | bytes 15364
  0.7 44.5 %copy-start.9 = (f32[2,640]{1,0:T(2,128)S(1)}, f32[2,640]{1,0:T(2,128)}, u32[]{:S(2)}) copy-start(f32[2,640]{1,0:T(2,128)} %refs_3_.1) | copy-start | bytes 15364
  46.5 14.8 %all-to-all-start.2 = ((bf16[32,8,640]{2,1,0:T(8,128)(2,1)}), bf16[32,8,640]{2,1,0:T(8,128)(2,1)S(1)}, u32[]{:S(2)}, u32[]{:S(2)}) async-start(bf16[32,8,640]{2,1,0:T(8,128)(2,1)} %bitcast.21), calls=%async_computation.2 | async-start | bytes 655360 | tf_op jit(solution)/shard_map/all_to_all | solution.py:367
  52.4 9.0 %collective-permute-start = (f32[104,128]{1,0:T(8,128)S(1)}, f32[104,128]{1,0:T(8,128)S(1)}, u32[]{:S(2)}, u32[]{:S(2)}) collective-permute-start(f32[104,128]{1,0:T(8,128)S(1)} %get-tuple-element.41), channel_id=1, source_target_pairs={{0,1},{1,0},{2,3},{3,2},{4,5},{5,4},{6,7},{7,6},{8,9},{9,8},{10,11... | collective-permute-start | bytes 159752 | tf_op jit(solution)/shard_map/ppermute | solution.py:366
  62.1 15.6 %all-to-all-start.3 = ((bf16[16,8,640]{2,1,0:T(8,128)(2,1)}), bf16[16,8,640]{2,1,0:T(8,128)(2,1)S(1)}, u32[]{:S(2)}, u32[]{:S(2)}) async-start(bf16[16,8,640]{2,1,0:T(8,128)(2,1)} %broadcast_in_dim.10), calls=%async_computation.3 | async-start | bytes 327680 | tf_op jit(solution)/shard_map/all_to_all | solution.py:315
  65.7 7.0 %collective-permute-start.1 = (f32[2,104,128]{2,1,0:T(8,128)S(1)}, f32[2,104,128]{2,1,0:T(8,128)S(1)}, u32[]{:S(2)}, u32[]{:S(2)}) collective-permute-start(f32[2,104,128]{2,1,0:T(8,128)S(1)} %pad_maximum_fusion.refs_0_), channel_id=1, source_target_pairs={{0,2},{1,3},{2,0},{3,1},{4,6},{5,7},{6,4},{7,5},{8,10},{9,11},{10,... | collective-permute-start | bytes 319496 | tf_op jit(solution)/shard_map/ppermute | solution.py:371

commit v7 on v6

--- a/solution.py
+++ b/solution.py
@@ -123,8 +123,8 @@
     return pl.pallas_call(
         mid_kernel,
         in_specs=[pl.BlockSpec(memory_space=pltpu.VMEM)] * len(operands),
-        out_specs=[pl.BlockSpec(chunks, lambda: (0,) * len(chunks)), pl.BlockSpec(memory_space=pltpu.VMEM)],
-        out_shape=[jax.ShapeDtypeStruct(chunks, bf16), pltpu.VMEM((NORM_AT + 16, LANES), f32)],
+        out_specs=[pl.BlockSpec(memory_space=pltpu.VMEM)] * 2,
+        out_shape=[pltpu.VMEM(chunks, bf16), pltpu.VMEM((NORM_AT + 16, LANES), f32)],
         name="mid",
     )(*[in_vmem(x) for x in operands])
 
@@ -135,9 +135,14 @@
     identity = (rows == lax.broadcasted_iota(jnp.int32, gram.shape, 1)).astype(f32)
     square_side, root_side = gram / scaling, identity
     for sweep_index in range(ROOT_STEPS):
-        middle = 1.5 * identity - 0.5 * dot(root_side, square_side, 1, 0)
-        square_side = dot(square_side, middle, 1, 0)
-        root_side = dot(middle, root_side, 1, 0)
+        if sweep_index == 0:
+            middle = 1.5 * identity - 0.5 * square_side
+            root_side = middle
+        else:
+            middle = 1.5 * identity - 0.5 * dot(root_side, square_side, 1, 0)
+            root_side = dot(middle, root_side, 1, 0)
+        if sweep_index < ROOT_STEPS - 1:
+            square_side = dot(square_side, middle, 1, 0)
     return dot(root_side, root_side, 0, 0) / (scaling * replicas)
 
 
@@ -214,6 +219,22 @@
     )(*[in_vmem(x) for x in packs + norm_state])
 
 
+def spread_kernel(part_ref, out_ref):
+    total = jnp.sum(part_ref[...].astype(f32), axis=0).astype(bf16)
+    for place in range(out_ref.shape[0]):
+        out_ref[place] = total
+
+
+def spread_sum(part, size):
+    return pl.pallas_call(
+        spread_kernel,
+        in_specs=[pl.BlockSpec(memory_space=pltpu.VMEM)],
+        out_specs=pl.BlockSpec(memory_space=pltpu.VMEM),
+        out_shape=pltpu.VMEM((size,) + part.shape[1:], bf16),
+        name="spread",
+    )(in_vmem(part))
+
+
 def tail_kernel(
     t_ref, kg_ref, ke_ref, rg_ref, re_ref, lk_ref, lt_ref, lr_ref, dk_ref, dr_ref, km_ref, kw_ref, rm_ref, rw_ref,
     kc_ref, rc_ref, kv_ref, kn_ref, kp_ref, rv_ref, rn_ref, rp_ref,
@@ -365,18 +386,18 @@
     part = part.reshape(plane, 8, width // lane_groups)
     near = lax.ppermute(sent, "shard", [(i, i ^ 1) for i in range(n_x)])
     part = lax.all_to_all(part, PLANE, 0, 0, tiled=True)
-    mine = jnp.sum(part.astype(f32), axis=0).astype(bf16)
+    mine = spread_sum(part, n_z)
     mine, near = lax.optimization_barrier((mine, near))
     packs = jnp.stack([sent, near])
     far = lax.ppermute(packs, "shard", [(i, i ^ 2) for i in range(n_x)])
     *lefts, norm_velocity, norm_master, norm_params = side(
         [packs, far], [norm_momentum, norm_weight], replicas, rank_size, router_rows, col_width
     )
-    mine = jnp.sum(to_all(mine, "z", n_z).astype(f32), axis=0).astype(bf16)
+    mine = spread_sum(lax.all_to_all(mine, "z", 0, 0, tiled=True), n_y * n_x)
     mine, lefts, norm_velocity, norm_master, norm_params = lax.optimization_barrier(
         (mine, lefts, norm_velocity, norm_master, norm_params)
     )
-    sums = lax.all_gather(to_all(mine, CHIPS, n_y * n_x), "c", axis=0, tiled=False)
+    sums = lax.all_gather(lax.all_to_all(mine, CHIPS, 0, 0, tiled=True), "c", axis=0, tiled=False)
     sums = sums.reshape(groups, lane_groups, 8, width // lane_groups)
     (key_carry, router_carry, key_velocity, key_master, key_params, router_velocity, router_master, router_params) = (
         tail(

time: 98.9 us -> 98.3 us (level)
    all_to_all x0 -> x1, blocking collectives: none -> 11.8 us  [body(): lax.all_to_all(mine, CHIPS, 0, 0, tiled=True)]
    all_to_all x3 -> x2, blocking collectives: 44.6 us -> 33.1 us  [to_all(): return lax.all_to_all(spread, axes, 0, 0, tiled=True)]
    all_gather x1, blocking collectives: 6.87 us -> 5.85 us  [body(): lax.all_gather(lax.all_to_all(mine, CHIPS, 0, 0, tiled=True), 'c', axis=0...]
where the time goes in v7:
time: 98.3 us; the launch traced here: 97.8 us
  blocking collectives  59.1 us (60%)
  starting transfers between devices  16.7 us (17%)
  Pallas kernels  11.4 us (12%)
  waiting for transfers between devices  9.6 us (10%)
    all_to_all x2, blocking collectives, to_all(): return lax.all_to_all(spread, axes, 0, 0, tiled=True)  33.1 us
    all_to_all x1, blocking collectives, body(): lax.all_to_all(mine, CHIPS, 0, 0, tiled=True)  11.8 us
    all_gather x1, blocking collectives, body(): pair = lax.all_gather(pack, 'c', axis=0, tiled=False)  8.37 us
    all_to_all x1, starting transfers between devices, body(): part = lax.all_to_all(part, PLANE, 0, 0, tiled=True)  5.88 us
    all_gather x1, blocking collectives, body(): lax.all_gather(lax.all_to_all(mine, CHIPS, 0, 0, tiled=True), 'c', axis=0...  5.85 us
    all_to_all x1, waiting for transfers between devices, body(): part = lax.all_to_all(part, PLANE, 0, 0, tiled=True)  5.64 us
    pallas_call x1, Pallas kernels, side(): pl.pallas_call(lambda *refs: side_kernel(replicas, rank_size, router_rows...  4.2 us
    ppermute x1, starting transfers between devices, body(): far = lax.ppermute(packs, 'shard', [(i, i ^ 2) for i in range(n_x)])  3.89 us
  transfers between devices with their start and end apart: 4, of which 3 were waited for; matrix products, arithmetic and copies ran while one was open for 0% of the time, Pallas kernels for 5%

profile of v7, /device:TPU:1, one launch (start us, length us, event | category | flops | bytes accessed | tf_op | source)
XLA Modules:
  0.0 97.8 jit_solution(6772377353695280077)
XLA Ops:
  0.7 0.0 copy-start
  0.7 0.0 copy-start.1
  0.7 0.0 copy-start.2
  0.7 0.0 copy-start.3
  0.7 0.0 copy-start.5
  0.7 0.0 copy-start.6
  0.8 2.8 %head.1 = f32[48,128]{1,0:T(8,128)S(1)} custom-call(f32[32,2560]{1,0:T(8,128)} %kb_ref.1, f32[32,2560]{1,0:T(8,128)} %rb_ref.1, bf16[1,128,2560]{2,1,0:T(8,128)(2,1)} %kg_ref.5, f32[1,128,2560]{2,1,0:T(8,128)} %ke_ref.5, bf16[1,16,2560]{2,1,0:T(8,128)(2,1)} %rg_ref.5, f32[1,16,2560]{2,1,0:T(8,128)} %re_ref.5, bf16[1,2,640]{2,1,0:T(2,128)(2,1)} %ng_ref.1), custom_call_target="tpu_custom_call" | custom-call | tf_op jit(solution)/shard_map/head/pallas_call | solution.py:76
  3.5 8.4 %all-gather = f32[96,128]{1,0:T(8,128)S(1)} all-gather(f32[48,128]{1,0:T(8,128)S(1)} %head.1), channel_id=2, replica_groups=mesh['z'=16,'y'=4,'c'=2,'shard'=4] {'c'}, dimensions={0}, use_global_device_ids=true | all-gather | bytes 73728 | tf_op jit(solution)/shard_map/all_gather | solution.py:364
  11.9 21.2 %all_to_all.25 = bf16[16,24,128]{2,1,0:T(8,128)(2,1)S(1)} all-to-all(bf16[16,24,128]{2,1,0:T(8,128)(2,1)S(1)} %broadcast_in_dim.4), channel_id=1, replica_groups=mesh['z'=16,'y'=4,'c'=2,'shard'=4] {'z'}, dimensions={0} | all-to-all | bytes 196608 | tf_op jit(solution)/shard_map/all_to_all | solution.py:336
  33.2 11.9 %all_to_all.26 = f32[8,24,128]{2,1,0:T(8,128)S(1)} all-to-all(f32[8,24,128]{2,1,0:T(8,128)S(1)} %broadcast_in_dim.5), channel_id=1, replica_groups=mesh['z'=16,'y'=4,'c'=2,'shard'=4] {'y','c'}, dimensions={0} | all-to-all | bytes 196608 | tf_op jit(solution)/shard_map/all_to_all | solution.py:336
  45.2 1.3 %mid.1 = (bf16[8,4,8,640]{3,2,1,0:T(8,128)(2,1)}, f32[104,128]{1,0:T(8,128)S(1)}) custom-call(f32[48,128]{1,0:T(8,128)S(1)} %bitcast.14, bf16[1,128,2560]{2,1,0:T(8,128)(2,1)S(1)} %copy-done.1, f32[1,128,2560]{2,1,0:T(8,128)S(1)} %copy-done, bf16[1,16,2560]{2,1,0:T(8,128)(2,1)S(1)} %copy-done.3, f32[1,16,2560]{2,1,0:T(8,128)S(1)} %copy-done.2, ...), custom_call_target="tpu_custom_call" | custom-call | tf_op jit(solution)/shard_map/mid/pallas_call | solution.py:123
  46.6 5.9 %all-to-all-start.2 = ((bf16[32,8,640]{2,1,0:T(8,128)(2,1)}), bf16[32,8,640]{2,1,0:T(8,128)(2,1)S(1)}, u32[]{:S(2)}, u32[]{:S(2)}) async-start(bf16[32,8,640]{2,1,0:T(8,128)(2,1)} %bitcast.5), calls=%async_computation.2 | async-start | bytes 655360 | tf_op jit(solution)/shard_map/all_to_all | solution.py:388
  52.5 3.3 %collective-permute-start = (f32[104,128]{1,0:T(8,128)S(1)}, f32[104,128]{1,0:T(8,128)S(1)}, u32[]{:S(2)}, u32[]{:S(2)}) collective-permute-start(f32[104,128]{1,0:T(8,128)S(1)} %get-tuple-element.41), channel_id=1, source_target_pairs={{0,1},{1,0},{2,3},{3,2},{4,5},{5,4},{6,7},{7,6},{8,9},{9,8},{10,11... | collective-permute-start | bytes 159752 | tf_op jit(solution)/shard_map/ppermute | solution.py:387
  55.8 5.6 %all-to-all-done.2.part_ref = bf16[32,8,640]{2,1,0:T(8,128)(2,1)S(1)} async-done(((bf16[32,8,640]{2,1,0:T(8,128)(2,1)}), bf16[32,8,640]{2,1,0:T(8,128)(2,1)S(1)}, u32[]{:S(2)}, u32[]{:S(2)}) %all-to-all-start.2) | async-done | bytes 327712 | tf_op jit(solution)/shard_map/all_to_all | solution.py:388
  61.4 0.7 spread.2
  62.1 0.0 collective-permute-done
  62.1 3.7 %all-to-all-start.3 = ((bf16[16,8,640]{2,1,0:T(8,128)(2,1)}), bf16[16,8,640]{2,1,0:T(8,128)(2,1)S(1)}, u32[]{:S(2)}, u32[]{:S(2)}) async-start(bf16[16,8,640]{2,1,0:T(8,128)(2,1)} %spread.2), calls=%async_computation.3 | async-start | bytes 327680 | tf_op jit(solution)/shard_map/all_to_all | solution.py:396
  65.8 3.9 %collective-permute-start.1 = (f32[2,104,128]{2,1,0:T(8,128)S(1)}, f32[2,104,128]{2,1,0:T(8,128)S(1)}, u32[]{:S(2)}, u32[]{:S(2)}) collective-permute-start(f32[2,104,128]{2,1,0:T(8,128)S(1)} %pad_maximum_fusion.refs_0_), channel_id=1, source_target_pairs={{0,2},{1,3},{2,0},{3,1},{4,6},{5,7},{6,4},{7,5},{8,10},{9,11},{10,... | collective-permute-start | bytes 319496 | tf_op jit(solution)/shard_map/ppermute | solution.py:392
  69.7 3.1 %collective-permute-done.1.refs_1_ = f32[2,104,128]{2,1,0:T(8,128)S(1)} collective-permute-done((f32[2,104,128]{2,1,0:T(8,128)S(1)}, f32[2,104,128]{2,1,0:T(8,128)S(1)}, u32[]{:S(2)}, u32[]{:S(2)}) %collective-permute-start.1) | collective-permute-done | bytes 106528 | tf_op jit(solution)/shard_map/ppermute | solution.py:392
  72.7 4.2 %side.1 = (f32[128,32]{1,0:T(8,128)S(1)}, f32[32,512]{1,0:T(8,128)S(1)}, f32[64,32]{1,0:T(8,128)S(1)}, f32[20,512]{1,0:T(8,128)S(1)}, f32[64,128]{1,0:T(8,128)S(...) custom-call(f32[2,104,128]{2,1,0:T(8,128)S(1)} %pad_maximum_fusion.refs_0_, ...), custom_call_target="tpu_custom_call" | custom-call | flops 200000000 | bytes 8000000 | tf_op jit(solution)/shard_map/side/pallas_call | solution.py:209
  77.0 0.9 all-to-all-done.3.part_ref
  77.9 11.8 %all_to_all.27 = bf16[16,8,640]{2,1,0:T(8,128)(2,1)S(1)} all-to-all(bf16[16,8,640]{2,1,0:T(8,128)(2,1)S(1)} %spread.3), channel_id=1, replica_groups=mesh['z'=16,'y'=4,'c'=2,'shard'=4] {'y','shard'}, dimensions={0} | all-to-all | bytes 327680 | tf_op jit(solution)/shard_map/all_to_all | solution.py:400
  89.7 5.9 %all-gather.1 = bf16[32,8,640]{2,1,0:T(8,128)(2,1)S(1)} all-gather(bf16[16,8,640]{2,1,0:T(8,128)(2,1)S(1)} %all_to_all.27), channel_id=3, replica_groups=mesh['z'=16,'y'=4,'c'=2,'shard'=4] {'c'}, dimensions={0}, use_global_device_ids=true | all-gather | bytes 491520 | tf_op jit(solution)/shard_map/all_gather | solution.py:400
  95.5 2.3 %tail.1 = (f32[1,128,2560]{2,1,0:T(8,128)}, f32[1,16,2560]{2,1,0:T(8,128)}, f32[20,128]{1,0:T(8,128)}, f32[20,128]{1,0:T(8,128)}, bf16[20,512]{1,0:T(8,128)(2,1)...) custom-call(bf16[8,4,8,640]{3,2,1,0:T(8,128)(2,1)S(1)} %bitcast.13, ...), custom_call_target="tpu_custom_call" | custom-call | tf_op jit(solution)/shard_map/tail/pallas_call | solution.py:324
  (23 shorter events, 0.1 us)
Async XLA Ops:
  0.7 44.5 %copy-start = (f32[1,128,2560]{2,1,0:T(8,128)S(1)}, f32[1,128,2560]{2,1,0:T(8,128)}, u32[]{:S(2)}) copy-start(f32[1,128,2560]{2,1,0:T(8,128)} %ke_ref.5) | copy-start | bytes 3932164
  0.7 44.5 %copy-start.1 = (bf16[1,128,2560]{2,1,0:T(8,128)(2,1)S(1)}, bf16[1,128,2560]{2,1,0:T(8,128)(2,1)}, u32[]{:S(2)}) copy-start(bf16[1,128,2560]{2,1,0:T(8,128)(2,1)} %kg_ref.5) | copy-start | bytes 1966084
  0.7 44.5 %copy-start.2 = (f32[1,16,2560]{2,1,0:T(8,128)S(1)}, f32[1,16,2560]{2,1,0:T(8,128)}, u32[]{:S(2)}) copy-start(f32[1,16,2560]{2,1,0:T(8,128)} %re_ref.5) | copy-start | bytes 491524
  0.7 44.5 %copy-start.3 = (bf16[1,16,2560]{2,1,0:T(8,128)(2,1)S(1)}, bf16[1,16,2560]{2,1,0:T(8,128)(2,1)}, u32[]{:S(2)}) copy-start(bf16[1,16,2560]{2,1,0:T(8,128)(2,1)} %rg_ref.5) | copy-start | bytes 245764
  0.7 44.5 %copy-start.5 = (f32[128,20]{0,1:T(8,128)S(1)}, f32[128,20]{0,1:T(8,128)}, u32[]{:S(2)}) copy-start(f32[128,20]{0,1:T(8,128)} %param.20) | copy-start | bytes 30724
  0.7 44.5 %copy-start.6 = (f32[128,20]{0,1:T(8,128)S(1)}, f32[128,20]{0,1:T(8,128)}, u32[]{:S(2)}) copy-start(f32[128,20]{0,1:T(8,128)} %param.21) | copy-start | bytes 30724
  0.7 44.5 %copy-start.7 = (f32[16,20]{1,0:T(8,128)S(1)}, f32[16,20]{1,0:T(8,128)}, u32[]{:S(2)}) copy-start(f32[16,20]{1,0:T(8,128)} %rm_ref.3) | copy-start | bytes 3844
  0.7 44.5 %copy-start.8 = (f32[16,20]{1,0:T(8,128)S(1)}, f32[16,20]{1,0:T(8,128)}, u32[]{:S(2)}) copy-start(f32[16,20]{1,0:T(8,128)} %rw_ref.3) | copy-start | bytes 3844
  0.7 44.5 %copy-start.9 = (f32[2,640]{1,0:T(2,128)S(1)}, f32[2,640]{1,0:T(2,128)}, u32[]{:S(2)}) copy-start(f32[2,640]{1,0:T(2,128)} %refs_2_.1) | copy-start | bytes 15364
  0.7 44.5 %copy-start.10 = (f32[2,640]{1,0:T(2,128)S(1)}, f32[2,640]{1,0:T(2,128)}, u32[]{:S(2)}) copy-start(f32[2,640]{1,0:T(2,128)} %refs_3_.1) | copy-start | bytes 15364
  46.6 14.8 %all-to-all-start.2 = ((bf16[32,8,640]{2,1,0:T(8,128)(2,1)}), bf16[32,8,640]{2,1,0:T(8,128)(2,1)S(1)}, u32[]{:S(2)}, u32[]{:S(2)}) async-start(bf16[32,8,640]{2,1,0:T(8,128)(2,1)} %bitcast.5), calls=%async_computation.2 | async-start | bytes 655360 | tf_op jit(solution)/shard_map/all_to_all | solution.py:388
  52.5 9.7 %collective-permute-start = (f32[104,128]{1,0:T(8,128)S(1)}, f32[104,128]{1,0:T(8,128)S(1)}, u32[]{:S(2)}, u32[]{:S(2)}) collective-permute-start(f32[104,128]{1,0:T(8,128)S(1)} %get-tuple-element.41), channel_id=1, source_target_pairs={{0,1},{1,0},{2,3},{3,2},{4,5},{5,4},{6,7},{7,6},{8,9},{9,8},{10,11... | collective-permute-start | bytes 159752 | tf_op jit(solution)/shard_map/ppermute | solution.py:387
  62.1 33.4 %copy-start.4 = (bf16[1,16,2560]{2,1,0:T(8,128)(2,1)S(1)}, bf16[1,16,2560]{2,1,0:T(8,128)(2,1)}, u32[]{:S(2)}) copy-start(bf16[1,16,2560]{2,1,0:T(8,128)(2,1)} %rg_ref.5) | copy-start | bytes 245764
  62.1 15.7 %all-to-all-start.3 = ((bf16[16,8,640]{2,1,0:T(8,128)(2,1)}), bf16[16,8,640]{2,1,0:T(8,128)(2,1)S(1)}, u32[]{:S(2)}, u32[]{:S(2)}) async-start(bf16[16,8,640]{2,1,0:T(8,128)(2,1)} %spread.2), calls=%async_computation.3 | async-start | bytes 327680 | tf_op jit(solution)/shard_map/all_to_all | solution.py:396
  65.8 7.0 %collective-permute-start.1 = (f32[2,104,128]{2,1,0:T(8,128)S(1)}, f32[2,104,128]{2,1,0:T(8,128)S(1)}, u32[]{:S(2)}, u32[]{:S(2)}) collective-permute-start(f32[2,104,128]{2,1,0:T(8,128)S(1)} %pad_maximum_fusion.refs_0_), channel_id=1, source_target_pairs={{0,2},{1,3},{2,0},{3,1},{4,6},{5,7},{6,4},{7,5},{8,10},{9,11},{10,... | collective-permute-start | bytes 319496 | tf_op jit(solution)/shard_map/ppermute | solution.py:392

commit v8 on v7

--- a/solution.py
+++ b/solution.py
@@ -365,7 +365,7 @@
     half = PACK_ROWS // n_c
     mine = jnp.sum(lax.dynamic_slice_in_dim(pair, lax.axis_index("c") * half, half, 1), axis=0)
     mine = jnp.sum(to_all(mine.astype(bf16), "z", n_z).astype(f32), axis=0)
-    spread = to_all(mine, PAIRS, n_y * n_c).reshape(n_y, n_c, half, LANES)
+    spread = to_all(mine.astype(bf16), PAIRS, n_y * n_c).astype(f32).reshape(n_y, n_c, half, LANES)
     own = jnp.sum(spread, axis=0).reshape(PACK_ROWS, LANES)
 
     groups, lane_groups = 2 * rank_size // 8, plane // (2 * rank_size // 8)

time: 98.3 us -> 98.1 us (level)
  no operation moved by 1% of the time
where the time goes in v8:
time: 98.1 us; the launch traced here: 97.6 us
  blocking collectives  58.9 us (60%)
  starting transfers between devices  16.6 us (17%)
  Pallas kernels  11.4 us (12%)
  waiting for transfers between devices  9.61 us (10%)
    all_to_all x2, blocking collectives, to_all(): return lax.all_to_all(spread, axes, 0, 0, tiled=True)  33 us
    all_to_all x1, blocking collectives, body(): lax.all_to_all(mine, CHIPS, 0, 0, tiled=True)  11.8 us
    all_gather x1, blocking collectives, body(): pair = lax.all_gather(pack, 'c', axis=0, tiled=False)  8.37 us
    all_gather x1, blocking collectives, body(): lax.all_gather(lax.all_to_all(mine, CHIPS, 0, 0, tiled=True), 'c', axis=0...  5.85 us
    all_to_all x1, starting transfers between devices, body(): part = lax.all_to_all(part, PLANE, 0, 0, tiled=True)  5.82 us
    all_to_all x1, waiting for transfers between devices, body(): part = lax.all_to_all(part, PLANE, 0, 0, tiled=True)  5.64 us
    pallas_call x1, Pallas kernels, side(): pl.pallas_call(lambda *refs: side_kernel(replicas, rank_size, router_rows...  4.2 us
    ppermute x1, starting transfers between devices, body(): far = lax.ppermute(packs, 'shard', [(i, i ^ 2) for i in range(n_x)])  3.89 us
  transfers between devices with their start and end apart: 4, of which 3 were waited for; matrix products, arithmetic and copies ran while one was open for 0% of the time, Pallas kernels for 5%

profile of v8, /device:TPU:1, one launch (start us, length us, event | category | flops | bytes accessed | tf_op | source)
XLA Modules:
  0.0 97.6 jit_solution(15430732553328935213)
XLA Ops:
  0.7 0.0 copy-start
  0.7 0.0 copy-start.1
  0.7 0.0 copy-start.2
  0.7 0.0 copy-start.3
  0.7 0.0 copy-start.5
  0.7 0.0 copy-start.6
  0.8 2.8 %head.1 = f32[48,128]{1,0:T(8,128)S(1)} custom-call(f32[32,2560]{1,0:T(8,128)} %kb_ref.1, f32[32,2560]{1,0:T(8,128)} %rb_ref.1, bf16[1,128,2560]{2,1,0:T(8,128)(2,1)} %kg_ref.5, f32[1,128,2560]{2,1,0:T(8,128)} %ke_ref.5, bf16[1,16,2560]{2,1,0:T(8,128)(2,1)} %rg_ref.5, f32[1,16,2560]{2,1,0:T(8,128)} %re_ref.5, bf16[1,2,640]{2,1,0:T(2,128)(2,1)} %ng_ref.1), custom_call_target="tpu_custom_call" | custom-call | tf_op jit(solution)/shard_map/head/pallas_call | solution.py:76
  3.5 8.4 %all-gather = f32[96,128]{1,0:T(8,128)S(1)} all-gather(f32[48,128]{1,0:T(8,128)S(1)} %head.1), channel_id=2, replica_groups=mesh['z'=16,'y'=4,'c'=2,'shard'=4] {'c'}, dimensions={0}, use_global_device_ids=true | all-gather | bytes 73728 | tf_op jit(solution)/shard_map/all_gather | solution.py:364
  11.9 21.2 %all_to_all.25 = bf16[16,24,128]{2,1,0:T(8,128)(2,1)S(1)} all-to-all(bf16[16,24,128]{2,1,0:T(8,128)(2,1)S(1)} %broadcast_in_dim.4), channel_id=1, replica_groups=mesh['z'=16,'y'=4,'c'=2,'shard'=4] {'z'}, dimensions={0} | all-to-all | bytes 196608 | tf_op jit(solution)/shard_map/all_to_all | solution.py:336
  33.2 11.7 %all_to_all.26 = bf16[8,24,128]{2,1,0:T(8,128)(2,1)S(1)} all-to-all(bf16[8,24,128]{2,1,0:T(8,128)(2,1)S(1)} %broadcast_in_dim.5), channel_id=1, replica_groups=mesh['z'=16,'y'=4,'c'=2,'shard'=4] {'y','c'}, dimensions={0} | all-to-all | bytes 98304 | tf_op jit(solution)/shard_map/all_to_all | solution.py:336
  45.0 1.3 %mid.1 = (bf16[8,4,8,640]{3,2,1,0:T(8,128)(2,1)}, f32[104,128]{1,0:T(8,128)S(1)}) custom-call(f32[48,128]{1,0:T(8,128)S(1)} %bitcast.15, bf16[1,128,2560]{2,1,0:T(8,128)(2,1)S(1)} %copy-done.1, f32[1,128,2560]{2,1,0:T(8,128)S(1)} %copy-done, bf16[1,16,2560]{2,1,0:T(8,128)(2,1)S(1)} %copy-done.3, f32[1,16,2560]{2,1,0:T(8,128)S(1)} %copy-done.2, ...), custom_call_target="tpu_custom_call" | custom-call | tf_op jit(solution)/shard_map/mid/pallas_call | solution.py:123
  46.4 5.8 %all-to-all-start.2 = ((bf16[32,8,640]{2,1,0:T(8,128)(2,1)}), bf16[32,8,640]{2,1,0:T(8,128)(2,1)S(1)}, u32[]{:S(2)}, u32[]{:S(2)}) async-start(bf16[32,8,640]{2,1,0:T(8,128)(2,1)} %bitcast.5), calls=%async_computation.2 | async-start | bytes 655360 | tf_op jit(solution)/shard_map/all_to_all | solution.py:388
  52.2 3.3 %collective-permute-start = (f32[104,128]{1,0:T(8,128)S(1)}, f32[104,128]{1,0:T(8,128)S(1)}, u32[]{:S(2)}, u32[]{:S(2)}) collective-permute-start(f32[104,128]{1,0:T(8,128)S(1)} %get-tuple-element.41), channel_id=1, source_target_pairs={{0,1},{1,0},{2,3},{3,2},{4,5},{5,4},{6,7},{7,6},{8,9},{9,8},{10,11... | collective-permute-start | bytes 159752 | tf_op jit(solution)/shard_map/ppermute | solution.py:387
  55.5 5.6 %all-to-all-done.2.part_ref = bf16[32,8,640]{2,1,0:T(8,128)(2,1)S(1)} async-done(((bf16[32,8,640]{2,1,0:T(8,128)(2,1)}), bf16[32,8,640]{2,1,0:T(8,128)(2,1)S(1)}, u32[]{:S(2)}, u32[]{:S(2)}) %all-to-all-start.2) | async-done | bytes 327712 | tf_op jit(solution)/shard_map/all_to_all | solution.py:388
  61.1 0.7 spread.2
  61.9 0.0 collective-permute-done
  61.9 3.7 %all-to-all-start.3 = ((bf16[16,8,640]{2,1,0:T(8,128)(2,1)}), bf16[16,8,640]{2,1,0:T(8,128)(2,1)S(1)}, u32[]{:S(2)}, u32[]{:S(2)}) async-start(bf16[16,8,640]{2,1,0:T(8,128)(2,1)} %spread.2), calls=%async_computation.3 | async-start | bytes 327680 | tf_op jit(solution)/shard_map/all_to_all | solution.py:396
  65.5 3.9 %collective-permute-start.1 = (f32[2,104,128]{2,1,0:T(8,128)S(1)}, f32[2,104,128]{2,1,0:T(8,128)S(1)}, u32[]{:S(2)}, u32[]{:S(2)}) collective-permute-start(f32[2,104,128]{2,1,0:T(8,128)S(1)} %pad_maximum_fusion.refs_0_), channel_id=1, source_target_pairs={{0,2},{1,3},{2,0},{3,1},{4,6},{5,7},{6,4},{7,5},{8,10},{9,11},{10,... | collective-permute-start | bytes 319496 | tf_op jit(solution)/shard_map/ppermute | solution.py:392
  69.4 3.1 %collective-permute-done.1.refs_1_ = f32[2,104,128]{2,1,0:T(8,128)S(1)} collective-permute-done((f32[2,104,128]{2,1,0:T(8,128)S(1)}, f32[2,104,128]{2,1,0:T(8,128)S(1)}, u32[]{:S(2)}, u32[]{:S(2)}) %collective-permute-start.1) | collective-permute-done | bytes 106528 | tf_op jit(solution)/shard_map/ppermute | solution.py:392
  72.5 4.2 %side.1 = (f32[128,32]{1,0:T(8,128)S(1)}, f32[32,512]{1,0:T(8,128)S(1)}, f32[64,32]{1,0:T(8,128)S(1)}, f32[20,512]{1,0:T(8,128)S(1)}, f32[64,128]{1,0:T(8,128)S(...) custom-call(f32[2,104,128]{2,1,0:T(8,128)S(1)} %pad_maximum_fusion.refs_0_, ...), custom_call_target="tpu_custom_call" | custom-call | flops 200000000 | bytes 8000000 | tf_op jit(solution)/shard_map/side/pallas_call | solution.py:209
  76.7 0.9 all-to-all-done.3.part_ref
  77.6 11.8 %all_to_all.27 = bf16[16,8,640]{2,1,0:T(8,128)(2,1)S(1)} all-to-all(bf16[16,8,640]{2,1,0:T(8,128)(2,1)S(1)} %spread.3), channel_id=1, replica_groups=mesh['z'=16,'y'=4,'c'=2,'shard'=4] {'y','shard'}, dimensions={0} | all-to-all | bytes 327680 | tf_op jit(solution)/shard_map/all_to_all | solution.py:400
  89.4 5.9 %all-gather.1 = bf16[32,8,640]{2,1,0:T(8,128)(2,1)S(1)} all-gather(bf16[16,8,640]{2,1,0:T(8,128)(2,1)S(1)} %all_to_all.27), channel_id=3, replica_groups=mesh['z'=16,'y'=4,'c'=2,'shard'=4] {'c'}, dimensions={0}, use_global_device_ids=true | all-gather | bytes 491520 | tf_op jit(solution)/shard_map/all_gather | solution.py:400
  95.3 2.3 %tail.1 = (f32[1,128,2560]{2,1,0:T(8,128)}, f32[1,16,2560]{2,1,0:T(8,128)}, f32[20,128]{1,0:T(8,128)}, f32[20,128]{1,0:T(8,128)}, bf16[20,512]{1,0:T(8,128)(2,1)...) custom-call(bf16[8,4,8,640]{3,2,1,0:T(8,128)(2,1)S(1)} %bitcast.14, ...), custom_call_target="tpu_custom_call" | custom-call | tf_op jit(solution)/shard_map/tail/pallas_call | solution.py:324
  (23 shorter events, 0.1 us)
Async XLA Ops:
  0.7 44.3 %copy-start = (f32[1,128,2560]{2,1,0:T(8,128)S(1)}, f32[1,128,2560]{2,1,0:T(8,128)}, u32[]{:S(2)}) copy-start(f32[1,128,2560]{2,1,0:T(8,128)} %ke_ref.5) | copy-start | bytes 3932164
  0.7 44.3 %copy-start.1 = (bf16[1,128,2560]{2,1,0:T(8,128)(2,1)S(1)}, bf16[1,128,2560]{2,1,0:T(8,128)(2,1)}, u32[]{:S(2)}) copy-start(bf16[1,128,2560]{2,1,0:T(8,128)(2,1)} %kg_ref.5) | copy-start | bytes 1966084
  0.7 44.3 %copy-start.2 = (f32[1,16,2560]{2,1,0:T(8,128)S(1)}, f32[1,16,2560]{2,1,0:T(8,128)}, u32[]{:S(2)}) copy-start(f32[1,16,2560]{2,1,0:T(8,128)} %re_ref.5) | copy-start | bytes 491524
  0.7 44.3 %copy-start.3 = (bf16[1,16,2560]{2,1,0:T(8,128)(2,1)S(1)}, bf16[1,16,2560]{2,1,0:T(8,128)(2,1)}, u32[]{:S(2)}) copy-start(bf16[1,16,2560]{2,1,0:T(8,128)(2,1)} %rg_ref.5) | copy-start | bytes 245764
  0.7 44.3 %copy-start.5 = (f32[128,20]{0,1:T(8,128)S(1)}, f32[128,20]{0,1:T(8,128)}, u32[]{:S(2)}) copy-start(f32[128,20]{0,1:T(8,128)} %param.20) | copy-start | bytes 30724
  0.7 44.3 %copy-start.6 = (f32[128,20]{0,1:T(8,128)S(1)}, f32[128,20]{0,1:T(8,128)}, u32[]{:S(2)}) copy-start(f32[128,20]{0,1:T(8,128)} %param.21) | copy-start | bytes 30724
  0.7 44.3 %copy-start.7 = (f32[16,20]{1,0:T(8,128)S(1)}, f32[16,20]{1,0:T(8,128)}, u32[]{:S(2)}) copy-start(f32[16,20]{1,0:T(8,128)} %rm_ref.3) | copy-start | bytes 3844
  0.7 44.3 %copy-start.8 = (f32[16,20]{1,0:T(8,128)S(1)}, f32[16,20]{1,0:T(8,128)}, u32[]{:S(2)}) copy-start(f32[16,20]{1,0:T(8,128)} %rw_ref.3) | copy-start | bytes 3844
  0.7 44.3 %copy-start.9 = (f32[2,640]{1,0:T(2,128)S(1)}, f32[2,640]{1,0:T(2,128)}, u32[]{:S(2)}) copy-start(f32[2,640]{1,0:T(2,128)} %refs_2_.1) | copy-start | bytes 15364
  0.7 44.3 %copy-start.10 = (f32[2,640]{1,0:T(2,128)S(1)}, f32[2,640]{1,0:T(2,128)}, u32[]{:S(2)}) copy-start(f32[2,640]{1,0:T(2,128)} %refs_3_.1) | copy-start | bytes 15364
  46.4 14.8 %all-to-all-start.2 = ((bf16[32,8,640]{2,1,0:T(8,128)(2,1)}), bf16[32,8,640]{2,1,0:T(8,128)(2,1)S(1)}, u32[]{:S(2)}, u32[]{:S(2)}) async-start(bf16[32,8,640]{2,1,0:T(8,128)(2,1)} %bitcast.5), calls=%async_computation.2 | async-start | bytes 655360 | tf_op jit(solution)/shard_map/all_to_all | solution.py:388
  52.2 9.7 %collective-permute-start = (f32[104,128]{1,0:T(8,128)S(1)}, f32[104,128]{1,0:T(8,128)S(1)}, u32[]{:S(2)}, u32[]{:S(2)}) collective-permute-start(f32[104,128]{1,0:T(8,128)S(1)} %get-tuple-element.41), channel_id=1, source_target_pairs={{0,1},{1,0},{2,3},{3,2},{4,5},{5,4},{6,7},{7,6},{8,9},{9,8},{10,11... | collective-permute-start | bytes 159752 | tf_op jit(solution)/shard_map/ppermute | solution.py:387
  61.9 33.4 %copy-start.4 = (bf16[1,16,2560]{2,1,0:T(8,128)(2,1)S(1)}, bf16[1,16,2560]{2,1,0:T(8,128)(2,1)}, u32[]{:S(2)}) copy-start(bf16[1,16,2560]{2,1,0:T(8,128)(2,1)} %rg_ref.5) | copy-start | bytes 245764
  61.9 15.7 %all-to-all-start.3 = ((bf16[16,8,640]{2,1,0:T(8,128)(2,1)}), bf16[16,8,640]{2,1,0:T(8,128)(2,1)S(1)}, u32[]{:S(2)}, u32[]{:S(2)}) async-start(bf16[16,8,640]{2,1,0:T(8,128)(2,1)} %spread.2), calls=%async_computation.3 | async-start | bytes 327680 | tf_op jit(solution)/shard_map/all_to_all | solution.py:396
  65.5 7.0 %collective-permute-start.1 = (f32[2,104,128]{2,1,0:T(8,128)S(1)}, f32[2,104,128]{2,1,0:T(8,128)S(1)}, u32[]{:S(2)}, u32[]{:S(2)}) collective-permute-start(f32[2,104,128]{2,1,0:T(8,128)S(1)} %pad_maximum_fusion.refs_0_), channel_id=1, source_target_pairs={{0,2},{1,3},{2,0},{3,1},{4,6},{5,7},{6,4},{7,5},{8,10},{9,11},{10,... | collective-permute-start | bytes 319496 | tf_op jit(solution)/shard_map/ppermute | solution.py:392
